TPU v7x, 256 devices: a whole 4x4x8 slice. The times are simulated.
256 devices in a mesh: member: 2 (over core), space: 128 (over x, y, z).
Axes of the slice: x: 4, y: 4, z: 8, core: 2. Of those that a mesh axis runs over, the one named last changes fastest.
Arguments:
- initial_states: bfloat16 [4, 65536, 98], P('member', 'space'), may hold values from -6 to 6
- target: float32 [65536, 98], P('space'), may hold values from -6 to 6
- enc_owner: int32 [65536, 1], P('space'), may hold values from 0 to 127; in each aligned block of 512 rows (0 to 511, 512 to 1023, ...) at most 8 rows name the same one
- enc_local: int32 [65536, 1], P('space'), may hold values from 0 to 255
- dec_owner: int32 [65536, 1], P('space'), may hold values from 0 to 127; in each aligned block of 512 rows (0 to 511, 512 to 1023, ...) at most 8 rows name the same one
- dec_local: int32 [65536, 1], P('space'), may hold values from 0 to 255
- w_embed: bfloat16 [98, 1024], replicated, may hold values from -0.625 to 0.625
- w_qkv: bfloat16 [1024, 3072], replicated, may hold values from -5 to 5
- w_out: bfloat16 [1024, 1024], replicated, may hold values from -0.1875 to 0.1875
- w_decode: bfloat16 [1024, 98], replicated, may hold values from -0.1875 to 0.1875
Outputs:
- predicted_states: bfloat16 [4, 65536, 98], P('member', 'space')
- probabilistic_error: float32 [65536, 98], P('space')
Inputs may be any that keep to these rules, and one draw needn't show every extreme that they name: `enc_owner`: among the rows of one device, at most 8 name the same block. `dec_owner`: among the rows of one device, at most 8 name the same block.
All inputs are finite; a program needn't handle non-finite values.
Results may differ from a plain program's by a relative error of at most 0.012.
The roundings to bfloat16 on the way count: a program that leaves them out, or rounds other values in their place, can miss the bound.
Values may be sent and summed in bfloat16 or wider, within the bound.
No kernel may reach another device: no remote copies, remote signals or barrier semaphores. Data moves between devices by JAX's collectives and lax.ppermute only.
A program may use at most 128 MiB of HBM per device.

v0:
```python
import functools

import jax
import jax.numpy as jnp
from jax import lax
from jax.experimental import pallas as pl
from jax.experimental.pallas import tpu as pltpu
from jax.sharding import PartitionSpec as P

HEADS = 16
HALF_WIN = 128
NODE_DEV = 256
CAP = 8
LANES = 128

FAIR_ALPHA = 0.95
NORM_EPS = 1e-05

F32 = jnp.float32
BF16 = jnp.bfloat16
NT = (((1,), (1,)), ((), ()))
TN = (((0,), (0,)), ((), ()))
VMEM_SPEC = pl.BlockSpec(memory_space=pltpu.VMEM)
SMEM_SPEC = pl.BlockSpec(memory_space=pltpu.SMEM)


def nt_dot(a, b):
    return lax.dot_general(a, b, NT, preferred_element_type=F32)


def iota(shape, dim):
    return lax.broadcasted_iota(jnp.int32, shape, dim)


def slot_row(owner_row):
    pts = owner_row.shape[1]
    square = (pts, pts)
    wide = jnp.broadcast_to(owner_row, square)
    row_id, col_id = iota(square, 0), iota(square, 1)
    owner_col = jnp.sum(jnp.where(row_id == col_id, wide, 0), axis=1, keepdims=True)
    earlier = (owner_col == wide) & (row_id < col_id)
    rank = jnp.sum(earlier.astype(jnp.int32), axis=0, keepdims=True)
    return owner_row * CAP + rank


def pack_kernel(var_count, x_ref, eo_ref, el_ref, do_ref, dl_ref, out_ref, slot_ref, aug_ref):
    members, _, pts = x_ref.shape
    n_dest = out_ref.shape[0]
    slots = n_dest * CAP
    enc_slot = slot_row(eo_ref[...])
    dec_slot = slot_row(do_ref[...])
    slot_ref[...] = dec_slot
    slot_id = iota((slots, pts), 0)
    place = (slot_id == enc_slot).astype(F32).astype(BF16)
    request = (slot_id == dec_slot).astype(F32).astype(BF16)
    row_id = iota((LANES, pts), 0)
    enc_meta = jnp.where(row_id == var_count, el_ref[...] + 1, 0).astype(F32)
    dec_meta = jnp.where(row_id == var_count, dl_ref[...] + 1, 0).astype(F32)
    asked = nt_dot(request, dec_meta.astype(BF16))
    packed = []
    for m in range(members):
        aug_ref[...] = enc_meta if m == 0 else jnp.zeros_like(enc_meta)
        aug_ref[0:var_count, :] = x_ref[m].astype(F32)
        rows = nt_dot(place, aug_ref[...].astype(BF16))
        if m == 1:
            rows = rows + asked
        packed.append(rows.reshape(n_dest, 1, CAP, LANES))
    out_ref[...] = jnp.concatenate(packed, axis=1).astype(BF16)


def member_rows(ref, m):
    n_dest = ref.shape[0]
    return ref[:, m].astype(F32).reshape(n_dest * CAP, LANES).astype(BF16)


def encode_kernel(var_count, in_ref, w_ref, lo_ref, hi_ref, wpad_ref, pooled_ref):
    n_dest, members = in_ref.shape[:2]
    slots = n_dest * CAP
    width = w_ref.shape[1]
    nodes = NODE_DEV
    wpad_ref[...] = jnp.zeros_like(wpad_ref)
    wpad_ref[0:var_count, :] = w_ref[...].astype(F32)
    chunk = 256
    lane_id = iota((8, LANES), 1)
    pick = (lane_id == var_count).astype(F32).astype(BF16)
    node_row = nt_dot(pick, member_rows(in_ref, 0))[0:1, :]
    node_id = (iota((nodes, slots), 0) + 1).astype(F32)
    assign_f = (node_id == node_row).astype(F32)
    count = jnp.maximum(jnp.sum(assign_f, axis=1, keepdims=True), 1.0)
    assign = assign_f.astype(BF16)
    for m in range(members):
        x = member_rows(in_ref, m)

        def embed(c, carry):
            cols = pl.ds(pl.multiple_of(c * chunk, chunk), chunk)
            raw = jnp.dot(x, wpad_ref[:, cols].astype(BF16), preferred_element_type=F32)
            embedded = (raw / (1.0 + jnp.exp(-raw))).astype(BF16)
            pooled_ref[:, cols] = jnp.dot(assign, embedded, preferred_element_type=F32)
            return carry

        lax.fori_loop(0, width // chunk, embed, 0)
        pooled = pooled_ref[...] / count
        centred = pooled - jnp.mean(pooled, axis=1, keepdims=True)
        variance = jnp.mean(centred * centred, axis=1, keepdims=True)
        hidden = (centred * lax.rsqrt(variance + NORM_EPS)).astype(BF16)
        lo_ref[m] = hidden[0:HALF_WIN]
        hi_ref[m] = hidden[HALF_WIN:]


def qkv_kernel(lo_ref, hi_ref, w_ref, out_ref):
    members = lo_ref.shape[0]
    rows = jnp.concatenate([r[m] for m in range(members) for r in (lo_ref, hi_ref)], axis=0)
    acc = jnp.dot(rows, w_ref[...], preferred_element_type=F32)
    out_ref[...] = acc.astype(BF16)


def attend_kernel(
    var_count, ends_ref, qkv_ref, lo_ref, hi_ref, bef_ref, aft_ref, w_kv_ref, w_out_ref, w_dec_ref,
    in_ref, out_ref, kv_ref, att_ref, wdec_ref,
):
    n_dest, members = in_ref.shape[:2]
    slots = n_dest * CAP
    half, width = lo_ref.shape[1:]
    nodes = 2 * half
    head_dim = width // HEADS
    wdec_ref[...] = jnp.zeros_like(wdec_ref)
    wdec_ref[0:var_count, :] = w_dec_ref[...].astype(F32)
    halo = jnp.concatenate([r[m] for m in range(members) for r in (bef_ref, aft_ref)], axis=0)
    chunk = 512

    def project(c, carry):
        src = pl.ds(pl.multiple_of(width + c * chunk, chunk), chunk)
        cols = pl.ds(pl.multiple_of(c * chunk, chunk), chunk)
        kv_ref[:, cols] = jnp.dot(halo, w_kv_ref[:, src], preferred_element_type=F32).astype(BF16)
        return carry

    lax.fori_loop(0, 2 * width // chunk, project, 0)

    first = ends_ref[0]
    last = ends_ref[1]
    row_id, col_id = iota((half, half), 0), iota((half, half), 1)
    big = 4 * half
    left_lo = col_id >= row_id + first * big
    left_hi = col_id >= row_id
    right_lo = col_id <= row_id
    right_hi = col_id + last * big <= row_id
    even = iota((half, LANES), 1) < head_dim
    scale = head_dim ** (-0.5)

    for m in range(members):
        base = m * nodes

        def heads(p, carry):
            q_cols = pl.ds(pl.multiple_of(p * LANES, LANES), LANES)
            k_cols = pl.ds(pl.multiple_of(width + p * LANES, LANES), LANES)
            v_cols = pl.ds(pl.multiple_of(2 * width + p * LANES, LANES), LANES)
            hv_cols = pl.ds(pl.multiple_of(width + p * LANES, LANES), LANES)
            k_own = qkv_ref[base : base + nodes, k_cols]
            v_own = qkv_ref[base : base + nodes, v_cols]
            k_bef, k_aft = kv_ref[base : base + half, q_cols], kv_ref[base + half : base + nodes, q_cols]
            v_bef, v_aft = kv_ref[base : base + half, hv_cols], kv_ref[base + half : base + nodes, hv_cols]
            for side in range(2):
                q_pair = qkv_ref[base + side * half : base + (side + 1) * half, q_cols]
                if side == 0:
                    keys = jnp.concatenate([k_bef, k_own], axis=0)
                    values = jnp.concatenate([v_bef, v_own], axis=0)
                    left, right = left_lo, right_lo
                else:
                    keys = jnp.concatenate([k_own, k_aft], axis=0)
                    values = jnp.concatenate([v_own, v_aft], axis=0)
                    left, right = left_hi, right_hi
                pair = []
                for h in range(2):
                    mine = even if h == 0 else ~even
                    q = jnp.where(mine, q_pair, jnp.zeros_like(q_pair))
                    s = nt_dot(q, keys) * scale
                    s0 = jnp.where(left, s[:, 0:half], -1e30)
                    s1 = s[:, half : 2 * half]
                    s2 = jnp.where(right, s[:, 2 * half :], -1e30)
                    top = jnp.max(jnp.maximum(jnp.maximum(s0, s1), s2), axis=1, keepdims=True)
                    e0, e1, e2 = jnp.exp(s0 - top), jnp.exp(s1 - top), jnp.exp(s2 - top)
                    inv = 1.0 / jnp.sum(e0 + e1 + e2, axis=1, keepdims=True)
                    weights = jnp.concatenate([e0 * inv, e1 * inv, e2 * inv], axis=1).astype(BF16)
                    pair.append(jnp.dot(weights, values, preferred_element_type=F32))
                att_ref[base + side * half : base + (side + 1) * half, q_cols] = jnp.where(
                    even, pair[0], pair[1]
                ).astype(BF16)
            return carry

        lax.fori_loop(0, HEADS // 2, heads, 0)

    node_lane = (iota((slots, nodes), 1) + 1).astype(F32)
    asked = in_ref[:, 1].astype(F32).reshape(slots, LANES)[:, var_count : var_count + 1]
    reply = (node_lane == asked).astype(F32).astype(BF16)
    wdec = wdec_ref[...].astype(BF16)
    packed = []
    for m in range(members):
        base = m * nodes
        hidden = jnp.concatenate([lo_ref[m], hi_ref[m]], axis=0).astype(F32)
        mixed = jnp.dot(att_ref[base : base + nodes, :], w_out_ref[...], preferred_element_type=F32)
        processed = (hidden + mixed).astype(BF16)
        decoded = nt_dot(processed, wdec).astype(BF16)
        rows = jnp.dot(reply, decoded, preferred_element_type=F32)
        packed.append(rows.reshape(n_dest, 1, CAP, LANES))
    out_ref[...] = jnp.concatenate(packed, axis=1).astype(BF16)


def predict_kernel(var_count, slot_ref, back_ref, x_ref, out_ref):
    n_dest, members = back_ref.shape[:2]
    slots = n_dest * CAP
    pts = x_ref.shape[2]
    place = (iota((slots, pts), 0) == slot_ref[...]).astype(F32).astype(BF16)
    for m in range(members):
        rows = member_rows(back_ref, m)
        got = lax.dot_general(rows, place, TN, preferred_element_type=F32)
        out_ref[m] = (x_ref[m].astype(F32) + got[0:var_count]).astype(BF16)


def score_kernel(mine_ref, other_ref, target_ref, out_ref):
    fields = [r[m].astype(F32) for r in (mine_ref, other_ref) for m in range(mine_ref.shape[0])]
    count = len(fields)
    target = target_ref[...]
    skill = sum(jnp.abs(f - target) for f in fields) / count
    spread = 2.0 * sum(
        jnp.abs(fields[i] - fields[j]) for i in range(count) for j in range(i + 1, count)
    )
    fair_eps = (1.0 - FAIR_ALPHA) / count
    out_ref[...] = skill - (1.0 - fair_eps) / (2.0 * count * (count - 1)) * spread


def params(mib=32):
    return pltpu.CompilerParams(vmem_limit_bytes=mib << 20)


def on_device(
    initial_states,
    target,
    enc_owner,
    enc_local,
    dec_owner,
    dec_local,
    w_embed,
    w_qkv,
    w_out,
    w_decode,
):
    n_space = lax.axis_size("space")
    me = lax.axis_index("space")
    members, pts, var_count = initial_states.shape
    width = w_embed.shape[1]
    nodes, half = NODE_DEV, HALF_WIN
    slots = n_space * CAP
    states = jnp.transpose(initial_states, (0, 2, 1))
    rows = [a.reshape(1, pts) for a in (enc_owner, enc_local, dec_owner, dec_local)]
    wire = jax.ShapeDtypeStruct((n_space, members, CAP, LANES), BF16)

    outgoing, dec_slot = pl.pallas_call(
        functools.partial(pack_kernel, var_count),
        out_shape=(wire, jax.ShapeDtypeStruct((1, pts), jnp.int32)),
        scratch_shapes=[pltpu.VMEM((LANES, pts), F32)],
        compiler_params=params(),
        name="pack",
    )(states, *rows)
    arrived = lax.all_to_all(outgoing, "space", 0, 0, tiled=True)

    half_shape = jax.ShapeDtypeStruct((members, half, width), BF16)
    lo, hi = pl.pallas_call(
        functools.partial(encode_kernel, var_count),
        out_shape=(half_shape, half_shape),
        scratch_shapes=[pltpu.VMEM((LANES, width), F32), pltpu.VMEM((nodes, width), F32)],
        compiler_params=params(),
        name="encode",
    )(arrived, w_embed)

    up = [(i, (i + 1) % n_space) for i in range(n_space)]
    down = [(j, i) for i, j in up]
    before = lax.ppermute(hi, "space", up)
    after = lax.ppermute(lo, "space", down)

    step = 512
    qkv = pl.pallas_call(
        qkv_kernel,
        grid=(3 * width // step,),
        in_specs=[
            pl.BlockSpec((members, half, width), lambda c: (0, 0, 0)),
            pl.BlockSpec((members, half, width), lambda c: (0, 0, 0)),
            pl.BlockSpec((width, step), lambda c: (0, c)),
        ],
        out_specs=pl.BlockSpec((members * nodes, step), lambda c: (0, c)),
        out_shape=jax.ShapeDtypeStruct((members * nodes, 3 * width), BF16),
        cost_estimate=pl.CostEstimate(
            flops=2 * members * nodes * width * 3 * width, bytes_accessed=10 << 20, transcendentals=0
        ),
        compiler_params=params(),
        name="qkv",
    )(lo, hi, w_qkv)

    ends = jnp.stack([(me == 0), (me == n_space - 1)]).astype(jnp.int32)
    replies = pl.pallas_call(
        functools.partial(attend_kernel, var_count),
        in_specs=[SMEM_SPEC] + [VMEM_SPEC] * 9,
        out_shape=wire,
        scratch_shapes=[
            pltpu.VMEM((members * nodes, 2 * width), BF16),
            pltpu.VMEM((members * nodes, width), BF16),
            pltpu.VMEM((LANES, width), F32),
        ],
        compiler_params=params(40),
        name="attend",
    )(ends, qkv, lo, hi, before, after, w_qkv, w_out, w_decode.T, arrived)

    returned = lax.all_to_all(replies, "space", 0, 0, tiled=True)
    predicted = pl.pallas_call(
        functools.partial(predict_kernel, var_count),
        out_shape=jax.ShapeDtypeStruct((members, var_count, pts), BF16),
        compiler_params=params(),
        name="predict",
    )(dec_slot, returned, states)
    other = lax.ppermute(predicted, "member", [(0, 1), (1, 0)])
    error = pl.pallas_call(
        score_kernel,
        out_shape=jax.ShapeDtypeStruct((var_count, pts), F32),
        compiler_params=params(),
        name="score",
    )(predicted, other, target.T)
    return jnp.transpose(predicted, (0, 2, 1)), error.T


def solution(mesh):
    in_specs = (
        P("member", "space", None),
        P("space", None),
        P("space", None),
        P("space", None),
        P("space", None),
        P("space", None),
        P(),
        P(),
        P(),
        P(),
    )
    out_specs = (P("member", "space", None), P("space", None))
    return jax.shard_map(
        on_device, mesh=mesh, in_specs=in_specs, out_specs=out_specs, check_vma=False
    )
```

profile of v0, /device:TPU:1, one launch (start us, length us, event | category | flops | bytes accessed | tf_op | source)
XLA Modules:
  0.0 127.5 jit_solution(5251633210226040676)
XLA Ops:
  0.6 1.0 copy.15
  1.6 0.0 copy-start.5
  1.6 0.7 copy-done.5
  2.3 0.0 copy-start.6
  2.3 0.7 copy-done.6
  3.0 0.0 copy-start.7
  3.0 0.7 copy-done.7
  3.6 0.0 copy-start.8
  3.6 0.7 copy-done.8
  4.3 1.2 pack.1
  5.6 35.3 %all_to_all.10.in_ref = bf16[128,2,8,128]{3,2,1,0:T(8,128)(2,1)S(1)} all-to-all(bf16[128,2,8,128]{3,2,1,0:T(8,128)(2,1)S(1)} %get-tuple-element.7), channel_id=1, replica_groups=mesh['member'=2,'space'=128] {'space'}, dimensions={0} | all-to-all | bytes 1048576 | tf_op jit(solution)/shard_map/all_to_all | solution.py:264
  40.9 0.0 copy-start.2
  40.9 0.9 copy-done.2
  41.8 5.9 %encode.1 = (bf16[2,128,1024]{2,1,0:T(8,128)(2,1)S(1)}, bf16[2,128,1024]{2,1,0:T(8,128)(2,1)S(1)}) custom-call(bf16[128,2,8,128]{3,2,1,0:T(8,128)(2,1)S(1)} %all_to_all.10.in_ref, bf16[98,1024]{1,0:T(8,128)(2,1)S(1)} %copy-done.2), custom_call_target="tpu_custom_call" | custom-call | tf_op jit(solution)/shard_map/encode/pallas_call | solution.py:267
  47.7 0.7 collective-permute-start.1
  48.5 0.8 collective-permute-start
  49.3 0.1 add_convert_fusion.ends_ref
  49.3 0.0 copy-start
  49.3 2.8 %copy-done = bf16[1024,3072]{1,0:T(8,128)(2,1)S(1)} copy-done((bf16[1024,3072]{1,0:T(8,128)(2,1)S(1)}, bf16[1024,3072]{1,0:T(8,128)(2,1)}, u32[]{:S(2)}) %copy-start) | copy-done | bytes 6291480
  52.1 0.0 copy-start.1
  52.1 0.0 copy-start.4
  52.1 4.9 %qkv.1.qkv_ref = bf16[512,3072]{1,0:T(8,128)(2,1)S(1)} custom-call(bf16[2,128,1024]{2,1,0:T(8,128)(2,1)S(1)} %get-tuple-element.8.lo_ref, bf16[2,128,1024]{2,1,0:T(8,128)(2,1)S(1)} %get-tuple-element.9.hi_ref, bf16[1024,3072]{1,0:T(8,128)(2,1)S(1)} %copy-done), custom_call_target="tpu_custom_call" | custom-call | flops 3221225472 | bytes 10485760 | tf_op jit(solution)/shard_map/qkv/pallas_call | solution.py:281
  57.0 1.8 %collective-permute-done.1.aft_ref = bf16[2,128,1024]{2,1,0:T(8,128)(2,1)S(1)} collective-permute-done((bf16[2,128,1024]{2,1,0:T(8,128)(2,1)S(1)}, bf16[2,128,1024]{2,1,0:T(8,128)(2,1)S(1)}, u32[]{:S(2)}, u32[]{:S(2)}) %collective-permute-start.1) | collective-permute-done | bytes 524320 | tf_op jit(solution)/shard_map/ppermute | solution.py:278
  58.8 6.1 %collective-permute-done.bef_ref = bf16[2,128,1024]{2,1,0:T(8,128)(2,1)S(1)} collective-permute-done((bf16[2,128,1024]{2,1,0:T(8,128)(2,1)S(1)}, bf16[2,128,1024]{2,1,0:T(8,128)(2,1)S(1)}, u32[]{:S(2)}, u32[]{:S(2)}) %collective-permute-start) | collective-permute-done | bytes 524320 | tf_op jit(solution)/shard_map/ppermute | solution.py:277
  64.9 0.0 copy-done.1
  64.9 0.0 copy-done.4
  64.9 0.0 copy-start.3
  64.9 32.5 %attend.1 = bf16[128,2,8,128]{3,2,1,0:T(8,128)(2,1)S(1)} custom-call(s32[2]{0:T(128)S(1)} %add_convert_fusion.ends_ref, bf16[512,3072]{1,0:T(8,128)(2,1)S(1)} %qkv.1.qkv_ref, bf16[2,128,1024]{2,1,0:T(8,128)(2,1)S(1)} %get-tuple-element.8.lo_ref, bf16[2,128,1024]{2,1,0:T(8,128)(2,1)S(1)} %get-tuple-element.9.hi_ref, ...), custom_call_target="tpu_custom_call" | custom-call | tf_op jit(solution)/shard_map/attend/pallas_call | solution.py:299
  97.4 22.4 %all_to_all.11.back_ref = bf16[128,2,8,128]{3,2,1,0:T(8,128)(2,1)S(1)} all-to-all(bf16[128,2,8,128]{3,2,1,0:T(8,128)(2,1)S(1)} %attend.1), channel_id=1, replica_groups=mesh['member'=2,'space'=128] {'space'}, dimensions={0} | all-to-all | bytes 1048576 | tf_op jit(solution)/shard_map/all_to_all | solution.py:312
  119.8 0.6 predict.1.mine_ref
  120.4 5.0 %collective-permute-start.2 = (bf16[2,98,512]{2,1,0:T(8,128)(2,1)S(1)}, bf16[2,98,512]{2,1,0:T(8,128)(2,1)S(1)}, u32[]{:S(2)}, u32[]{:S(2)}) collective-permute-start(bf16[2,98,512]{2,1,0:T(8,128)(2,1)S(1)} %predict.1.mine_ref), channel_id=1, source_target_pairs={{0,128},{128,0},{1,129},{129,1},{2,130},{130,2},{3,131},{131,3},{4... | collective-permute-start | bytes 602120 | tf_op jit(solution)/shard_map/ppermute | solution.py:319
  125.4 0.8 copy.13
  126.3 0.3 collective-permute-done.2.other_ref
  126.5 0.0 copy-done.3
  126.5 0.9 score.1
Async XLA Ops:
  1.6 0.7 copy-start.5
  2.3 0.7 copy-start.6
  3.0 0.7 copy-start.7
  3.6 0.7 copy-start.8
  40.9 0.9 copy-start.2
  47.7 11.1 %collective-permute-start.1 = (bf16[2,128,1024]{2,1,0:T(8,128)(2,1)S(1)}, bf16[2,128,1024]{2,1,0:T(8,128)(2,1)S(1)}, u32[]{:S(2)}, u32[]{:S(2)}) collective-permute-start(bf16[2,128,1024]{2,1,0:T(8,128)(2,1)S(1)} %get-tuple-element.8.lo_ref), channel_id=1, source_target_pairs={{1,0},{2,1},{3,2},{4,3},{5,4},{6,5},{7,6},{8,7},{9,8},{10,9},{11,1... | collective-permute-start | bytes 1572872 | tf_op jit(solution)/shard_map/ppermute | solution.py:278
  48.5 16.5 %collective-permute-start = (bf16[2,128,1024]{2,1,0:T(8,128)(2,1)S(1)}, bf16[2,128,1024]{2,1,0:T(8,128)(2,1)S(1)}, u32[]{:S(2)}, u32[]{:S(2)}) collective-permute-start(bf16[2,128,1024]{2,1,0:T(8,128)(2,1)S(1)} %get-tuple-element.9.hi_ref), channel_id=1, source_target_pairs={{0,1},{1,2},{2,3},{3,4},{4,5},{5,6},{6,7},{7,8},{8,9},{9,10},{10,1... | collective-permute-start | bytes 1572872 | tf_op jit(solution)/shard_map/ppermute | solution.py:277
  49.3 2.8 %copy-start = (bf16[1024,3072]{1,0:T(8,128)(2,1)S(1)}, bf16[1024,3072]{1,0:T(8,128)(2,1)}, u32[]{:S(2)}) copy-start(bf16[1024,3072]{1,0:T(8,128)(2,1)} %w_kv_ref.1) | copy-start | bytes 18874372
  52.1 12.8 %copy-start.1 = (bf16[1024,1024]{1,0:T(8,128)(2,1)S(1)}, bf16[1024,1024]{1,0:T(8,128)(2,1)}, u32[]{:S(2)}) copy-start(bf16[1024,1024]{1,0:T(8,128)(2,1)} %w_out_ref.1) | copy-start | bytes 6291460
  52.1 12.8 %copy-start.4 = (bf16[1024,98]{0,1:T(8,128)(2,1)S(1)}, bf16[1024,98]{0,1:T(8,128)(2,1)}, u32[]{:S(2)}) copy-start(bf16[1024,98]{0,1:T(8,128)(2,1)} %param.19) | copy-start | bytes 602116
  64.9 61.6 %copy-start.3 = (f32[512,98]{0,1:T(8,128)S(1)}, f32[512,98]{0,1:T(8,128)}, u32[]{:S(2)}) copy-start(f32[512,98]{0,1:T(8,128)} %param.11) | copy-start | bytes 602116
  120.4 6.1 %collective-permute-start.2 = (bf16[2,98,512]{2,1,0:T(8,128)(2,1)S(1)}, bf16[2,98,512]{2,1,0:T(8,128)(2,1)S(1)}, u32[]{:S(2)}, u32[]{:S(2)}) collective-permute-start(bf16[2,98,512]{2,1,0:T(8,128)(2,1)S(1)} %predict.1.mine_ref), channel_id=1, source_target_pairs={{0,128},{128,0},{1,129},{129,1},{2,130},{130,2},{3,131},{131,3},{4... | collective-permute-start | bytes 602120 | tf_op jit(solution)/shard_map/ppermute | solution.py:319
where the time goes:
time: 128 us; the launch traced here: 127 us
  blocking collectives  57.7 us (45%)
  Pallas kernels  46 us (36%)
  local copies, waits for them, and re-layouts  8.23 us (6%)
  waiting for transfers between devices  8.18 us (6%)
  starting transfers between devices  6.57 us (5%)
    all_to_all x1, blocking collectives, on_device(): arrived = lax.all_to_all(outgoing, 'space', 0, 0, tiled=True)  35.3 us
    pallas_call x1, Pallas kernels, on_device(): pl.pallas_call(functools.partial(attend_kernel, var_count), in_specs=[SME...  32.5 us
    all_to_all x1, blocking collectives, on_device(): returned = lax.all_to_all(replies, 'space', 0, 0, tiled=True)  22.4 us
    unnamed x20, local copies, waits for them, and re-layouts  8.23 us
    ppermute x1, waiting for transfers between devices, on_device(): before = lax.ppermute(hi, 'space', up)  6.14 us
    pallas_call x1, Pallas kernels, on_device(): pl.pallas_call(functools.partial(encode_kernel, var_count), out_shape=(ha...  5.92 us
    ppermute x1, starting transfers between devices, on_device(): other = lax.ppermute(predicted, 'member', [(0, 1), (1, 0)])  5.02 us
    pallas_call x1, Pallas kernels, on_device(): pl.pallas_call(qkv_kernel, grid=(3 * width // step,), in_specs=[pl.BlockS...  4.88 us
  transfers between devices with their start and end apart: 3, of which 3 were waited for; matrix products, arithmetic and copies ran while one was open for 1% of the time, Pallas kernels for 4%

commit v1 on v0

v1 whole, which is shorter than its diff:
```python
import functools

import jax
import jax.numpy as jnp
from jax import lax
from jax.experimental import pallas as pl
from jax.experimental.pallas import tpu as pltpu
from jax.sharding import PartitionSpec as P

HEADS = 16
HALF_WIN = 128
NODE_DEV = 256
CAP = 8
LANES = 128

FAIR_ALPHA = 0.95
NORM_EPS = 1e-05

F32 = jnp.float32
BF16 = jnp.bfloat16
NT = (((1,), (1,)), ((), ()))
TN = (((0,), (0,)), ((), ()))
VMEM_SPEC = pl.BlockSpec(memory_space=pltpu.VMEM)
SMEM_SPEC = pl.BlockSpec(memory_space=pltpu.SMEM)


def nt_dot(a, b):
    return lax.dot_general(a, b, NT, preferred_element_type=F32)


def iota(shape, dim):
    return lax.broadcasted_iota(jnp.int32, shape, dim)


def slot_row(owner_row):
    pts = owner_row.shape[1]
    square = (pts, pts)
    wide = jnp.broadcast_to(owner_row, square)
    row_id, col_id = iota(square, 0), iota(square, 1)
    owner_col = jnp.sum(jnp.where(row_id == col_id, wide, 0), axis=1, keepdims=True)
    earlier = (owner_col == wide) & (row_id < col_id)
    rank = jnp.sum(earlier.astype(jnp.int32), axis=0, keepdims=True)
    return owner_row * CAP + rank


def pack_kernel(var_count, x_ref, eo_ref, el_ref, do_ref, dl_ref, out_ref, slot_ref, aug_ref):
    members, _, pts = x_ref.shape
    n_dest = out_ref.shape[0]
    slots = n_dest * CAP
    enc_slot = slot_row(eo_ref[...])
    dec_slot = slot_row(do_ref[...])
    slot_ref[...] = dec_slot
    slot_id = iota((slots, pts), 0)
    place = (slot_id == enc_slot).astype(F32).astype(BF16)
    request = (slot_id == dec_slot).astype(F32).astype(BF16)
    row_id = iota((LANES, pts), 0)
    enc_meta = jnp.where(row_id == var_count, el_ref[...] + 1, 0).astype(F32)
    dec_meta = jnp.where(row_id == var_count, dl_ref[...] + 1, 0).astype(F32)
    asked = nt_dot(request, dec_meta.astype(BF16))
    packed = []
    for m in range(members):
        aug_ref[...] = enc_meta if m == 0 else jnp.zeros_like(enc_meta)
        aug_ref[0:var_count, :] = x_ref[m].astype(F32)
        rows = nt_dot(place, aug_ref[...].astype(BF16))
        if m == 1:
            rows = rows + asked
        packed.append(rows.reshape(n_dest, 1, CAP, LANES))
    out_ref[...] = jnp.concatenate(packed, axis=1).astype(BF16)


def member_rows(ref, m):
    n_dest = ref.shape[0]
    return ref[:, m].astype(F32).reshape(n_dest * CAP, LANES).astype(BF16)


def encode_kernel(var_count, m, in_ref, w_ref, lo_ref, hi_ref, pooled_ref):
    n_dest = in_ref.shape[0]
    slots = n_dest * CAP
    width = w_ref.shape[1]
    nodes = NODE_DEV
    chunk = 256
    lane_id = iota((8, LANES), 1)
    pick = (lane_id == var_count).astype(F32).astype(BF16)
    node_row = nt_dot(pick, member_rows(in_ref, 0))[0:1, :]
    node_id = (iota((nodes, slots), 0) + 1).astype(F32)
    assign_f = (node_id == node_row).astype(F32)
    share = 1.0 / jnp.maximum(jnp.sum(assign_f, axis=1, keepdims=True), 1.0)
    assign = assign_f.astype(BF16)
    x = member_rows(in_ref, m)[:, 0:var_count]

    def embed(c, carry):
        cols = pl.ds(pl.multiple_of(c * chunk, chunk), chunk)
        raw = 0.5 * jnp.dot(x, w_ref[:, cols], preferred_element_type=F32)
        embedded = (raw + raw * jnp.tanh(raw)).astype(BF16)
        pooled_ref[:, cols] = jnp.dot(assign, embedded, preferred_element_type=F32)
        return carry

    lax.fori_loop(0, width // chunk, embed, 0)
    step = 32
    for out_ref, first in ((lo_ref, 0), (hi_ref, HALF_WIN)):
        for r in range(0, HALF_WIN, step):
            part = slice(first + r, first + r + step)
            pooled = pooled_ref[part, :] * share[part]
            centred = pooled - jnp.mean(pooled, axis=1, keepdims=True)
            variance = jnp.mean(centred * centred, axis=1, keepdims=True)
            out_ref[r : r + step, :] = (centred * lax.rsqrt(variance + NORM_EPS)).astype(BF16)


def qkv_kernel(halves, *refs):
    hidden_refs, w_ref, qk_ref, vt_ref = refs[:halves], refs[halves], refs[halves + 1], refs[halves + 2]
    c = pl.program_id(0)
    rows = jnp.concatenate([r[...] for r in hidden_refs], axis=0)
    acc = jnp.dot(rows, w_ref[...], preferred_element_type=F32).astype(BF16)

    @pl.when(c < 4)
    def _():
        qk_ref[...] = acc

    @pl.when(c >= 4)
    def _():
        vt_ref[...] = acc.T


def attend_kernel(
    var_count, m, ends_ref, qk_ref, vt_ref, lo_ref, hi_ref, bef_ref, aft_ref, w_kv_ref, w_out_ref,
    w_dec_ref, *rest,
):
    if m == 0:
        out_ref, kh_ref, vth_ref, att_ref, proc_ref, left_ref, right_ref = rest
    else:
        dec_ref, in_ref, out_ref, kh_ref, vth_ref, att_ref, proc_ref, left_ref, right_ref = rest
    half, width = lo_ref.shape
    nodes = 2 * half
    head_dim = width // HEADS
    halo = jnp.concatenate([bef_ref[...], aft_ref[...]], axis=0)
    chunk = 256

    def project(c, carry):
        cols = pl.ds(pl.multiple_of(c * chunk, chunk), chunk)
        k_src = pl.ds(pl.multiple_of(width + c * chunk, chunk), chunk)
        v_src = pl.ds(pl.multiple_of(2 * width + c * chunk, chunk), chunk)
        kh_ref[:, cols] = jnp.dot(halo, w_kv_ref[:, k_src], preferred_element_type=F32).astype(BF16)
        vh = jnp.dot(halo, w_kv_ref[:, v_src], preferred_element_type=F32).astype(BF16)
        vth_ref[cols, :] = vh.T
        return carry

    lax.fori_loop(0, width // chunk, project, 0)

    key_id = iota((half, 2 * half), 0)
    query_id = iota((half, 2 * half), 1)
    query_id = jnp.where(query_id >= half, query_id - half, query_id)
    big = 4 * half
    zero, low = jnp.zeros((half, 2 * half), F32), jnp.full((half, 2 * half), -1e30, F32)
    left_ref[0] = jnp.where(key_id >= query_id + ends_ref[0] * big, zero, low)
    left_ref[1] = jnp.where(key_id >= query_id, zero, low)
    right_ref[0] = jnp.where(key_id <= query_id, zero, low)
    right_ref[1] = jnp.where(key_id + ends_ref[1] * big <= query_id, zero, low)
    even = iota((half, LANES), 1) < head_dim
    gain = head_dim ** (-0.5) * 1.4426950408889634
    base = m * nodes

    def heads(p, carry):
        cols = pl.ds(pl.multiple_of(p * LANES, LANES), LANES)
        k_cols = pl.ds(pl.multiple_of(width + p * LANES, LANES), LANES)
        k_own = qk_ref[base : base + nodes, k_cols]
        vt_own = vt_ref[cols, base : base + nodes]
        for side in range(2):
            row0 = side * half
            q = qk_ref[base + row0 : base + row0 + half, cols]
            none = jnp.zeros_like(q)
            q2 = jnp.concatenate([jnp.where(even, q, none), jnp.where(even, none, q)], axis=0)
            s_own = nt_dot(k_own, q2)
            s_halo = nt_dot(kh_ref[row0 : row0 + half, cols], q2)
            if side == 0:
                s0 = s_halo + left_ref[0]
                s1 = s_own[0:half]
                s2 = s_own[half:] + right_ref[0]
            else:
                s0 = s_own[0:half] + left_ref[1]
                s1 = s_own[half:]
                s2 = s_halo + right_ref[1]
            top = jnp.max(jnp.maximum(jnp.maximum(s0, s1), s2), axis=0, keepdims=True)
            e0, e1, e2 = (jnp.exp2((s - top) * gain) for s in (s0, s1, s2))
            inv = 1.0 / jnp.sum(e0 + e1 + e2, axis=0, keepdims=True)
            p0, p1, p2 = ((e * inv).astype(BF16) for e in (e0, e1, e2))
            if side == 0:
                p_halo, p_own = p0, jnp.concatenate([p1, p2], axis=0)
            else:
                p_own, p_halo = jnp.concatenate([p0, p1], axis=0), p2
            out = jnp.dot(vt_own, p_own, preferred_element_type=F32)
            out += jnp.dot(vth_ref[cols, row0 : row0 + half], p_halo, preferred_element_type=F32)
            pair = jnp.concatenate([out[0:head_dim, 0:half], out[head_dim:, half:]], axis=0)
            att_ref[row0 : row0 + half, cols] = pair.T.astype(BF16)
        return carry

    lax.fori_loop(0, HEADS // 2, heads, 0)

    def mix(c, carry):
        cols = pl.ds(pl.multiple_of(c * chunk, chunk), chunk)
        mixed = jnp.dot(att_ref[...], w_out_ref[:, cols], preferred_element_type=F32)
        proc_ref[0:half, cols] = (lo_ref[:, cols].astype(F32) + mixed[0:half]).astype(BF16)
        proc_ref[half:, cols] = (hi_ref[:, cols].astype(F32) + mixed[half:]).astype(BF16)
        return carry

    lax.fori_loop(0, width // chunk, mix, 0)
    decoded = nt_dot(proc_ref[...], w_dec_ref[...]).astype(BF16)
    if m == 0:
        out_ref[...] = jnp.zeros_like(out_ref)
        out_ref[:, 0:var_count] = decoded
    else:
        n_dest = in_ref.shape[0]
        slots = n_dest * CAP
        mine_ref = att_ref.at[:, 0:LANES]
        mine_ref[...] = jnp.zeros_like(mine_ref)
        mine_ref[:, 0:var_count] = decoded
        both = jnp.concatenate([dec_ref[...], mine_ref[...]], axis=1)
        node_lane = (iota((slots, nodes), 1) + 1).astype(F32)
        asked = in_ref[:, 1].astype(F32).reshape(slots, LANES)[:, var_count : var_count + 1]
        reply = (node_lane == asked).astype(F32).astype(BF16)
        rows = jnp.dot(reply, both, preferred_element_type=F32)
        packed = [rows[:, i * LANES : (i + 1) * LANES].reshape(n_dest, 1, CAP, LANES) for i in range(2)]
        out_ref[...] = jnp.concatenate(packed, axis=1).astype(BF16)


def predict_kernel(var_count, slot_ref, back_ref, x_ref, out_ref):
    n_dest, members = back_ref.shape[:2]
    slots = n_dest * CAP
    pts = x_ref.shape[2]
    place = (iota((slots, pts), 0) == slot_ref[...]).astype(F32).astype(BF16)
    for m in range(members):
        rows = member_rows(back_ref, m)
        got = lax.dot_general(rows, place, TN, preferred_element_type=F32)
        out_ref[m] = (x_ref[m].astype(F32) + got[0:var_count]).astype(BF16)


def score_kernel(mine_ref, other_ref, target_ref, out_ref):
    fields = [r[m].astype(F32) for r in (mine_ref, other_ref) for m in range(mine_ref.shape[0])]
    count = len(fields)
    target = target_ref[...]
    skill = sum(jnp.abs(f - target) for f in fields) / count
    spread = 2.0 * sum(
        jnp.abs(fields[i] - fields[j]) for i in range(count) for j in range(i + 1, count)
    )
    fair_eps = (1.0 - FAIR_ALPHA) / count
    out_ref[...] = skill - (1.0 - fair_eps) / (2.0 * count * (count - 1)) * spread


def params(mib=32):
    return pltpu.CompilerParams(vmem_limit_bytes=mib << 20)


def cost(micros):
    return pl.CostEstimate(flops=int(micros * 7e8), bytes_accessed=1 << 20, transcendentals=0)


def on_device(
    initial_states,
    target,
    enc_owner,
    enc_local,
    dec_owner,
    dec_local,
    w_embed,
    w_qkv,
    w_out,
    w_decode,
):
    n_space = lax.axis_size("space")
    me = lax.axis_index("space")
    members, pts, var_count = initial_states.shape
    width = w_embed.shape[1]
    nodes, half = NODE_DEV, HALF_WIN
    slots = n_space * CAP
    states = jnp.transpose(initial_states, (0, 2, 1))
    rows = [a.reshape(1, pts) for a in (enc_owner, enc_local, dec_owner, dec_local)]
    wire = jax.ShapeDtypeStruct((n_space, members, CAP, LANES), BF16)

    outgoing, dec_slot = pl.pallas_call(
        functools.partial(pack_kernel, var_count),
        out_shape=(wire, jax.ShapeDtypeStruct((1, pts), jnp.int32)),
        scratch_shapes=[pltpu.VMEM((LANES, pts), F32)],
        compiler_params=params(),
        name="pack",
    )(states, *rows)
    arrived = lax.all_to_all(outgoing, "space", 0, 0, tiled=True)

    half_shape = jax.ShapeDtypeStruct((half, width), BF16)
    up = [(i, (i + 1) % n_space) for i in range(n_space)]
    down = [(j, i) for i, j in up]
    hidden, halos = [], []
    for m in range(members):
        lo, hi = pl.pallas_call(
            functools.partial(encode_kernel, var_count, m),
            out_shape=(half_shape, half_shape),
            scratch_shapes=[pltpu.VMEM((nodes, width), F32)],
            compiler_params=params(),
            cost_estimate=cost(3),
            name=f"encode{m}",
        )(arrived, w_embed)
        hidden += [lo, hi]
        halos.append((lax.ppermute(hi, "space", up), lax.ppermute(lo, "space", down)))

    step = 512
    half_spec = pl.BlockSpec((half, width), lambda c: (0, 0))
    qk, vt = pl.pallas_call(
        functools.partial(qkv_kernel, len(hidden)),
        grid=(3 * width // step,),
        in_specs=[half_spec] * len(hidden) + [pl.BlockSpec((width, step), lambda c: (0, c))],
        out_specs=(
            pl.BlockSpec((members * nodes, step), lambda c: (0, jnp.minimum(c, 3))),
            pl.BlockSpec((step, members * nodes), lambda c: (jnp.maximum(c - 4, 0), 0)),
        ),
        out_shape=(
            jax.ShapeDtypeStruct((members * nodes, 2 * width), BF16),
            jax.ShapeDtypeStruct((width, members * nodes), BF16),
        ),
        cost_estimate=cost(5),
        compiler_params=params(),
        name="qkv",
    )(*hidden, w_qkv)

    ends = jnp.stack([(me == 0), (me == n_space - 1)]).astype(jnp.int32)
    decoded = None
    for m in range(members):
        extra = () if m == 0 else (decoded, arrived)
        decoded = pl.pallas_call(
            functools.partial(attend_kernel, var_count, m),
            in_specs=[SMEM_SPEC] + [VMEM_SPEC] * (9 + len(extra)),
            out_shape=jax.ShapeDtypeStruct((nodes, LANES), BF16) if m == 0 else wire,
            scratch_shapes=[
                pltpu.VMEM((nodes, width), BF16),
                pltpu.VMEM((width, nodes), BF16),
                pltpu.VMEM((nodes, width), BF16),
                pltpu.VMEM((nodes, width), BF16),
                pltpu.VMEM((2, half, nodes), F32),
                pltpu.VMEM((2, half, nodes), F32),
            ],
            compiler_params=params(),
            cost_estimate=cost(8),
            name=f"attend{m}",
        )(ends, qk, vt, *hidden[2 * m : 2 * m + 2], *halos[m], w_qkv, w_out, w_decode.T, *extra)
    replies = decoded

    returned = lax.all_to_all(replies, "space", 0, 0, tiled=True)
    predicted = pl.pallas_call(
        functools.partial(predict_kernel, var_count),
        out_shape=jax.ShapeDtypeStruct((members, var_count, pts), BF16),
        compiler_params=params(),
        name="predict",
    )(dec_slot, returned, states)
    other = lax.ppermute(predicted, "member", [(0, 1), (1, 0)])
    error = pl.pallas_call(
        score_kernel,
        out_shape=jax.ShapeDtypeStruct((var_count, pts), F32),
        compiler_params=params(),
        name="score",
    )(predicted, other, target.T)
    return jnp.transpose(predicted, (0, 2, 1)), error.T


def solution(mesh):
    in_specs = (
        P("member", "space", None),
        P("space", None),
        P("space", None),
        P("space", None),
        P("space", None),
        P("space", None),
        P(),
        P(),
        P(),
        P(),
    )
    out_specs = (P("member", "space", None), P("space", None))
    return jax.shard_map(
        on_device, mesh=mesh, in_specs=in_specs, out_specs=out_specs, check_vma=False
    )
```

time: 128 us -> 123 us (0.961)
  blocking collectives: 57.7 us -> 22.3 us
  starting transfers between devices: 6.57 us -> 35.3 us
  waiting for transfers between devices: 8.18 us -> 19.3 us
  Pallas kernels: 46 us -> 39.1 us
  local copies, waits for them, and re-layouts: 8.23 us -> 5.47 us
    all_to_all x1 -> x0, blocking collectives: 35.3 us -> none  [on_device(): arrived = lax.all_to_all(outgoing, 'space', 0, 0, tiled=True)]
    all_to_all x0 -> x1, waiting for transfers between devices: none -> 19.1 us  [on_device(): arrived = lax.all_to_all(outgoing, 'space', 0, 0, tiled=True)]
    all_to_all x0 -> x1, starting transfers between devices: none -> 16.3 us  [on_device(): arrived = lax.all_to_all(outgoing, 'space', 0, 0, tiled=True)]
    ppermute x2 -> x4, starting transfers between devices: 1.54 us -> 13.9 us  [the longest x2 12.9 us: on_device(): lax.ppermute(lo, 'space', down)]
    ppermute x2 -> x4, waiting for transfers between devices: 7.92 us -> 0.01 us  [the longest x2 0.01 us: on_device(): lax.ppermute(lo, 'space', down)]
    pallas_call x3 -> x5, Pallas kernels: 43.3 us -> 35.5 us  [the longest x2 23.9 us: on_device(): pl.pallas_call(functools.partial(attend_kernel, var_count, m), in_specs=[...]
    unnamed x20 -> x22, local copies, waits for them, and re-layouts: 8.23 us -> 5.47 us
  transfers between devices with their start and end apart: 3 -> 6, of which waited for: 3 -> 2; matrix products, arithmetic and copies ran while one was open for 1% -> 1% of each run, Pallas kernels for 4% -> 17%
where the time goes in v1:
time: 123 us; the launch traced here: 122 us
  Pallas kernels  39.1 us (32%)
  starting transfers between devices  35.3 us (29%)
  blocking collectives  22.3 us (18%)
  waiting for transfers between devices  19.3 us (16%)
  local copies, waits for them, and re-layouts  5.47 us (4%)
    pallas_call x2, Pallas kernels, on_device(): pl.pallas_call(functools.partial(attend_kernel, var_count, m), in_specs=[...  23.9 us
    all_to_all x1, blocking collectives, on_device(): returned = lax.all_to_all(replies, 'space', 0, 0, tiled=True)  22.3 us
    all_to_all x1, waiting for transfers between devices, on_device(): arrived = lax.all_to_all(outgoing, 'space', 0, 0, tiled=True)  19.1 us
    all_to_all x1, starting transfers between devices, on_device(): arrived = lax.all_to_all(outgoing, 'space', 0, 0, tiled=True)  16.3 us
    ppermute x2, starting transfers between devices, on_device(): lax.ppermute(lo, 'space', down)  12.9 us
    pallas_call x2, Pallas kernels, on_device(): pl.pallas_call(functools.partial(encode_kernel, var_count, m), out_shape=...  6.07 us
    pallas_call x1, Pallas kernels, on_device(): pl.pallas_call(functools.partial(qkv_kernel, len(hidden)), grid=(3 * widt...  5.56 us
    unnamed x22, local copies, waits for them, and re-layouts  5.47 us
  transfers between devices with their start and end apart: 6, of which 2 were waited for; matrix products, arithmetic and copies ran while one was open for 1% of the time, Pallas kernels for 17%

profile of v1, /device:TPU:1, one launch (start us, length us, event | category | flops | bytes accessed | tf_op | source)
XLA Modules:
  0.0 122.4 jit_solution(1876528268620860161)
XLA Ops:
  0.6 1.0 copy.15
  1.6 0.0 copy-start.1
  1.6 0.7 copy-done.1
  2.3 0.0 copy-start.2
  2.3 0.7 copy-done.2
  3.0 0.0 copy-start.3
  3.0 0.7 copy-done.3
  3.6 0.0 copy-start.4
  3.6 0.7 copy-done.4
  4.3 2.1 %pack.1 = (bf16[128,2,8,128]{3,2,1,0:T(8,128)(2,1)}, s32[1,512]{1,0:T(1,128)S(1)}) custom-call(bf16[2,98,512]{2,1,0:T(8,128)(2,1)S(1)} %bitcast.13, s32[1,512]{1,0:T(1,128)S(1)} %bitcast.17, s32[1,512]{1,0:T(1,128)S(1)} %bitcast.18, s32[1,512]{1,0:T(1,128)S(1)} %bitcast.19, s32[1,512]{1,0:T(1,128)S(1)} %bitcast.20), custom_call_target="tpu_custom_call" | custom-call | tf_op jit(solution)/shard_map/pack/pallas_call | solution.py:278
  6.4 16.3 %all-to-all-start = ((bf16[128,2,8,128]{3,2,1,0:T(8,128)(2,1)}), bf16[128,2,8,128]{3,2,1,0:T(8,128)(2,1)S(1)}, u32[]{:S(2)}, u32[]{:S(2)}) async-start(bf16[128,2,8,128]{3,2,1,0:T(8,128)(2,1)} %get-tuple-element.11), calls=%async_computation | async-start | bytes 1048576 | tf_op jit(solution)/shard_map/all_to_all | solution.py:285
  22.7 0.1 add_convert_fusion.ends_ref
  22.8 19.1 %all-to-all-done.in_ref.rest_1_ = bf16[128,2,8,128]{3,2,1,0:T(8,128)(2,1)S(1)} async-done(((bf16[128,2,8,128]{3,2,1,0:T(8,128)(2,1)}), bf16[128,2,8,128]{3,2,1,0:T(8,128)(2,1)S(1)}, u32[]{:S(2)}, u32[]{:S(2)}) %all-to-all-start) | async-done | bytes 524320 | tf_op jit(solution)/shard_map/all_to_all | solution.py:285
  41.9 0.0 copy-start.6
  41.9 0.9 copy-done.6
  42.8 0.0 slice-start
  42.8 3.0 %encode0.1 = (bf16[128,1024]{1,0:T(8,128)(2,1)S(1)}, bf16[128,1024]{1,0:T(8,128)(2,1)S(1)}) custom-call(bf16[128,2,8,128]{3,2,1,0:T(8,128)(2,1)S(1)} %all-to-all-done.in_ref.rest_1_, bf16[98,1024]{1,0:T(8,128)(2,1)S(1)} %copy-done.6), custom_call_target="tpu_custom_call" | custom-call | flops 2100000000 | bytes 1048576 | tf_op jit(solution)/shard_map/encode0/pallas_call | solution.py:292
  45.8 0.0 slice-start.1
  45.9 0.9 collective-permute-start.2
  46.7 6.1 %collective-permute-start.3 = (bf16[128,1024]{1,0:T(8,128)(2,1)S(1)}, bf16[128,1024]{1,0:T(8,128)(2,1)S(1)}, u32[]{:S(2)}, u32[]{:S(2)}) collective-permute-start(bf16[128,1024]{1,0:T(8,128)(2,1)S(1)} %get-tuple-element.12.refs_0_.lo_ref), channel_id=1, source_target_pairs={{1,0},{2,1},{3,2},{4,3},{5,4},{6,5},{7,6},{8,7},{9,8},{10,9},{11,1... | collective-permute-start | bytes 786440 | tf_op jit(solution)/shard_map/ppermute | solution.py:301
  52.8 3.0 %encode1.1 = (bf16[128,1024]{1,0:T(8,128)(2,1)S(1)}, bf16[128,1024]{1,0:T(8,128)(2,1)S(1)}) custom-call(bf16[128,2,8,128]{3,2,1,0:T(8,128)(2,1)S(1)} %all-to-all-done.in_ref.rest_1_, bf16[98,1024]{1,0:T(8,128)(2,1)S(1)} %copy-done.6), custom_call_target="tpu_custom_call" | custom-call | flops 2100000000 | bytes 1048576 | tf_op jit(solution)/shard_map/encode1/pallas_call | solution.py:292
  55.9 0.1 collective-permute-start
  56.0 0.0 copy-start.5
  56.0 0.0 copy-start.7
  56.0 6.9 %collective-permute-start.1 = (bf16[128,1024]{1,0:T(8,128)(2,1)S(1)}, bf16[128,1024]{1,0:T(8,128)(2,1)S(1)}, u32[]{:S(2)}, u32[]{:S(2)}) collective-permute-start(bf16[128,1024]{1,0:T(8,128)(2,1)S(1)} %get-tuple-element.14.refs_2_.lo_ref), channel_id=1, source_target_pairs={{1,0},{2,1},{3,2},{4,3},{5,4},{6,5},{7,6},{8,7},{9,8},{10,9},{11,1... | collective-permute-start | bytes 786440 | tf_op jit(solution)/shard_map/ppermute | solution.py:301
  62.9 0.0 slice-done
  62.9 0.0 slice-done.1
  62.9 5.6 %qkv.1 = (bf16[512,2048]{1,0:T(8,128)(2,1)S(1)}, bf16[1024,512]{1,0:T(8,128)(2,1)S(1)}) custom-call(bf16[128,1024]{1,0:T(8,128)(2,1)S(1)} %get-tuple-element.12.refs_0_.lo_ref, bf16[128,1024]{1,0:T(8,128)(2,1)S(1)} %get-tuple-element.13.refs_1_.hi_ref, bf16[128,1024]{1,0:T(8,128)(2,1)S(1)} %get-tuple-element.14.refs_2_.lo_ref, ...), custom_call_target="tpu_custom_call" | custom-call | flops 3500000000 | bytes 1048576 | tf_op jit(solution)/shard_map/qkv/pallas_call | solution.py:305
  68.4 0.0 collective-permute-done.2.bef_ref
  68.4 0.0 collective-permute-done.3.aft_ref
  68.5 0.0 copy-done.5
  68.5 0.0 copy-done.7
  68.5 11.7 %attend0.1.rest_0_ = bf16[256,128]{1,0:T(8,128)(2,1)S(1)} custom-call(s32[2]{0:T(128)S(1)} %add_convert_fusion.ends_ref, bf16[512,2048]{1,0:T(8,128)(2,1)S(1)} %get-tuple-element.16.qk_ref, bf16[1024,512]{1,0:T(8,128)(2,1)S(1)} %get-tuple-element.17.vt_ref, bf16[128,1024]{1,0:T(8,128)(2,1)S(1)} %get-tuple-element.12.refs_0_.lo_ref, ...), custom_call_target="tpu_custom_call" | custom-call | flops 5600000000 | bytes 1048576 | tf_op jit(solution)/shard_map/attend0/pallas_call | solution.py:326
  80.2 0.0 collective-permute-done.bef_ref
  80.2 0.0 collective-permute-done.1.aft_ref
  80.2 12.2 %attend1.1 = bf16[128,2,8,128]{3,2,1,0:T(8,128)(2,1)S(1)} custom-call(s32[2]{0:T(128)S(1)} %add_convert_fusion.ends_ref, bf16[512,2048]{1,0:T(8,128)(2,1)S(1)} %get-tuple-element.16.qk_ref, bf16[1024,512]{1,0:T(8,128)(2,1)S(1)} %get-tuple-element.17.vt_ref, bf16[128,1024]{1,0:T(8,128)(2,1)S(1)} %get-tuple-element.14.refs_2_.lo_ref, ...), custom_call_target="tpu_custom_call" | custom-call | flops 5600000000 | bytes 1048576 | tf_op jit(solution)/shard_map/attend1/pallas_call | solution.py:326
  92.4 0.0 copy-start
  92.4 22.3 %all_to_all.10.back_ref = bf16[128,2,8,128]{3,2,1,0:T(8,128)(2,1)S(1)} all-to-all(bf16[128,2,8,128]{3,2,1,0:T(8,128)(2,1)S(1)} %attend1.1), channel_id=1, replica_groups=mesh['member'=2,'space'=128] {'space'}, dimensions={0} | all-to-all | bytes 1048576 | tf_op jit(solution)/shard_map/all_to_all | solution.py:344
  114.7 0.6 predict.1.mine_ref
  115.3 5.1 %collective-permute-start.4 = (bf16[2,98,512]{2,1,0:T(8,128)(2,1)S(1)}, bf16[2,98,512]{2,1,0:T(8,128)(2,1)S(1)}, u32[]{:S(2)}, u32[]{:S(2)}) collective-permute-start(bf16[2,98,512]{2,1,0:T(8,128)(2,1)S(1)} %predict.1.mine_ref), channel_id=1, source_target_pairs={{0,128},{128,0},{1,129},{129,1},{2,130},{130,2},{3,131},{131,3},{4... | collective-permute-start | bytes 602120 | tf_op jit(solution)/shard_map/ppermute | solution.py:351
  120.4 0.8 copy.13
  121.2 0.3 collective-permute-done.4.other_ref
  121.5 0.0 copy-done
  121.5 0.9 score.1
  (1 shorter events, 0.0 us)
Async XLA Ops:
  1.6 0.7 copy-start.1
  2.3 0.7 copy-start.2
  3.0 0.7 copy-start.3
  3.6 0.7 copy-start.4
  6.4 35.5 %all-to-all-start = ((bf16[128,2,8,128]{3,2,1,0:T(8,128)(2,1)}), bf16[128,2,8,128]{3,2,1,0:T(8,128)(2,1)S(1)}, u32[]{:S(2)}, u32[]{:S(2)}) async-start(bf16[128,2,8,128]{3,2,1,0:T(8,128)(2,1)} %get-tuple-element.11), calls=%async_computation | async-start | bytes 1048576 | tf_op jit(solution)/shard_map/all_to_all | solution.py:285
  41.9 0.9 copy-start.6
  42.8 20.1 %slice-start = ((s8[6291456]{0:T(1024)(128)(4,1)}), s8[4194304]{0:T(1024)(128)(4,1)S(1)}, s32[]{:S(2)}) async-start(s8[6291456]{0:T(1024)(128)(4,1)} %bitcast.21), calls=%async_computation.2 | async-start | bytes 8388608
  45.8 17.0 %slice-start.1 = ((s8[6291456]{0:T(1024)(128)(4,1)}), s8[2097152]{0:T(1024)(128)(4,1)S(1)}, s32[]{:S(2)}) async-start(s8[6291456]{0:T(1024)(128)(4,1)} %bitcast.21), calls=%async_computation.3 | async-start | bytes 4194304
  45.9 22.6 %collective-permute-start.2 = (bf16[128,1024]{1,0:T(8,128)(2,1)S(1)}, bf16[128,1024]{1,0:T(8,128)(2,1)S(1)}, u32[]{:S(2)}, u32[]{:S(2)}) collective-permute-start(bf16[128,1024]{1,0:T(8,128)(2,1)S(1)} %get-tuple-element.13.refs_1_.hi_ref), channel_id=1, source_target_pairs={{0,1},{1,2},{2,3},{3,4},{4,5},{5,6},{6,7},{7,8},{8,9},{9,10},{10,1... | collective-permute-start | bytes 786440 | tf_op jit(solution)/shard_map/ppermute | solution.py:301
  46.7 21.7 %collective-permute-start.3 = (bf16[128,1024]{1,0:T(8,128)(2,1)S(1)}, bf16[128,1024]{1,0:T(8,128)(2,1)S(1)}, u32[]{:S(2)}, u32[]{:S(2)}) collective-permute-start(bf16[128,1024]{1,0:T(8,128)(2,1)S(1)} %get-tuple-element.12.refs_0_.lo_ref), channel_id=1, source_target_pairs={{1,0},{2,1},{3,2},{4,3},{5,4},{6,5},{7,6},{8,7},{9,8},{10,9},{11,1... | collective-permute-start | bytes 786440 | tf_op jit(solution)/shard_map/ppermute | solution.py:301
  55.9 24.3 %collective-permute-start = (bf16[128,1024]{1,0:T(8,128)(2,1)S(1)}, bf16[128,1024]{1,0:T(8,128)(2,1)S(1)}, u32[]{:S(2)}, u32[]{:S(2)}) collective-permute-start(bf16[128,1024]{1,0:T(8,128)(2,1)S(1)} %get-tuple-element.15.refs_3_.hi_ref), channel_id=1, source_target_pairs={{0,1},{1,2},{2,3},{3,4},{4,5},{5,6},{6,7},{7,8},{8,9},{9,10},{10,1... | collective-permute-start | bytes 786440 | tf_op jit(solution)/shard_map/ppermute | solution.py:301
  56.0 12.5 %copy-start.5 = (bf16[1024,1024]{1,0:T(8,128)(2,1)S(1)}, bf16[1024,1024]{1,0:T(8,128)(2,1)}, u32[]{:S(2)}) copy-start(bf16[1024,1024]{1,0:T(8,128)(2,1)} %w_out_ref.3) | copy-start | bytes 6291460
  56.0 12.5 %copy-start.7 = (bf16[1024,98]{0,1:T(8,128)(2,1)S(1)}, bf16[1024,98]{0,1:T(8,128)(2,1)}, u32[]{:S(2)}) copy-start(bf16[1024,98]{0,1:T(8,128)(2,1)} %param.19) | copy-start | bytes 602116
  56.0 24.2 %collective-permute-start.1 = (bf16[128,1024]{1,0:T(8,128)(2,1)S(1)}, bf16[128,1024]{1,0:T(8,128)(2,1)S(1)}, u32[]{:S(2)}, u32[]{:S(2)}) collective-permute-start(bf16[128,1024]{1,0:T(8,128)(2,1)S(1)} %get-tuple-element.14.refs_2_.lo_ref), channel_id=1, source_target_pairs={{1,0},{2,1},{3,2},{4,3},{5,4},{6,5},{7,6},{8,7},{9,8},{10,9},{11,1... | collective-permute-start | bytes 786440 | tf_op jit(solution)/shard_map/ppermute | solution.py:301
  92.4 29.1 %copy-start = (f32[512,98]{0,1:T(8,128)S(1)}, f32[512,98]{0,1:T(8,128)}, u32[]{:S(2)}) copy-start(f32[512,98]{0,1:T(8,128)} %param.11) | copy-start | bytes 602116
  115.3 6.2 %collective-permute-start.4 = (bf16[2,98,512]{2,1,0:T(8,128)(2,1)S(1)}, bf16[2,98,512]{2,1,0:T(8,128)(2,1)S(1)}, u32[]{:S(2)}, u32[]{:S(2)}) collective-permute-start(bf16[2,98,512]{2,1,0:T(8,128)(2,1)S(1)} %predict.1.mine_ref), channel_id=1, source_target_pairs={{0,128},{128,0},{1,129},{129,1},{2,130},{130,2},{3,131},{131,3},{4... | collective-permute-start | bytes 602120 | tf_op jit(solution)/shard_map/ppermute | solution.py:351

commit v2 on v1

--- a/solution.py
+++ b/solution.py
@@ -12,6 +12,7 @@
 NODE_DEV = 256
 CAP = 8
 LANES = 128
+GRID = (4, 4, 8)
 
 FAIR_ALPHA = 0.95
 NORM_EPS = 1e-05
@@ -21,6 +22,7 @@
 NT = (((1,), (1,)), ((), ()))
 TN = (((0,), (0,)), ((), ()))
 VMEM_SPEC = pl.BlockSpec(memory_space=pltpu.VMEM)
+HBM_SPEC = pl.BlockSpec(memory_space=pltpu.HBM)
 SMEM_SPEC = pl.BlockSpec(memory_space=pltpu.SMEM)
 
 
@@ -30,6 +32,16 @@
 
 def iota(shape, dim):
     return lax.broadcasted_iota(jnp.int32, shape, dim)
+
+
+def path_place(block, dims):
+    _, ny, nz = dims
+    x, rest = block // (ny * nz), block % (ny * nz)
+    y, z = rest // nz, rest % nz
+    turn = (x * ny + y) % 2
+    y = jnp.where(x % 2 == 1, ny - 1 - y, y) if not isinstance(block, int) else (ny - 1 - y if x % 2 else y)
+    z = jnp.where(turn == 1, nz - 1 - z, z) if not isinstance(block, int) else (nz - 1 - z if turn else z)
+    return (x * ny + y) * nz + z
 
 
 def slot_row(owner_row):
@@ -40,20 +52,35 @@
     owner_col = jnp.sum(jnp.where(row_id == col_id, wide, 0), axis=1, keepdims=True)
     earlier = (owner_col == wide) & (row_id < col_id)
     rank = jnp.sum(earlier.astype(jnp.int32), axis=0, keepdims=True)
-    return owner_row * CAP + rank
-
-
-def pack_kernel(var_count, x_ref, eo_ref, el_ref, do_ref, dl_ref, out_ref, slot_ref, aug_ref):
+    return path_place(owner_row, GRID) * CAP + rank
+
+
+def pack_kernel(
+    var_count, x_ref, eo_hbm, el_hbm, do_hbm, dl_hbm, w_hbm, out_ref, slot_ref, w_ref,
+    eo_ref, el_ref, do_ref, dl_ref, aug_ref, sems,
+):
     members, _, pts = x_ref.shape
     n_dest = out_ref.shape[0]
     slots = n_dest * CAP
+    copies = [
+        pltpu.make_async_copy(src, dst, sems.at[i])
+        for i, (src, dst) in enumerate(
+            [(eo_hbm, eo_ref), (do_hbm, do_ref), (el_hbm, el_ref), (dl_hbm, dl_ref), (w_hbm, w_ref)]
+        )
+    ]
+    for copy in copies:
+        copy.start()
+    copies[0].wait()
     enc_slot = slot_row(eo_ref[...])
+    copies[1].wait()
     dec_slot = slot_row(do_ref[...])
     slot_ref[...] = dec_slot
     slot_id = iota((slots, pts), 0)
     place = (slot_id == enc_slot).astype(F32).astype(BF16)
     request = (slot_id == dec_slot).astype(F32).astype(BF16)
     row_id = iota((LANES, pts), 0)
+    copies[2].wait()
+    copies[3].wait()
     enc_meta = jnp.where(row_id == var_count, el_ref[...] + 1, 0).astype(F32)
     dec_meta = jnp.where(row_id == var_count, dl_ref[...] + 1, 0).astype(F32)
     asked = nt_dot(request, dec_meta.astype(BF16))
@@ -66,6 +93,7 @@
             rows = rows + asked
         packed.append(rows.reshape(n_dest, 1, CAP, LANES))
     out_ref[...] = jnp.concatenate(packed, axis=1).astype(BF16)
+    copies[4].wait()
 
 
 def member_rows(ref, m):
@@ -73,7 +101,7 @@
     return ref[:, m].astype(F32).reshape(n_dest * CAP, LANES).astype(BF16)
 
 
-def encode_kernel(var_count, m, in_ref, w_ref, lo_ref, hi_ref, pooled_ref):
+def encode_kernel(var_count, m, in_ref, w_ref, lo_ref, hi_ref, pooled_ref, ea_ref, eb_ref):
     n_dest = in_ref.shape[0]
     slots = n_dest * CAP
     width = w_ref.shape[1]
@@ -88,14 +116,22 @@
     assign = assign_f.astype(BF16)
     x = member_rows(in_ref, m)[:, 0:var_count]
 
-    def embed(c, carry):
+    def embed(c, e_ref):
         cols = pl.ds(pl.multiple_of(c * chunk, chunk), chunk)
         raw = 0.5 * jnp.dot(x, w_ref[:, cols], preferred_element_type=F32)
-        embedded = (raw + raw * jnp.tanh(raw)).astype(BF16)
-        pooled_ref[:, cols] = jnp.dot(assign, embedded, preferred_element_type=F32)
-        return carry
-
-    lax.fori_loop(0, width // chunk, embed, 0)
+        e_ref[...] = (raw + raw * jnp.tanh(raw)).astype(BF16)
+
+    def pool(c, e_ref):
+        cols = pl.ds(pl.multiple_of(c * chunk, chunk), chunk)
+        pooled_ref[:, cols] = jnp.dot(assign, e_ref[...], preferred_element_type=F32)
+
+    chunks = width // chunk
+    embed(0, ea_ref)
+    for c in range(chunks):
+        here, there = (ea_ref, eb_ref) if c % 2 == 0 else (eb_ref, ea_ref)
+        if c + 1 < chunks:
+            embed(c + 1, there)
+        pool(c, here)
     step = 32
     for out_ref, first in ((lo_ref, 0), (hi_ref, HALF_WIN)):
         for r in range(0, HALF_WIN, step):
@@ -107,18 +143,25 @@
 
 
 def qkv_kernel(halves, *refs):
-    hidden_refs, w_ref, qk_ref, vt_ref = refs[:halves], refs[halves], refs[halves + 1], refs[halves + 2]
-    c = pl.program_id(0)
-    rows = jnp.concatenate([r[...] for r in hidden_refs], axis=0)
-    acc = jnp.dot(rows, w_ref[...], preferred_element_type=F32).astype(BF16)
-
-    @pl.when(c < 4)
-    def _():
-        qk_ref[...] = acc
-
-    @pl.when(c >= 4)
-    def _():
-        vt_ref[...] = acc.T
+    hidden_refs, (w_ref, qk_ref, vt_ref, rows_ref) = refs[:halves], refs[halves:]
+    width = rows_ref.shape[1]
+    half = rows_ref.shape[0] // halves
+    for i, ref in enumerate(hidden_refs):
+        rows_ref[i * half : (i + 1) * half, :] = ref[...]
+    chunk = 256
+
+    def project(cols):
+        return jnp.dot(rows_ref[...], w_ref[:, cols], preferred_element_type=F32).astype(BF16)
+
+    @pl.loop(0, 2 * width // chunk)
+    def _(c):
+        cols = pl.ds(pl.multiple_of(c * chunk, chunk), chunk)
+        qk_ref[:, cols] = project(cols)
+
+    @pl.loop(0, width // chunk)
+    def _(c):
+        rows = pl.ds(pl.multiple_of(c * chunk, chunk), chunk)
+        vt_ref[rows, :] = project(pl.ds(pl.multiple_of(2 * width + c * chunk, chunk), chunk)).T
 
 
 def attend_kernel(
@@ -126,21 +169,22 @@
     w_dec_ref, *rest,
 ):
     if m == 0:
-        out_ref, kh_ref, vth_ref, att_ref, proc_ref, left_ref, right_ref = rest
+        out_ref, kh_ref, vth_ref, att_ref, proc_ref, left_ref, right_ref, sa_ref, sb_ref, e_ref = rest
     else:
-        dec_ref, in_ref, out_ref, kh_ref, vth_ref, att_ref, proc_ref, left_ref, right_ref = rest
+        dec_ref, in_ref, out_ref, kh_ref, vth_ref, att_ref, proc_ref, left_ref, right_ref, sa_ref, sb_ref, e_ref = rest
     half, width = lo_ref.shape
     nodes = 2 * half
     head_dim = width // HEADS
-    halo = jnp.concatenate([bef_ref[...], aft_ref[...]], axis=0)
+    proc_ref[0:half, :] = bef_ref[...]
+    proc_ref[half:, :] = aft_ref[...]
     chunk = 256
 
     def project(c, carry):
         cols = pl.ds(pl.multiple_of(c * chunk, chunk), chunk)
         k_src = pl.ds(pl.multiple_of(width + c * chunk, chunk), chunk)
         v_src = pl.ds(pl.multiple_of(2 * width + c * chunk, chunk), chunk)
-        kh_ref[:, cols] = jnp.dot(halo, w_kv_ref[:, k_src], preferred_element_type=F32).astype(BF16)
-        vh = jnp.dot(halo, w_kv_ref[:, v_src], preferred_element_type=F32).astype(BF16)
+        kh_ref[:, cols] = jnp.dot(proc_ref[...], w_kv_ref[:, k_src], preferred_element_type=F32).astype(BF16)
+        vh = jnp.dot(proc_ref[...], w_kv_ref[:, v_src], preferred_element_type=F32).astype(BF16)
         vth_ref[cols, :] = vh.T
         return carry
 
@@ -159,11 +203,10 @@
     gain = head_dim ** (-0.5) * 1.4426950408889634
     base = m * nodes
 
-    def heads(p, carry):
+    def scores(p, s_ref):
         cols = pl.ds(pl.multiple_of(p * LANES, LANES), LANES)
         k_cols = pl.ds(pl.multiple_of(width + p * LANES, LANES), LANES)
         k_own = qk_ref[base : base + nodes, k_cols]
-        vt_own = vt_ref[cols, base : base + nodes]
         for side in range(2):
             row0 = side * half
             q = qk_ref[base + row0 : base + row0 + half, cols]
@@ -172,28 +215,46 @@
             s_own = nt_dot(k_own, q2)
             s_halo = nt_dot(kh_ref[row0 : row0 + half, cols], q2)
             if side == 0:
-                s0 = s_halo + left_ref[0]
-                s1 = s_own[0:half]
-                s2 = s_own[half:] + right_ref[0]
+                s_ref[side, 0:half] = s_own[0:half]
+                s_ref[side, half:nodes] = s_own[half:] + right_ref[0]
+                s_ref[side, nodes:] = s_halo + left_ref[0]
             else:
-                s0 = s_own[0:half] + left_ref[1]
-                s1 = s_own[half:]
-                s2 = s_halo + right_ref[1]
+                s_ref[side, 0:half] = s_own[0:half] + left_ref[1]
+                s_ref[side, half:nodes] = s_own[half:]
+                s_ref[side, nodes:] = s_halo + right_ref[1]
+
+    def finish(p, s_ref):
+        cols = pl.ds(pl.multiple_of(p * LANES, LANES), LANES)
+        blocks = (slice(0, half), slice(half, nodes), slice(nodes, nodes + half))
+        for side in range(2):
+            row0 = side * half
+            s0, s1, s2 = (s_ref[side, b] for b in blocks)
             top = jnp.max(jnp.maximum(jnp.maximum(s0, s1), s2), axis=0, keepdims=True)
-            e0, e1, e2 = (jnp.exp2((s - top) * gain) for s in (s0, s1, s2))
-            inv = 1.0 / jnp.sum(e0 + e1 + e2, axis=0, keepdims=True)
-            p0, p1, p2 = ((e * inv).astype(BF16) for e in (e0, e1, e2))
-            if side == 0:
-                p_halo, p_own = p0, jnp.concatenate([p1, p2], axis=0)
-            else:
-                p_own, p_halo = jnp.concatenate([p0, p1], axis=0), p2
-            out = jnp.dot(vt_own, p_own, preferred_element_type=F32)
+            total = None
+            for b in blocks:
+                e = jnp.exp2((s_ref[side, b] - top) * gain)
+                e_ref[side, b] = e
+                total = e if total is None else total + e
+            inv = 1.0 / jnp.sum(total, axis=0, keepdims=True)
+            p_own = (e_ref[side, 0:nodes] * inv).astype(BF16)
+            p_halo = (e_ref[side, nodes:] * inv).astype(BF16)
+            out = jnp.dot(vt_ref[cols, base : base + nodes], p_own, preferred_element_type=F32)
             out += jnp.dot(vth_ref[cols, row0 : row0 + half], p_halo, preferred_element_type=F32)
             pair = jnp.concatenate([out[0:head_dim, 0:half], out[head_dim:, half:]], axis=0)
             att_ref[row0 : row0 + half, cols] = pair.T.astype(BF16)
+
+    pairs = HEADS // 2
+    scores(0, sa_ref)
+
+    def heads(i, carry):
+        p = 2 * i
+        scores(p + 1, sb_ref)
+        finish(p, sa_ref)
+        scores(jnp.minimum(p + 2, pairs - 1), sa_ref)
+        finish(p + 1, sb_ref)
         return carry
 
-    lax.fori_loop(0, HEADS // 2, heads, 0)
+    lax.fori_loop(0, pairs // 2, heads, 0)
 
     def mix(c, carry):
         cols = pl.ds(pl.multiple_of(c * chunk, chunk), chunk)
@@ -275,51 +336,54 @@
     rows = [a.reshape(1, pts) for a in (enc_owner, enc_local, dec_owner, dec_local)]
     wire = jax.ShapeDtypeStruct((n_space, members, CAP, LANES), BF16)
 
-    outgoing, dec_slot = pl.pallas_call(
+    row_shape = pltpu.VMEM((1, pts), jnp.int32)
+    outgoing, dec_slot, w_enc = pl.pallas_call(
         functools.partial(pack_kernel, var_count),
-        out_shape=(wire, jax.ShapeDtypeStruct((1, pts), jnp.int32)),
-        scratch_shapes=[pltpu.VMEM((LANES, pts), F32)],
+        in_specs=[VMEM_SPEC] + [HBM_SPEC] * 5,
+        out_shape=(
+            wire,
+            jax.ShapeDtypeStruct((1, pts), jnp.int32),
+            jax.ShapeDtypeStruct(w_embed.shape, BF16),
+        ),
+        scratch_shapes=[row_shape] * 4
+        + [pltpu.VMEM((LANES, pts), F32), pltpu.SemaphoreType.DMA((5,))],
         compiler_params=params(),
+        cost_estimate=cost(2),
         name="pack",
-    )(states, *rows)
+    )(states, *rows, w_embed)
+    at = [path_place(b, GRID) for b in range(n_space)]
+    ends = jnp.stack([(me == at[0]), (me == at[-1])]).astype(jnp.int32)
+    outgoing, ends = lax.optimization_barrier((outgoing, ends))
     arrived = lax.all_to_all(outgoing, "space", 0, 0, tiled=True)
 
     half_shape = jax.ShapeDtypeStruct((half, width), BF16)
-    up = [(i, (i + 1) % n_space) for i in range(n_space)]
+    up = [(at[i], at[(i + 1) % n_space]) for i in range(n_space)]
     down = [(j, i) for i, j in up]
     hidden, halos = [], []
     for m in range(members):
         lo, hi = pl.pallas_call(
             functools.partial(encode_kernel, var_count, m),
             out_shape=(half_shape, half_shape),
-            scratch_shapes=[pltpu.VMEM((nodes, width), F32)],
+            scratch_shapes=[pltpu.VMEM((nodes, width), F32)] + [pltpu.VMEM((slots, 256), BF16)] * 2,
             compiler_params=params(),
             cost_estimate=cost(3),
             name=f"encode{m}",
-        )(arrived, w_embed)
+        )(arrived, w_enc)
         hidden += [lo, hi]
         halos.append((lax.ppermute(hi, "space", up), lax.ppermute(lo, "space", down)))
 
-    step = 512
-    half_spec = pl.BlockSpec((half, width), lambda c: (0, 0))
     qk, vt = pl.pallas_call(
         functools.partial(qkv_kernel, len(hidden)),
-        grid=(3 * width // step,),
-        in_specs=[half_spec] * len(hidden) + [pl.BlockSpec((width, step), lambda c: (0, c))],
-        out_specs=(
-            pl.BlockSpec((members * nodes, step), lambda c: (0, jnp.minimum(c, 3))),
-            pl.BlockSpec((step, members * nodes), lambda c: (jnp.maximum(c - 4, 0), 0)),
-        ),
         out_shape=(
             jax.ShapeDtypeStruct((members * nodes, 2 * width), BF16),
             jax.ShapeDtypeStruct((width, members * nodes), BF16),
         ),
+        scratch_shapes=[pltpu.VMEM((members * nodes, width), BF16)],
         cost_estimate=cost(5),
         compiler_params=params(),
         name="qkv",
     )(*hidden, w_qkv)
 
-    ends = jnp.stack([(me == 0), (me == n_space - 1)]).astype(jnp.int32)
     decoded = None
     for m in range(members):
         extra = () if m == 0 else (decoded, arrived)
@@ -334,6 +398,9 @@
                 pltpu.VMEM((nodes, width), BF16),
                 pltpu.VMEM((2, half, nodes), F32),
                 pltpu.VMEM((2, half, nodes), F32),
+                pltpu.VMEM((2, nodes + half, nodes), F32),
+                pltpu.VMEM((2, nodes + half, nodes), F32),
+                pltpu.VMEM((2, nodes + half, nodes), F32),
             ],
             compiler_params=params(),
             cost_estimate=cost(8),

time: 123 us -> 104 us (0.85)
  blocking collectives: 22.3 us -> 57.6 us
  starting transfers between devices: 35.3 us -> 10.6 us
  waiting for transfers between devices: 19.3 us -> 0.27 us
  Pallas kernels: 39.1 us -> 29.2 us
    all_to_all x0 -> x1, blocking collectives: none -> 35.3 us  [on_device(): arrived = lax.all_to_all(outgoing, 'space', 0, 0, tiled=True)]
    all_to_all x1 -> x0, waiting for transfers between devices: 19.1 us -> none  [on_device(): arrived = lax.all_to_all(outgoing, 'space', 0, 0, tiled=True)]
    all_to_all x1 -> x0, starting transfers between devices: 16.3 us -> none  [on_device(): arrived = lax.all_to_all(outgoing, 'space', 0, 0, tiled=True)]
    ppermute x2, starting transfers between devices: 12.9 us -> 4.51 us  [on_device(): lax.ppermute(lo, 'space', down)]
    pallas_call x2, Pallas kernels: 23.9 us -> 16 us  [on_device(): pl.pallas_call(functools.partial(attend_kernel, var_count, m), in_specs=[...]
    pallas_call x2, Pallas kernels: 6.07 us -> 3.64 us  [on_device(): pl.pallas_call(functools.partial(encode_kernel, var_count, m), out_shape=...]
  transfers between devices with their start and end apart: 6 -> 5, of which waited for: 2 -> 1; matrix products, arithmetic and copies ran while one was open for 1% -> 1% of each run, Pallas kernels for 17% -> 15%
where the time goes in v2:
time: 104 us
  blocking collectives  57.6 us (55%)
  Pallas kernels  29.2 us (28%)
  starting transfers between devices  10.6 us (10%)
  local copies, waits for them, and re-layouts  5.47 us (5%)
    all_to_all x1, blocking collectives, on_device(): arrived = lax.all_to_all(outgoing, 'space', 0, 0, tiled=True)  35.3 us
    all_to_all x1, blocking collectives, on_device(): returned = lax.all_to_all(replies, 'space', 0, 0, tiled=True)  22.3 us
    pallas_call x2, Pallas kernels, on_device(): pl.pallas_call(functools.partial(attend_kernel, var_count, m), in_specs=[...  16 us
    pallas_call x1, Pallas kernels, on_device(): pl.pallas_call(functools.partial(qkv_kernel, len(hidden)), out_shape=(jax...  5.72 us
    unnamed x22, local copies, waits for them, and re-layouts  5.47 us
    ppermute x1, starting transfers between devices, on_device(): other = lax.ppermute(predicted, 'member', [(0, 1), (1, 0)])  5.07 us
    ppermute x2, starting transfers between devices, on_device(): lax.ppermute(lo, 'space', down)  4.51 us
    pallas_call x2, Pallas kernels, on_device(): pl.pallas_call(functools.partial(encode_kernel, var_count, m), out_shape=...  3.64 us
  transfers between devices with their start and end apart: 5, of which 1 were waited for; matrix products, arithmetic and copies ran while one was open for 1% of the time, Pallas kernels for 15%

profile of v2, /device:TPU:1, one launch (start us, length us, event | category | flops | bytes accessed | tf_op | source)
XLA Modules:
  0.0 103.9 jit_solution(1484655408745149411)
XLA Ops:
  0.6 1.0 copy.15
  1.6 0.1 add_convert_fusion.ends_ref
  1.7 0.0 copy-start.2
  1.7 0.9 copy-done.2
  2.6 0.0 copy-start.4
  2.6 0.7 copy-done.4
  3.3 0.0 copy-start.5
  3.3 0.7 copy-done.5
  4.0 0.0 copy-start.6
  4.0 0.7 copy-done.6
  4.7 0.0 copy-start.7
  4.7 0.7 copy-done.7
  5.3 2.3 %pack.1 = (bf16[128,2,8,128]{3,2,1,0:T(8,128)(2,1)S(1)}, s32[1,512]{1,0:T(1,128)S(1)}, bf16[98,1024]{1,0:T(8,128)(2,1)S(1)}) custom-call(bf16[2,98,512]{2,1,0:T(8,128)(2,1)S(1)} %bitcast.14, s32[1,512]{1,0:T(1,128)S(1)} %bitcast.21, s32[1,512]{1,0:T(1,128)S(1)} %bitcast.22, s32[1,512]{1,0:T(1,128)S(1)} %bitcast.23, s32[1,512]{1,0:T(1,128)S(1)} %bitcast.24, ...), custom_call_target="tpu_custom_call" | custom-call | flops 1400000000 | bytes 1048576 | tf_op jit(solution)/shard_map/pack/pallas_call | solution.py:340
  7.6 35.3 %all_to_all.10.in_ref.rest_1_ = bf16[128,2,8,128]{3,2,1,0:T(8,128)(2,1)S(1)} all-to-all(bf16[128,2,8,128]{3,2,1,0:T(8,128)(2,1)S(1)} %get-tuple-element.16), channel_id=1, replica_groups=mesh['member'=2,'space'=128] {'space'}, dimensions={0} | all-to-all | bytes 1048576 | tf_op jit(solution)/shard_map/all_to_all | solution.py:357
  42.9 0.0 slice-start
  42.9 1.8 %encode0.1 = (bf16[128,1024]{1,0:T(8,128)(2,1)S(1)}, bf16[128,1024]{1,0:T(8,128)(2,1)S(1)}) custom-call(bf16[128,2,8,128]{3,2,1,0:T(8,128)(2,1)S(1)} %all_to_all.10.in_ref.rest_1_, bf16[98,1024]{1,0:T(8,128)(2,1)S(1)} %get-tuple-element.17.w_ref), custom_call_target="tpu_custom_call" | custom-call | flops 2100000000 | bytes 1048576 | tf_op jit(solution)/shard_map/encode0/pallas_call | solution.py:364
  44.8 0.0 slice-start.1
  44.8 0.9 collective-permute-start.2
  45.7 1.9 %collective-permute-start.3 = (bf16[128,1024]{1,0:T(8,128)(2,1)S(1)}, bf16[128,1024]{1,0:T(8,128)(2,1)S(1)}, u32[]{:S(2)}, u32[]{:S(2)}) collective-permute-start(bf16[128,1024]{1,0:T(8,128)(2,1)S(1)} %get-tuple-element.18.refs_0_.lo_ref), channel_id=1, source_target_pairs={{1,0},{2,1},{3,2},{4,3},{5,4},{6,5},{7,6},{15,7},{14,15},{13,14},{... | collective-permute-start | bytes 786440 | tf_op jit(solution)/shard_map/ppermute | solution.py:373
  47.5 1.8 %encode1.1 = (bf16[128,1024]{1,0:T(8,128)(2,1)S(1)}, bf16[128,1024]{1,0:T(8,128)(2,1)S(1)}) custom-call(bf16[128,2,8,128]{3,2,1,0:T(8,128)(2,1)S(1)} %all_to_all.10.in_ref.rest_1_, bf16[98,1024]{1,0:T(8,128)(2,1)S(1)} %get-tuple-element.17.w_ref), custom_call_target="tpu_custom_call" | custom-call | flops 2100000000 | bytes 1048576 | tf_op jit(solution)/shard_map/encode1/pallas_call | solution.py:364
  49.3 0.1 collective-permute-start
  49.4 0.0 copy-start.1
  49.4 0.0 copy-start.3
  49.5 2.6 %collective-permute-start.1 = (bf16[128,1024]{1,0:T(8,128)(2,1)S(1)}, bf16[128,1024]{1,0:T(8,128)(2,1)S(1)}, u32[]{:S(2)}, u32[]{:S(2)}) collective-permute-start(bf16[128,1024]{1,0:T(8,128)(2,1)S(1)} %get-tuple-element.20.refs_2_.lo_ref), channel_id=1, source_target_pairs={{1,0},{2,1},{3,2},{4,3},{5,4},{6,5},{7,6},{15,7},{14,15},{13,14},{... | collective-permute-start | bytes 786440 | tf_op jit(solution)/shard_map/ppermute | solution.py:373
  52.1 0.0 slice-done
  52.1 0.0 slice-done.1
  52.1 5.7 %qkv.1 = (bf16[512,2048]{1,0:T(8,128)(2,1)S(1)}, bf16[1024,512]{1,0:T(8,128)(2,1)S(1)}) custom-call(bf16[128,1024]{1,0:T(8,128)(2,1)S(1)} %get-tuple-element.18.refs_0_.lo_ref, bf16[128,1024]{1,0:T(8,128)(2,1)S(1)} %get-tuple-element.19.refs_1_.hi_ref, bf16[128,1024]{1,0:T(8,128)(2,1)S(1)} %get-tuple-element.20.refs_2_.lo_ref, ...), custom_call_target="tpu_custom_call" | custom-call | flops 3500000000 | bytes 1048576 | tf_op jit(solution)/shard_map/qkv/pallas_call | solution.py:375
  57.8 0.0 collective-permute-done.2.bef_ref
  57.9 0.0 collective-permute-done.3.aft_ref
  57.9 0.0 copy-done.1
  57.9 0.0 copy-done.3
  57.9 7.7 %attend0.1.rest_0_ = bf16[256,128]{1,0:T(8,128)(2,1)S(1)} custom-call(s32[2]{0:T(128)S(1)} %add_convert_fusion.ends_ref, bf16[512,2048]{1,0:T(8,128)(2,1)S(1)} %get-tuple-element.22.qk_ref, bf16[1024,512]{1,0:T(8,128)(2,1)S(1)} %get-tuple-element.23.vt_ref, bf16[128,1024]{1,0:T(8,128)(2,1)S(1)} %get-tuple-element.18.refs_0_.lo_ref, ...), custom_call_target="tpu_custom_call" | custom-call | flops 5600000000 | bytes 1048576 | tf_op jit(solution)/shard_map/attend0/pallas_call | solution.py:390
  65.6 0.0 collective-permute-done.bef_ref
  65.6 0.0 collective-permute-done.1.aft_ref
  65.6 8.3 %attend1.1 = bf16[128,2,8,128]{3,2,1,0:T(8,128)(2,1)S(1)} custom-call(s32[2]{0:T(128)S(1)} %add_convert_fusion.ends_ref, bf16[512,2048]{1,0:T(8,128)(2,1)S(1)} %get-tuple-element.22.qk_ref, bf16[1024,512]{1,0:T(8,128)(2,1)S(1)} %get-tuple-element.23.vt_ref, bf16[128,1024]{1,0:T(8,128)(2,1)S(1)} %get-tuple-element.20.refs_2_.lo_ref, ...), custom_call_target="tpu_custom_call" | custom-call | flops 5600000000 | bytes 1048576 | tf_op jit(solution)/shard_map/attend1/pallas_call | solution.py:390
  73.9 0.0 copy-start
  73.9 22.3 %all_to_all.11.back_ref = bf16[128,2,8,128]{3,2,1,0:T(8,128)(2,1)S(1)} all-to-all(bf16[128,2,8,128]{3,2,1,0:T(8,128)(2,1)S(1)} %attend1.1), channel_id=1, replica_groups=mesh['member'=2,'space'=128] {'space'}, dimensions={0} | all-to-all | bytes 1048576 | tf_op jit(solution)/shard_map/all_to_all | solution.py:411
  96.2 0.6 predict.1.mine_ref
  96.8 5.1 %collective-permute-start.4 = (bf16[2,98,512]{2,1,0:T(8,128)(2,1)S(1)}, bf16[2,98,512]{2,1,0:T(8,128)(2,1)S(1)}, u32[]{:S(2)}, u32[]{:S(2)}) collective-permute-start(bf16[2,98,512]{2,1,0:T(8,128)(2,1)S(1)} %predict.1.mine_ref), channel_id=1, source_target_pairs={{0,128},{128,0},{1,129},{129,1},{2,130},{130,2},{3,131},{131,3},{4... | collective-permute-start | bytes 602120 | tf_op jit(solution)/shard_map/ppermute | solution.py:418
  101.9 0.8 copy.13
  102.7 0.3 collective-permute-done.4.other_ref
  103.0 0.0 copy-done
  103.0 0.9 score.1
  (1 shorter events, 0.0 us)
Async XLA Ops:
  1.7 0.9 copy-start.2
  2.6 0.7 copy-start.4
  3.3 0.7 copy-start.5
  4.0 0.7 copy-start.6
  4.7 0.7 copy-start.7
  42.9 9.2 %slice-start = ((s8[6291456]{0:T(1024)(128)(4,1)}), s8[4194304]{0:T(1024)(128)(4,1)S(1)}, s32[]{:S(2)}) async-start(s8[6291456]{0:T(1024)(128)(4,1)} %bitcast.17), calls=%async_computation.2 | async-start | bytes 8388608
  44.8 7.4 %slice-start.1 = ((s8[6291456]{0:T(1024)(128)(4,1)}), s8[2097152]{0:T(1024)(128)(4,1)S(1)}, s32[]{:S(2)}) async-start(s8[6291456]{0:T(1024)(128)(4,1)} %bitcast.17), calls=%async_computation.3 | async-start | bytes 4194304
  44.8 13.1 %collective-permute-start.2 = (bf16[128,1024]{1,0:T(8,128)(2,1)S(1)}, bf16[128,1024]{1,0:T(8,128)(2,1)S(1)}, u32[]{:S(2)}, u32[]{:S(2)}) collective-permute-start(bf16[128,1024]{1,0:T(8,128)(2,1)S(1)} %get-tuple-element.19.refs_1_.hi_ref), channel_id=1, source_target_pairs={{0,1},{1,2},{2,3},{3,4},{4,5},{5,6},{6,7},{7,15},{15,14},{14,13},{... | collective-permute-start | bytes 786440 | tf_op jit(solution)/shard_map/ppermute | solution.py:373
  45.7 12.2 %collective-permute-start.3 = (bf16[128,1024]{1,0:T(8,128)(2,1)S(1)}, bf16[128,1024]{1,0:T(8,128)(2,1)S(1)}, u32[]{:S(2)}, u32[]{:S(2)}) collective-permute-start(bf16[128,1024]{1,0:T(8,128)(2,1)S(1)} %get-tuple-element.18.refs_0_.lo_ref), channel_id=1, source_target_pairs={{1,0},{2,1},{3,2},{4,3},{5,4},{6,5},{7,6},{15,7},{14,15},{13,14},{... | collective-permute-start | bytes 786440 | tf_op jit(solution)/shard_map/ppermute | solution.py:373
  49.3 16.3 %collective-permute-start = (bf16[128,1024]{1,0:T(8,128)(2,1)S(1)}, bf16[128,1024]{1,0:T(8,128)(2,1)S(1)}, u32[]{:S(2)}, u32[]{:S(2)}) collective-permute-start(bf16[128,1024]{1,0:T(8,128)(2,1)S(1)} %get-tuple-element.21.refs_3_.hi_ref), channel_id=1, source_target_pairs={{0,1},{1,2},{2,3},{3,4},{4,5},{5,6},{6,7},{7,15},{15,14},{14,13},{... | collective-permute-start | bytes 786440 | tf_op jit(solution)/shard_map/ppermute | solution.py:373
  49.4 8.4 %copy-start.1 = (bf16[1024,1024]{1,0:T(8,128)(2,1)S(1)}, bf16[1024,1024]{1,0:T(8,128)(2,1)}, u32[]{:S(2)}) copy-start(bf16[1024,1024]{1,0:T(8,128)(2,1)} %w_out_ref.3) | copy-start | bytes 6291460
  49.4 8.4 %copy-start.3 = (bf16[1024,98]{0,1:T(8,128)(2,1)S(1)}, bf16[1024,98]{0,1:T(8,128)(2,1)}, u32[]{:S(2)}) copy-start(bf16[1024,98]{0,1:T(8,128)(2,1)} %param.19) | copy-start | bytes 602116
  49.5 16.2 %collective-permute-start.1 = (bf16[128,1024]{1,0:T(8,128)(2,1)S(1)}, bf16[128,1024]{1,0:T(8,128)(2,1)S(1)}, u32[]{:S(2)}, u32[]{:S(2)}) collective-permute-start(bf16[128,1024]{1,0:T(8,128)(2,1)S(1)} %get-tuple-element.20.refs_2_.lo_ref), channel_id=1, source_target_pairs={{1,0},{2,1},{3,2},{4,3},{5,4},{6,5},{7,6},{15,7},{14,15},{13,14},{... | collective-permute-start | bytes 786440 | tf_op jit(solution)/shard_map/ppermute | solution.py:373
  73.9 29.1 %copy-start = (f32[512,98]{0,1:T(8,128)S(1)}, f32[512,98]{0,1:T(8,128)}, u32[]{:S(2)}) copy-start(f32[512,98]{0,1:T(8,128)} %param.11) | copy-start | bytes 602116
  96.8 6.2 %collective-permute-start.4 = (bf16[2,98,512]{2,1,0:T(8,128)(2,1)S(1)}, bf16[2,98,512]{2,1,0:T(8,128)(2,1)S(1)}, u32[]{:S(2)}, u32[]{:S(2)}) collective-permute-start(bf16[2,98,512]{2,1,0:T(8,128)(2,1)S(1)} %predict.1.mine_ref), channel_id=1, source_target_pairs={{0,128},{128,0},{1,129},{129,1},{2,130},{130,2},{3,131},{131,3},{4... | collective-permute-start | bytes 602120 | tf_op jit(solution)/shard_map/ppermute | solution.py:418

commit v3 on v2

--- a/solution.py
+++ b/solution.py
@@ -13,6 +13,7 @@
 CAP = 8
 LANES = 128
 GRID = (4, 4, 8)
+Y_BITS, Z_BITS = 2, 3
 
 FAIR_ALPHA = 0.95
 NORM_EPS = 1e-05
@@ -23,7 +24,6 @@
 TN = (((0,), (0,)), ((), ()))
 VMEM_SPEC = pl.BlockSpec(memory_space=pltpu.VMEM)
 HBM_SPEC = pl.BlockSpec(memory_space=pltpu.HBM)
-SMEM_SPEC = pl.BlockSpec(memory_space=pltpu.SMEM)
 
 
 def nt_dot(a, b):
@@ -34,38 +34,43 @@
     return lax.broadcasted_iota(jnp.int32, shape, dim)
 
 
-def path_place(block, dims):
-    _, ny, nz = dims
-    x, rest = block // (ny * nz), block % (ny * nz)
-    y, z = rest // nz, rest % nz
-    turn = (x * ny + y) % 2
-    y = jnp.where(x % 2 == 1, ny - 1 - y, y) if not isinstance(block, int) else (ny - 1 - y if x % 2 else y)
-    z = jnp.where(turn == 1, nz - 1 - z, z) if not isinstance(block, int) else (nz - 1 - z if turn else z)
-    return (x * ny + y) * nz + z
+def path_place(block):
+    _, ny, nz = GRID
+    line, z = block >> Z_BITS, block & (nz - 1)
+    x, y = line >> Y_BITS, line & (ny - 1)
+    z = z + (line & 1) * (nz - 1 - 2 * z)
+    y = y + (x & 1) * (ny - 1 - 2 * y)
+    return (((x << Y_BITS) + y) << Z_BITS) + z
 
 
 def slot_row(owner_row):
     pts = owner_row.shape[1]
-    square = (pts, pts)
-    wide = jnp.broadcast_to(owner_row, square)
-    row_id, col_id = iota(square, 0), iota(square, 1)
-    owner_col = jnp.sum(jnp.where(row_id == col_id, wide, 0), axis=1, keepdims=True)
-    earlier = (owner_col == wide) & (row_id < col_id)
-    rank = jnp.sum(earlier.astype(jnp.int32), axis=0, keepdims=True)
-    return path_place(owner_row, GRID) * CAP + rank
+    owner = owner_row.astype(F32)
+    owner_col = jnp.broadcast_to(owner, (8, pts)).T[:, 0:1]
+    block = LANES
+    ahead = iota((block, block), 0) < iota((block, block), 1)
+    ranks = []
+    for c in range(0, pts, block):
+        wide = jnp.broadcast_to(owner[:, c : c + block], (block, block))
+        count = jnp.where(ahead & (owner_col[c : c + block] == wide), 1.0, 0.0)
+        for r in range(0, c, block):
+            count += jnp.where(owner_col[r : r + block] == wide, 1.0, 0.0)
+        ranks.append(jnp.sum(count, axis=0, keepdims=True))
+    rank = jnp.concatenate(ranks, axis=1).astype(jnp.int32)
+    return path_place(owner_row) * CAP + rank
 
 
 def pack_kernel(
-    var_count, x_ref, eo_hbm, el_hbm, do_hbm, dl_hbm, w_hbm, out_ref, slot_ref, w_ref,
-    eo_ref, el_ref, do_ref, dl_ref, aug_ref, sems,
+    var_count, x_hbm, eo_hbm, el_hbm, do_hbm, dl_hbm, w_hbm, out_ref, slot_ref, w_ref, states_ref,
+    x_ref, eo_ref, el_ref, do_ref, dl_ref, aug_ref, sems,
 ):
-    members, _, pts = x_ref.shape
+    members, _, pts = states_ref.shape
     n_dest = out_ref.shape[0]
     slots = n_dest * CAP
     copies = [
         pltpu.make_async_copy(src, dst, sems.at[i])
         for i, (src, dst) in enumerate(
-            [(eo_hbm, eo_ref), (do_hbm, do_ref), (el_hbm, el_ref), (dl_hbm, dl_ref), (w_hbm, w_ref)]
+            [(eo_hbm, eo_ref), (do_hbm, do_ref), (el_hbm, el_ref), (dl_hbm, dl_ref), (x_hbm, x_ref), (w_hbm, w_ref)]
         )
     ]
     for copy in copies:
@@ -85,15 +90,18 @@
     dec_meta = jnp.where(row_id == var_count, dl_ref[...] + 1, 0).astype(F32)
     asked = nt_dot(request, dec_meta.astype(BF16))
     packed = []
+    copies[4].wait()
     for m in range(members):
         aug_ref[...] = enc_meta if m == 0 else jnp.zeros_like(enc_meta)
-        aug_ref[0:var_count, :] = x_ref[m].astype(F32)
+        field = x_ref[:, m, :]
+        aug_ref[0:var_count, :] = field.astype(F32)
+        states_ref[m] = field
         rows = nt_dot(place, aug_ref[...].astype(BF16))
         if m == 1:
             rows = rows + asked
         packed.append(rows.reshape(n_dest, 1, CAP, LANES))
     out_ref[...] = jnp.concatenate(packed, axis=1).astype(BF16)
-    copies[4].wait()
+    copies[5].wait()
 
 
 def member_rows(ref, m):
@@ -165,7 +173,7 @@
 
 
 def attend_kernel(
-    var_count, m, ends_ref, qk_ref, vt_ref, lo_ref, hi_ref, bef_ref, aft_ref, w_kv_ref, w_out_ref,
+    var_count, m, first_at, last_at, qk_ref, vt_ref, lo_ref, hi_ref, bef_ref, aft_ref, w_kv_ref, w_out_ref,
     w_dec_ref, *rest,
 ):
     if m == 0:
@@ -173,6 +181,8 @@
     else:
         dec_ref, in_ref, out_ref, kh_ref, vth_ref, att_ref, proc_ref, left_ref, right_ref, sa_ref, sb_ref, e_ref = rest
     half, width = lo_ref.shape
+    me = lax.axis_index("space")
+    at_first, at_last = (me == first_at).astype(jnp.int32), (me == last_at).astype(jnp.int32)
     nodes = 2 * half
     head_dim = width // HEADS
     proc_ref[0:half, :] = bef_ref[...]
@@ -195,10 +205,10 @@
     query_id = jnp.where(query_id >= half, query_id - half, query_id)
     big = 4 * half
     zero, low = jnp.zeros((half, 2 * half), F32), jnp.full((half, 2 * half), -1e30, F32)
-    left_ref[0] = jnp.where(key_id >= query_id + ends_ref[0] * big, zero, low)
+    left_ref[0] = jnp.where(key_id >= query_id + at_first * big, zero, low)
     left_ref[1] = jnp.where(key_id >= query_id, zero, low)
     right_ref[0] = jnp.where(key_id <= query_id, zero, low)
-    right_ref[1] = jnp.where(key_id + ends_ref[1] * big <= query_id, zero, low)
+    right_ref[1] = jnp.where(key_id + at_last * big <= query_id, zero, low)
     even = iota((half, LANES), 1) < head_dim
     gain = head_dim ** (-0.5) * 1.4426950408889634
     base = m * nodes
@@ -212,8 +222,8 @@
             q = qk_ref[base + row0 : base + row0 + half, cols]
             none = jnp.zeros_like(q)
             q2 = jnp.concatenate([jnp.where(even, q, none), jnp.where(even, none, q)], axis=0)
-            s_own = nt_dot(k_own, q2)
-            s_halo = nt_dot(kh_ref[row0 : row0 + half, cols], q2)
+            s_all = nt_dot(jnp.concatenate([k_own, kh_ref[row0 : row0 + half, cols]], axis=0), q2)
+            s_own, s_halo = s_all[0:nodes], s_all[nodes:]
             if side == 0:
                 s_ref[side, 0:half] = s_own[0:half]
                 s_ref[side, half:nodes] = s_own[half:] + right_ref[0]
@@ -327,33 +337,32 @@
     w_decode,
 ):
     n_space = lax.axis_size("space")
-    me = lax.axis_index("space")
     members, pts, var_count = initial_states.shape
     width = w_embed.shape[1]
     nodes, half = NODE_DEV, HALF_WIN
     slots = n_space * CAP
-    states = jnp.transpose(initial_states, (0, 2, 1))
-    rows = [a.reshape(1, pts) for a in (enc_owner, enc_local, dec_owner, dec_local)]
+    in_hbm = functools.partial(pltpu.with_memory_space_constraint, memory_space=pltpu.HBM)
+    rows = [in_hbm(a.reshape(1, pts)) for a in (enc_owner, enc_local, dec_owner, dec_local)]
     wire = jax.ShapeDtypeStruct((n_space, members, CAP, LANES), BF16)
 
     row_shape = pltpu.VMEM((1, pts), jnp.int32)
-    outgoing, dec_slot, w_enc = pl.pallas_call(
+    outgoing, dec_slot, w_enc, states = pl.pallas_call(
         functools.partial(pack_kernel, var_count),
-        in_specs=[VMEM_SPEC] + [HBM_SPEC] * 5,
+        in_specs=[HBM_SPEC] * 6,
         out_shape=(
             wire,
             jax.ShapeDtypeStruct((1, pts), jnp.int32),
             jax.ShapeDtypeStruct(w_embed.shape, BF16),
+            jax.ShapeDtypeStruct((members, var_count, pts), BF16),
         ),
-        scratch_shapes=[row_shape] * 4
-        + [pltpu.VMEM((LANES, pts), F32), pltpu.SemaphoreType.DMA((5,))],
+        scratch_shapes=[pltpu.VMEM((var_count, members, pts), BF16)]
+        + [row_shape] * 4
+        + [pltpu.VMEM((LANES, pts), F32), pltpu.SemaphoreType.DMA((6,))],
         compiler_params=params(),
         cost_estimate=cost(2),
         name="pack",
-    )(states, *rows, w_embed)
-    at = [path_place(b, GRID) for b in range(n_space)]
-    ends = jnp.stack([(me == at[0]), (me == at[-1])]).astype(jnp.int32)
-    outgoing, ends = lax.optimization_barrier((outgoing, ends))
+    )(in_hbm(jnp.transpose(initial_states, (2, 0, 1))), *rows, in_hbm(w_embed))
+    at = [path_place(b) for b in range(n_space)]
     arrived = lax.all_to_all(outgoing, "space", 0, 0, tiled=True)
 
     half_shape = jax.ShapeDtypeStruct((half, width), BF16)
@@ -388,8 +397,7 @@
     for m in range(members):
         extra = () if m == 0 else (decoded, arrived)
         decoded = pl.pallas_call(
-            functools.partial(attend_kernel, var_count, m),
-            in_specs=[SMEM_SPEC] + [VMEM_SPEC] * (9 + len(extra)),
+            functools.partial(attend_kernel, var_count, m, at[0], at[-1]),
             out_shape=jax.ShapeDtypeStruct((nodes, LANES), BF16) if m == 0 else wire,
             scratch_shapes=[
                 pltpu.VMEM((nodes, width), BF16),
@@ -405,7 +413,7 @@
             compiler_params=params(),
             cost_estimate=cost(8),
             name=f"attend{m}",
-        )(ends, qk, vt, *hidden[2 * m : 2 * m + 2], *halos[m], w_qkv, w_out, w_decode.T, *extra)
+        )(qk, vt, *hidden[2 * m : 2 * m + 2], *halos[m], w_qkv, w_out, w_decode.T, *extra)
     replies = decoded
 
     returned = lax.all_to_all(replies, "space", 0, 0, tiled=True)

time: 104 us -> 99.4 us (0.956)
  local copies, waits for them, and re-layouts: 5.47 us -> 0.86 us
    unnamed x22 -> x11, local copies, waits for them, and re-layouts: 5.47 us -> 0.86 us
where the time goes in v3:
time: 99.4 us; the launch traced here: 99.2 us
  blocking collectives  57.5 us (58%)
  Pallas kernels  29.1 us (29%)
  starting transfers between devices  10.6 us (11%)
    all_to_all x1, blocking collectives, on_device(): arrived = lax.all_to_all(outgoing, 'space', 0, 0, tiled=True)  35.3 us
    all_to_all x1, blocking collectives, on_device(): returned = lax.all_to_all(replies, 'space', 0, 0, tiled=True)  22.3 us
    pallas_call x2, Pallas kernels, on_device(): pl.pallas_call(functools.partial(attend_kernel, var_count, m, at[0], at[-...  14.8 us
    pallas_call x1, Pallas kernels, on_device(): pl.pallas_call(functools.partial(qkv_kernel, len(hidden)), out_shape=(jax...  5.72 us
    ppermute x1, starting transfers between devices, on_device(): other = lax.ppermute(predicted, 'member', [(0, 1), (1, 0)])  5.12 us
    ppermute x2, starting transfers between devices, on_device(): lax.ppermute(lo, 'space', down)  4.51 us
    pallas_call x2, Pallas kernels, on_device(): pl.pallas_call(functools.partial(encode_kernel, var_count, m), out_shape=...  3.61 us
    pallas_call x1, Pallas kernels, on_device(): pl.pallas_call(functools.partial(pack_kernel, var_count), in_specs=[HBM_S...  3.46 us
  transfers between devices with their start and end apart: 5, of which 1 were waited for; matrix products, arithmetic and copies ran while one was open for 1% of the time, Pallas kernels for 15%

profile of v3, /device:TPU:1, one launch (start us, length us, event | category | flops | bytes accessed | tf_op | source)
XLA Modules:
  0.0 99.2 jit_solution(16712449598677011300)
XLA Ops:
  0.6 3.5 %pack.1 = (bf16[128,2,8,128]{3,2,1,0:T(8,128)(2,1)S(1)}, s32[1,512]{1,0:T(1,128)S(1)}, bf16[98,1024]{1,0:T(8,128)(2,1)S(1)}, bf16[2,98,512]{2,1,0:T(8,128)(2,1)S(1)}) custom-call(bf16[98,2,512]{2,1,0:T(2,128)(2,1)} %bitcast.16, s32[1,512]{1,0:T(1,128)} %bitcast.17, s32[1,512]{1,0:T(1,128)} %bitcast.18, s32[1,512]{1,0:T(1,128)} %bitcast.19, ...), custom_call_target="tpu_custom_call" | custom-call | flops 1400000000 | bytes 1048576 | tf_op jit(solution)/shard_map/pack/pallas_call | solution.py:349
  4.1 35.3 %all_to_all.10.in_ref.rest_1_ = bf16[128,2,8,128]{3,2,1,0:T(8,128)(2,1)S(1)} all-to-all(bf16[128,2,8,128]{3,2,1,0:T(8,128)(2,1)S(1)} %get-tuple-element.13), channel_id=1, replica_groups=mesh['member'=2,'space'=128] {'space'}, dimensions={0} | all-to-all | bytes 1048576 | tf_op jit(solution)/shard_map/all_to_all | solution.py:366
  39.4 0.0 slice-start
  39.4 1.8 %encode0.1 = (bf16[128,1024]{1,0:T(8,128)(2,1)S(1)}, bf16[128,1024]{1,0:T(8,128)(2,1)S(1)}) custom-call(bf16[128,2,8,128]{3,2,1,0:T(8,128)(2,1)S(1)} %all_to_all.10.in_ref.rest_1_, bf16[98,1024]{1,0:T(8,128)(2,1)S(1)} %get-tuple-element.14.w_ref), custom_call_target="tpu_custom_call" | custom-call | flops 2100000000 | bytes 1048576 | tf_op jit(solution)/shard_map/encode0/pallas_call | solution.py:373
  41.2 0.0 slice-start.1
  41.2 0.9 collective-permute-start.2
  42.1 1.9 %collective-permute-start.3 = (bf16[128,1024]{1,0:T(8,128)(2,1)S(1)}, bf16[128,1024]{1,0:T(8,128)(2,1)S(1)}, u32[]{:S(2)}, u32[]{:S(2)}) collective-permute-start(bf16[128,1024]{1,0:T(8,128)(2,1)S(1)} %get-tuple-element.15.refs_0_.lo_ref), channel_id=1, source_target_pairs={{1,0},{2,1},{3,2},{4,3},{5,4},{6,5},{7,6},{15,7},{14,15},{13,14},{... | collective-permute-start | bytes 786440 | tf_op jit(solution)/shard_map/ppermute | solution.py:382
  44.0 1.8 %encode1.1 = (bf16[128,1024]{1,0:T(8,128)(2,1)S(1)}, bf16[128,1024]{1,0:T(8,128)(2,1)S(1)}) custom-call(bf16[128,2,8,128]{3,2,1,0:T(8,128)(2,1)S(1)} %all_to_all.10.in_ref.rest_1_, bf16[98,1024]{1,0:T(8,128)(2,1)S(1)} %get-tuple-element.14.w_ref), custom_call_target="tpu_custom_call" | custom-call | flops 2100000000 | bytes 1048576 | tf_op jit(solution)/shard_map/encode1/pallas_call | solution.py:373
  45.8 0.1 collective-permute-start
  45.9 0.0 copy-start.1
  45.9 0.0 copy-start.2
  45.9 2.6 %collective-permute-start.1 = (bf16[128,1024]{1,0:T(8,128)(2,1)S(1)}, bf16[128,1024]{1,0:T(8,128)(2,1)S(1)}, u32[]{:S(2)}, u32[]{:S(2)}) collective-permute-start(bf16[128,1024]{1,0:T(8,128)(2,1)S(1)} %get-tuple-element.17.refs_2_.lo_ref), channel_id=1, source_target_pairs={{1,0},{2,1},{3,2},{4,3},{5,4},{6,5},{7,6},{15,7},{14,15},{13,14},{... | collective-permute-start | bytes 786440 | tf_op jit(solution)/shard_map/ppermute | solution.py:382
  48.5 0.0 slice-done
  48.5 0.0 slice-done.1
  48.5 5.7 %qkv.1 = (bf16[512,2048]{1,0:T(8,128)(2,1)S(1)}, bf16[1024,512]{1,0:T(8,128)(2,1)S(1)}) custom-call(bf16[128,1024]{1,0:T(8,128)(2,1)S(1)} %get-tuple-element.15.refs_0_.lo_ref, bf16[128,1024]{1,0:T(8,128)(2,1)S(1)} %get-tuple-element.16.refs_1_.hi_ref, bf16[128,1024]{1,0:T(8,128)(2,1)S(1)} %get-tuple-element.17.refs_2_.lo_ref, ...), custom_call_target="tpu_custom_call" | custom-call | flops 3500000000 | bytes 1048576 | tf_op jit(solution)/shard_map/qkv/pallas_call | solution.py:384
  54.3 0.0 collective-permute-done.2.bef_ref
  54.3 0.0 collective-permute-done.3.aft_ref
  54.3 0.0 copy-done.1
  54.3 0.0 copy-done.2
  54.3 7.1 %attend0.1.rest_0_ = bf16[256,128]{1,0:T(8,128)(2,1)S(1)} custom-call(bf16[512,2048]{1,0:T(8,128)(2,1)S(1)} %get-tuple-element.19.qk_ref, bf16[1024,512]{1,0:T(8,128)(2,1)S(1)} %get-tuple-element.20.vt_ref, bf16[128,1024]{1,0:T(8,128)(2,1)S(1)} %get-tuple-element.15.refs_0_.lo_ref, bf16[128,1024]{1,0:T(8,128)(2,1)S(1)} %get-tuple-element.16.refs_1_.hi_ref, ...), custom_call_target="tpu_custom_call" | custom-call | flops 5600000000 | bytes 1048576 | tf_op jit(solution)/shard_map/attend0/pallas_call | solution.py:399
  61.4 0.0 collective-permute-done.bef_ref
  61.5 0.0 collective-permute-done.1.aft_ref
  61.5 7.7 %attend1.1 = bf16[128,2,8,128]{3,2,1,0:T(8,128)(2,1)S(1)} custom-call(bf16[512,2048]{1,0:T(8,128)(2,1)S(1)} %get-tuple-element.19.qk_ref, bf16[1024,512]{1,0:T(8,128)(2,1)S(1)} %get-tuple-element.20.vt_ref, bf16[128,1024]{1,0:T(8,128)(2,1)S(1)} %get-tuple-element.17.refs_2_.lo_ref, bf16[128,1024]{1,0:T(8,128)(2,1)S(1)} %get-tuple-element.18.refs_3_.hi_ref, ...), custom_call_target="tpu_custom_call" | custom-call | flops 5600000000 | bytes 1048576 | tf_op jit(solution)/shard_map/attend1/pallas_call | solution.py:399
  69.1 0.0 copy-start
  69.1 22.3 %all_to_all.11.back_ref = bf16[128,2,8,128]{3,2,1,0:T(8,128)(2,1)S(1)} all-to-all(bf16[128,2,8,128]{3,2,1,0:T(8,128)(2,1)S(1)} %attend1.1), channel_id=1, replica_groups=mesh['member'=2,'space'=128] {'space'}, dimensions={0} | all-to-all | bytes 1048576 | tf_op jit(solution)/shard_map/all_to_all | solution.py:419
  91.4 0.6 predict.1.mine_ref
  92.0 5.1 %collective-permute-start.4 = (bf16[2,98,512]{2,1,0:T(8,128)(2,1)S(1)}, bf16[2,98,512]{2,1,0:T(8,128)(2,1)S(1)}, u32[]{:S(2)}, u32[]{:S(2)}) collective-permute-start(bf16[2,98,512]{2,1,0:T(8,128)(2,1)S(1)} %predict.1.mine_ref), channel_id=1, source_target_pairs={{0,128},{128,0},{1,129},{129,1},{2,130},{130,2},{3,131},{131,3},{4... | collective-permute-start | bytes 602120 | tf_op jit(solution)/shard_map/ppermute | solution.py:426
  97.1 0.8 copy.12
  98.0 0.3 collective-permute-done.4.other_ref
  98.2 0.0 copy-done
  98.2 0.9 score.1
  (1 shorter events, 0.0 us)
Async XLA Ops:
  39.4 9.2 %slice-start = ((s8[6291456]{0:T(1024)(128)(4,1)}), s8[4194304]{0:T(1024)(128)(4,1)S(1)}, s32[]{:S(2)}) async-start(s8[6291456]{0:T(1024)(128)(4,1)} %bitcast.11), calls=%async_computation.2 | async-start | bytes 8388608
  41.2 7.3 %slice-start.1 = ((s8[6291456]{0:T(1024)(128)(4,1)}), s8[2097152]{0:T(1024)(128)(4,1)S(1)}, s32[]{:S(2)}) async-start(s8[6291456]{0:T(1024)(128)(4,1)} %bitcast.11), calls=%async_computation.3 | async-start | bytes 4194304
  41.2 13.1 %collective-permute-start.2 = (bf16[128,1024]{1,0:T(8,128)(2,1)S(1)}, bf16[128,1024]{1,0:T(8,128)(2,1)S(1)}, u32[]{:S(2)}, u32[]{:S(2)}) collective-permute-start(bf16[128,1024]{1,0:T(8,128)(2,1)S(1)} %get-tuple-element.16.refs_1_.hi_ref), channel_id=1, source_target_pairs={{0,1},{1,2},{2,3},{3,4},{4,5},{5,6},{6,7},{7,15},{15,14},{14,13},{... | collective-permute-start | bytes 786440 | tf_op jit(solution)/shard_map/ppermute | solution.py:382
  42.1 12.2 %collective-permute-start.3 = (bf16[128,1024]{1,0:T(8,128)(2,1)S(1)}, bf16[128,1024]{1,0:T(8,128)(2,1)S(1)}, u32[]{:S(2)}, u32[]{:S(2)}) collective-permute-start(bf16[128,1024]{1,0:T(8,128)(2,1)S(1)} %get-tuple-element.15.refs_0_.lo_ref), channel_id=1, source_target_pairs={{1,0},{2,1},{3,2},{4,3},{5,4},{6,5},{7,6},{15,7},{14,15},{13,14},{... | collective-permute-start | bytes 786440 | tf_op jit(solution)/shard_map/ppermute | solution.py:382
  45.8 15.7 %collective-permute-start = (bf16[128,1024]{1,0:T(8,128)(2,1)S(1)}, bf16[128,1024]{1,0:T(8,128)(2,1)S(1)}, u32[]{:S(2)}, u32[]{:S(2)}) collective-permute-start(bf16[128,1024]{1,0:T(8,128)(2,1)S(1)} %get-tuple-element.18.refs_3_.hi_ref), channel_id=1, source_target_pairs={{0,1},{1,2},{2,3},{3,4},{4,5},{5,6},{6,7},{7,15},{15,14},{14,13},{... | collective-permute-start | bytes 786440 | tf_op jit(solution)/shard_map/ppermute | solution.py:382
  45.9 8.4 %copy-start.1 = (bf16[1024,1024]{1,0:T(8,128)(2,1)S(1)}, bf16[1024,1024]{1,0:T(8,128)(2,1)}, u32[]{:S(2)}) copy-start(bf16[1024,1024]{1,0:T(8,128)(2,1)} %w_out_ref.3) | copy-start | bytes 6291460
  45.9 8.4 %copy-start.2 = (bf16[1024,98]{0,1:T(8,128)(2,1)S(1)}, bf16[1024,98]{0,1:T(8,128)(2,1)}, u32[]{:S(2)}) copy-start(bf16[1024,98]{0,1:T(8,128)(2,1)} %param.19) | copy-start | bytes 602116
  45.9 15.6 %collective-permute-start.1 = (bf16[128,1024]{1,0:T(8,128)(2,1)S(1)}, bf16[128,1024]{1,0:T(8,128)(2,1)S(1)}, u32[]{:S(2)}, u32[]{:S(2)}) collective-permute-start(bf16[128,1024]{1,0:T(8,128)(2,1)S(1)} %get-tuple-element.17.refs_2_.lo_ref), channel_id=1, source_target_pairs={{1,0},{2,1},{3,2},{4,3},{5,4},{6,5},{7,6},{15,7},{14,15},{13,14},{... | collective-permute-start | bytes 786440 | tf_op jit(solution)/shard_map/ppermute | solution.py:382
  69.1 29.1 %copy-start = (f32[512,98]{0,1:T(8,128)S(1)}, f32[512,98]{0,1:T(8,128)}, u32[]{:S(2)}) copy-start(f32[512,98]{0,1:T(8,128)} %param.11) | copy-start | bytes 602116
  92.0 6.2 %collective-permute-start.4 = (bf16[2,98,512]{2,1,0:T(8,128)(2,1)S(1)}, bf16[2,98,512]{2,1,0:T(8,128)(2,1)S(1)}, u32[]{:S(2)}, u32[]{:S(2)}) collective-permute-start(bf16[2,98,512]{2,1,0:T(8,128)(2,1)S(1)} %predict.1.mine_ref), channel_id=1, source_target_pairs={{0,128},{128,0},{1,129},{129,1},{2,130},{130,2},{3,131},{131,3},{4... | collective-permute-start | bytes 602120 | tf_op jit(solution)/shard_map/ppermute | solution.py:426

commit v4 on v3

--- a/solution.py
+++ b/solution.py
@@ -156,20 +156,15 @@
     half = rows_ref.shape[0] // halves
     for i, ref in enumerate(hidden_refs):
         rows_ref[i * half : (i + 1) * half, :] = ref[...]
-    chunk = 256
 
     def project(cols):
         return jnp.dot(rows_ref[...], w_ref[:, cols], preferred_element_type=F32).astype(BF16)
 
-    @pl.loop(0, 2 * width // chunk)
-    def _(c):
-        cols = pl.ds(pl.multiple_of(c * chunk, chunk), chunk)
-        qk_ref[:, cols] = project(cols)
-
-    @pl.loop(0, width // chunk)
-    def _(c):
-        rows = pl.ds(pl.multiple_of(c * chunk, chunk), chunk)
-        vt_ref[rows, :] = project(pl.ds(pl.multiple_of(2 * width + c * chunk, chunk), chunk)).T
+    chunk = 512
+    for c in range(0, 2 * width, chunk):
+        qk_ref[:, c : c + chunk] = project(slice(c, c + chunk))
+    for c in range(0, width, chunk):
+        vt_ref[c : c + chunk, :] = project(slice(2 * width + c, 2 * width + c + chunk)).T
 
 
 def attend_kernel(
@@ -189,16 +184,12 @@
     proc_ref[half:, :] = aft_ref[...]
     chunk = 256
 
-    def project(c, carry):
-        cols = pl.ds(pl.multiple_of(c * chunk, chunk), chunk)
-        k_src = pl.ds(pl.multiple_of(width + c * chunk, chunk), chunk)
-        v_src = pl.ds(pl.multiple_of(2 * width + c * chunk, chunk), chunk)
-        kh_ref[:, cols] = jnp.dot(proc_ref[...], w_kv_ref[:, k_src], preferred_element_type=F32).astype(BF16)
-        vh = jnp.dot(proc_ref[...], w_kv_ref[:, v_src], preferred_element_type=F32).astype(BF16)
-        vth_ref[cols, :] = vh.T
-        return carry
-
-    lax.fori_loop(0, width // chunk, project, 0)
+    for c in range(0, width, chunk):
+        k_src, v_src = slice(width + c, width + c + chunk), slice(2 * width + c, 2 * width + c + chunk)
+        kh = jnp.dot(proc_ref[...], w_kv_ref[:, k_src], preferred_element_type=F32)
+        kh_ref[:, c : c + chunk] = kh.astype(BF16)
+        vh = jnp.dot(proc_ref[...], w_kv_ref[:, v_src], preferred_element_type=F32)
+        vth_ref[c : c + chunk, :] = vh.astype(BF16).T
 
     key_id = iota((half, 2 * half), 0)
     query_id = iota((half, 2 * half), 1)
@@ -214,8 +205,8 @@
     base = m * nodes
 
     def scores(p, s_ref):
-        cols = pl.ds(pl.multiple_of(p * LANES, LANES), LANES)
-        k_cols = pl.ds(pl.multiple_of(width + p * LANES, LANES), LANES)
+        cols = slice(p * LANES, (p + 1) * LANES)
+        k_cols = slice(width + p * LANES, width + (p + 1) * LANES)
         k_own = qk_ref[base : base + nodes, k_cols]
         for side in range(2):
             row0 = side * half
@@ -234,7 +225,7 @@
                 s_ref[side, nodes:] = s_halo + right_ref[1]
 
     def finish(p, s_ref):
-        cols = pl.ds(pl.multiple_of(p * LANES, LANES), LANES)
+        cols = slice(p * LANES, (p + 1) * LANES)
         blocks = (slice(0, half), slice(half, nodes), slice(nodes, nodes + half))
         for side in range(2):
             row0 = side * half
@@ -256,24 +247,17 @@
     pairs = HEADS // 2
     scores(0, sa_ref)
 
-    def heads(i, carry):
-        p = 2 * i
-        scores(p + 1, sb_ref)
-        finish(p, sa_ref)
-        scores(jnp.minimum(p + 2, pairs - 1), sa_ref)
-        finish(p + 1, sb_ref)
-        return carry
-
-    lax.fori_loop(0, pairs // 2, heads, 0)
-
-    def mix(c, carry):
-        cols = pl.ds(pl.multiple_of(c * chunk, chunk), chunk)
+    for p in range(pairs):
+        here, there = (sa_ref, sb_ref) if p % 2 == 0 else (sb_ref, sa_ref)
+        if p + 1 < pairs:
+            scores(p + 1, there)
+        finish(p, here)
+
+    for c in range(0, width, chunk):
+        cols = slice(c, c + chunk)
         mixed = jnp.dot(att_ref[...], w_out_ref[:, cols], preferred_element_type=F32)
         proc_ref[0:half, cols] = (lo_ref[:, cols].astype(F32) + mixed[0:half]).astype(BF16)
         proc_ref[half:, cols] = (hi_ref[:, cols].astype(F32) + mixed[half:]).astype(BF16)
-        return carry
-
-    lax.fori_loop(0, width // chunk, mix, 0)
     decoded = nt_dot(proc_ref[...], w_dec_ref[...]).astype(BF16)
     if m == 0:
         out_ref[...] = jnp.zeros_like(out_ref)

time: 99.4 us -> 92 us (0.926)
  Pallas kernels: 29.1 us -> 21.5 us
    pallas_call x2, Pallas kernels: 14.8 us -> 9.42 us  [on_device(): pl.pallas_call(functools.partial(attend_kernel, var_count, m, at[0], at[-...]
    pallas_call x1, Pallas kernels: 5.72 us -> 3.52 us  [on_device(): pl.pallas_call(functools.partial(qkv_kernel, len(hidden)), out_shape=(jax...]
  transfers between devices with their start and end apart: 5 -> 5, of which waited for: 1 -> 1; matrix products, arithmetic and copies ran while one was open for 1% -> 1% of each run, Pallas kernels for 15% -> 11%
where the time goes in v4:
time: 92 us; the launch traced here: 91.8 us
  blocking collectives  57.8 us (63%)
  Pallas kernels  21.5 us (23%)
  starting transfers between devices  10.6 us (12%)
    all_to_all x1, blocking collectives, on_device(): arrived = lax.all_to_all(outgoing, 'space', 0, 0, tiled=True)  35.3 us
    all_to_all x1, blocking collectives, on_device(): returned = lax.all_to_all(replies, 'space', 0, 0, tiled=True)  22.5 us
    pallas_call x2, Pallas kernels, on_device(): pl.pallas_call(functools.partial(attend_kernel, var_count, m, at[0], at[-...  9.42 us
    ppermute x1, starting transfers between devices, on_device(): other = lax.ppermute(predicted, 'member', [(0, 1), (1, 0)])  5.08 us
    ppermute x2, starting transfers between devices, on_device(): lax.ppermute(lo, 'space', down)  4.51 us
    pallas_call x2, Pallas kernels, on_device(): pl.pallas_call(functools.partial(encode_kernel, var_count, m), out_shape=...  3.61 us
    pallas_call x1, Pallas kernels, on_device(): pl.pallas_call(functools.partial(qkv_kernel, len(hidden)), out_shape=(jax...  3.52 us
    pallas_call x1, Pallas kernels, on_device(): pl.pallas_call(functools.partial(pack_kernel, var_count), in_specs=[HBM_S...  3.46 us
  transfers between devices with their start and end apart: 5, of which 1 were waited for; matrix products, arithmetic and copies ran while one was open for 1% of the time, Pallas kernels for 11%

profile of v4, /device:TPU:1, one launch (start us, length us, event | category | flops | bytes accessed | tf_op | source)
XLA Modules:
  0.0 91.8 jit_solution(6085418681999010190)
XLA Ops:
  0.6 3.5 %pack.1 = (bf16[128,2,8,128]{3,2,1,0:T(8,128)(2,1)S(1)}, s32[1,512]{1,0:T(1,128)S(1)}, bf16[98,1024]{1,0:T(8,128)(2,1)S(1)}, bf16[2,98,512]{2,1,0:T(8,128)(2,1)S(1)}) custom-call(bf16[98,2,512]{2,1,0:T(2,128)(2,1)} %bitcast.16, s32[1,512]{1,0:T(1,128)} %bitcast.17, s32[1,512]{1,0:T(1,128)} %bitcast.18, s32[1,512]{1,0:T(1,128)} %bitcast.19, ...), custom_call_target="tpu_custom_call" | custom-call | flops 1400000000 | bytes 1048576 | tf_op jit(solution)/shard_map/pack/pallas_call | solution.py:333
  4.1 35.3 %all_to_all.10.in_ref.rest_1_ = bf16[128,2,8,128]{3,2,1,0:T(8,128)(2,1)S(1)} all-to-all(bf16[128,2,8,128]{3,2,1,0:T(8,128)(2,1)S(1)} %get-tuple-element.13), channel_id=1, replica_groups=mesh['member'=2,'space'=128] {'space'}, dimensions={0} | all-to-all | bytes 1048576 | tf_op jit(solution)/shard_map/all_to_all | solution.py:350
  39.4 0.0 slice-start
  39.4 1.8 %encode0.1 = (bf16[128,1024]{1,0:T(8,128)(2,1)S(1)}, bf16[128,1024]{1,0:T(8,128)(2,1)S(1)}) custom-call(bf16[128,2,8,128]{3,2,1,0:T(8,128)(2,1)S(1)} %all_to_all.10.in_ref.rest_1_, bf16[98,1024]{1,0:T(8,128)(2,1)S(1)} %get-tuple-element.14.w_ref), custom_call_target="tpu_custom_call" | custom-call | flops 2100000000 | bytes 1048576 | tf_op jit(solution)/shard_map/encode0/pallas_call | solution.py:357
  41.2 0.0 slice-start.1
  41.2 0.9 collective-permute-start.2
  42.1 1.9 %collective-permute-start.3 = (bf16[128,1024]{1,0:T(8,128)(2,1)S(1)}, bf16[128,1024]{1,0:T(8,128)(2,1)S(1)}, u32[]{:S(2)}, u32[]{:S(2)}) collective-permute-start(bf16[128,1024]{1,0:T(8,128)(2,1)S(1)} %get-tuple-element.15.refs_0_.lo_ref), channel_id=1, source_target_pairs={{1,0},{2,1},{3,2},{4,3},{5,4},{6,5},{7,6},{15,7},{14,15},{13,14},{... | collective-permute-start | bytes 786440 | tf_op jit(solution)/shard_map/ppermute | solution.py:366
  44.0 1.8 %encode1.1 = (bf16[128,1024]{1,0:T(8,128)(2,1)S(1)}, bf16[128,1024]{1,0:T(8,128)(2,1)S(1)}) custom-call(bf16[128,2,8,128]{3,2,1,0:T(8,128)(2,1)S(1)} %all_to_all.10.in_ref.rest_1_, bf16[98,1024]{1,0:T(8,128)(2,1)S(1)} %get-tuple-element.14.w_ref), custom_call_target="tpu_custom_call" | custom-call | flops 2100000000 | bytes 1048576 | tf_op jit(solution)/shard_map/encode1/pallas_call | solution.py:357
  45.8 0.1 collective-permute-start
  45.9 0.0 copy-start.1
  45.9 0.0 copy-start.2
  45.9 2.6 %collective-permute-start.1 = (bf16[128,1024]{1,0:T(8,128)(2,1)S(1)}, bf16[128,1024]{1,0:T(8,128)(2,1)S(1)}, u32[]{:S(2)}, u32[]{:S(2)}) collective-permute-start(bf16[128,1024]{1,0:T(8,128)(2,1)S(1)} %get-tuple-element.17.refs_2_.lo_ref), channel_id=1, source_target_pairs={{1,0},{2,1},{3,2},{4,3},{5,4},{6,5},{7,6},{15,7},{14,15},{13,14},{... | collective-permute-start | bytes 786440 | tf_op jit(solution)/shard_map/ppermute | solution.py:366
  48.5 0.0 slice-done
  48.5 0.0 slice-done.1
  48.5 3.5 %qkv.1 = (bf16[512,2048]{1,0:T(8,128)(2,1)S(1)}, bf16[1024,512]{1,0:T(8,128)(2,1)S(1)}) custom-call(bf16[128,1024]{1,0:T(8,128)(2,1)S(1)} %get-tuple-element.15.refs_0_.lo_ref, bf16[128,1024]{1,0:T(8,128)(2,1)S(1)} %get-tuple-element.16.refs_1_.hi_ref, bf16[128,1024]{1,0:T(8,128)(2,1)S(1)} %get-tuple-element.17.refs_2_.lo_ref, ...), custom_call_target="tpu_custom_call" | custom-call | flops 3500000000 | bytes 1048576 | tf_op jit(solution)/shard_map/qkv/pallas_call | solution.py:368
  52.1 0.0 collective-permute-done.2.bef_ref
  52.1 0.0 collective-permute-done.3.aft_ref
  52.1 0.0 copy-done.1
  52.1 0.0 copy-done.2
  52.1 4.3 %attend0.1.rest_0_ = bf16[256,128]{1,0:T(8,128)(2,1)S(1)} custom-call(bf16[512,2048]{1,0:T(8,128)(2,1)S(1)} %get-tuple-element.19.qk_ref, bf16[1024,512]{1,0:T(8,128)(2,1)S(1)} %get-tuple-element.20.vt_ref, bf16[128,1024]{1,0:T(8,128)(2,1)S(1)} %get-tuple-element.15.refs_0_.lo_ref, bf16[128,1024]{1,0:T(8,128)(2,1)S(1)} %get-tuple-element.16.refs_1_.hi_ref, ...), custom_call_target="tpu_custom_call" | custom-call | flops 5600000000 | bytes 1048576 | tf_op jit(solution)/shard_map/attend0/pallas_call | solution.py:383
  56.4 0.0 collective-permute-done.bef_ref
  56.4 0.0 collective-permute-done.1.aft_ref
  56.5 5.1 %attend1.1 = bf16[128,2,8,128]{3,2,1,0:T(8,128)(2,1)S(1)} custom-call(bf16[512,2048]{1,0:T(8,128)(2,1)S(1)} %get-tuple-element.19.qk_ref, bf16[1024,512]{1,0:T(8,128)(2,1)S(1)} %get-tuple-element.20.vt_ref, bf16[128,1024]{1,0:T(8,128)(2,1)S(1)} %get-tuple-element.17.refs_2_.lo_ref, bf16[128,1024]{1,0:T(8,128)(2,1)S(1)} %get-tuple-element.18.refs_3_.hi_ref, ...), custom_call_target="tpu_custom_call" | custom-call | flops 5600000000 | bytes 1048576 | tf_op jit(solution)/shard_map/attend1/pallas_call | solution.py:383
  61.6 0.0 copy-start
  61.6 22.5 %all_to_all.11.back_ref = bf16[128,2,8,128]{3,2,1,0:T(8,128)(2,1)S(1)} all-to-all(bf16[128,2,8,128]{3,2,1,0:T(8,128)(2,1)S(1)} %attend1.1), channel_id=1, replica_groups=mesh['member'=2,'space'=128] {'space'}, dimensions={0} | all-to-all | bytes 1048576 | tf_op jit(solution)/shard_map/all_to_all | solution.py:403
  84.1 0.6 predict.1.mine_ref
  84.7 5.1 %collective-permute-start.4 = (bf16[2,98,512]{2,1,0:T(8,128)(2,1)S(1)}, bf16[2,98,512]{2,1,0:T(8,128)(2,1)S(1)}, u32[]{:S(2)}, u32[]{:S(2)}) collective-permute-start(bf16[2,98,512]{2,1,0:T(8,128)(2,1)S(1)} %predict.1.mine_ref), channel_id=1, source_target_pairs={{0,128},{128,0},{1,129},{129,1},{2,130},{130,2},{3,131},{131,3},{4... | collective-permute-start | bytes 602120 | tf_op jit(solution)/shard_map/ppermute | solution.py:410
  89.8 0.8 copy.12
  90.6 0.3 collective-permute-done.4.other_ref
  90.9 0.0 copy-done
  90.9 0.9 %score.1 = f32[98,512]{1,0:T(8,128)} custom-call(bf16[2,98,512]{2,1,0:T(8,128)(2,1)S(1)} %predict.1.mine_ref, bf16[2,98,512]{2,1,0:T(8,128)(2,1)S(1)} %collective-permute-done.4.other_ref, f32[98,512]{1,0:T(8,128)S(1)} %bitcast.10), custom_call_target="tpu_custom_call" | custom-call | tf_op jit(solution)/shard_map/score/pallas_call | solution.py:411
  (1 shorter events, 0.0 us)
Async XLA Ops:
  39.4 9.2 %slice-start = ((s8[6291456]{0:T(1024)(128)(4,1)}), s8[4194304]{0:T(1024)(128)(4,1)S(1)}, s32[]{:S(2)}) async-start(s8[6291456]{0:T(1024)(128)(4,1)} %bitcast.11), calls=%async_computation.2 | async-start | bytes 8388608
  41.2 7.3 %slice-start.1 = ((s8[6291456]{0:T(1024)(128)(4,1)}), s8[2097152]{0:T(1024)(128)(4,1)S(1)}, s32[]{:S(2)}) async-start(s8[6291456]{0:T(1024)(128)(4,1)} %bitcast.11), calls=%async_computation.3 | async-start | bytes 4194304
  41.2 10.9 %collective-permute-start.2 = (bf16[128,1024]{1,0:T(8,128)(2,1)S(1)}, bf16[128,1024]{1,0:T(8,128)(2,1)S(1)}, u32[]{:S(2)}, u32[]{:S(2)}) collective-permute-start(bf16[128,1024]{1,0:T(8,128)(2,1)S(1)} %get-tuple-element.16.refs_1_.hi_ref), channel_id=1, source_target_pairs={{0,1},{1,2},{2,3},{3,4},{4,5},{5,6},{6,7},{7,15},{15,14},{14,13},{... | collective-permute-start | bytes 786440 | tf_op jit(solution)/shard_map/ppermute | solution.py:366
  42.1 10.0 %collective-permute-start.3 = (bf16[128,1024]{1,0:T(8,128)(2,1)S(1)}, bf16[128,1024]{1,0:T(8,128)(2,1)S(1)}, u32[]{:S(2)}, u32[]{:S(2)}) collective-permute-start(bf16[128,1024]{1,0:T(8,128)(2,1)S(1)} %get-tuple-element.15.refs_0_.lo_ref), channel_id=1, source_target_pairs={{1,0},{2,1},{3,2},{4,3},{5,4},{6,5},{7,6},{15,7},{14,15},{13,14},{... | collective-permute-start | bytes 786440 | tf_op jit(solution)/shard_map/ppermute | solution.py:366
  45.8 10.7 %collective-permute-start = (bf16[128,1024]{1,0:T(8,128)(2,1)S(1)}, bf16[128,1024]{1,0:T(8,128)(2,1)S(1)}, u32[]{:S(2)}, u32[]{:S(2)}) collective-permute-start(bf16[128,1024]{1,0:T(8,128)(2,1)S(1)} %get-tuple-element.18.refs_3_.hi_ref), channel_id=1, source_target_pairs={{0,1},{1,2},{2,3},{3,4},{4,5},{5,6},{6,7},{7,15},{15,14},{14,13},{... | collective-permute-start | bytes 786440 | tf_op jit(solution)/shard_map/ppermute | solution.py:366
  45.9 6.2 %copy-start.1 = (bf16[1024,1024]{1,0:T(8,128)(2,1)S(1)}, bf16[1024,1024]{1,0:T(8,128)(2,1)}, u32[]{:S(2)}) copy-start(bf16[1024,1024]{1,0:T(8,128)(2,1)} %w_out_ref.3) | copy-start | bytes 6291460
  45.9 6.2 %copy-start.2 = (bf16[1024,98]{0,1:T(8,128)(2,1)S(1)}, bf16[1024,98]{0,1:T(8,128)(2,1)}, u32[]{:S(2)}) copy-start(bf16[1024,98]{0,1:T(8,128)(2,1)} %param.19) | copy-start | bytes 602116
  45.9 10.6 %collective-permute-start.1 = (bf16[128,1024]{1,0:T(8,128)(2,1)S(1)}, bf16[128,1024]{1,0:T(8,128)(2,1)S(1)}, u32[]{:S(2)}, u32[]{:S(2)}) collective-permute-start(bf16[128,1024]{1,0:T(8,128)(2,1)S(1)} %get-tuple-element.17.refs_2_.lo_ref), channel_id=1, source_target_pairs={{1,0},{2,1},{3,2},{4,3},{5,4},{6,5},{7,6},{15,7},{14,15},{13,14},{... | collective-permute-start | bytes 786440 | tf_op jit(solution)/shard_map/ppermute | solution.py:366
  61.6 29.3 %copy-start = (f32[512,98]{0,1:T(8,128)S(1)}, f32[512,98]{0,1:T(8,128)}, u32[]{:S(2)}) copy-start(f32[512,98]{0,1:T(8,128)} %param.11) | copy-start | bytes 602116
  84.7 6.2 %collective-permute-start.4 = (bf16[2,98,512]{2,1,0:T(8,128)(2,1)S(1)}, bf16[2,98,512]{2,1,0:T(8,128)(2,1)S(1)}, u32[]{:S(2)}, u32[]{:S(2)}) collective-permute-start(bf16[2,98,512]{2,1,0:T(8,128)(2,1)S(1)} %predict.1.mine_ref), channel_id=1, source_target_pairs={{0,128},{128,0},{1,129},{129,1},{2,130},{130,2},{3,131},{131,3},{4... | collective-permute-start | bytes 602120 | tf_op jit(solution)/shard_map/ppermute | solution.py:410

commit v5 on v4

--- a/solution.py
+++ b/solution.py
@@ -11,6 +11,8 @@
 HALF_WIN = 128
 NODE_DEV = 256
 CAP = 8
+CAP_BITS = 3
+META = 104
 LANES = 128
 GRID = (4, 4, 8)
 Y_BITS, Z_BITS = 2, 3
@@ -60,19 +62,27 @@
     return path_place(owner_row) * CAP + rank
 
 
+def one_hot(count, row):
+    ids = iota((count, row.shape[1]), 0).astype(jnp.int16)
+    return jnp.where(ids == row.astype(jnp.int16), jnp.ones((), BF16), jnp.zeros((), BF16))
+
+
 def pack_kernel(
     var_count, x_hbm, eo_hbm, el_hbm, do_hbm, dl_hbm, w_hbm, out_ref, slot_ref, w_ref, states_ref,
-    x_ref, eo_ref, el_ref, do_ref, dl_ref, aug_ref, sems,
+    x_ref, eo_ref, el_ref, do_ref, dl_ref, sems,
 ):
     members, _, pts = states_ref.shape
     n_dest = out_ref.shape[0]
     slots = n_dest * CAP
-    copies = [
-        pltpu.make_async_copy(src, dst, sems.at[i])
-        for i, (src, dst) in enumerate(
-            [(eo_hbm, eo_ref), (do_hbm, do_ref), (el_hbm, el_ref), (dl_hbm, dl_ref), (x_hbm, x_ref), (w_hbm, w_ref)]
-        )
+    pairs = [
+        (eo_hbm, eo_ref),
+        (do_hbm, do_ref),
+        (el_hbm, el_ref),
+        (dl_hbm, dl_ref),
+        (x_hbm, x_ref),
+        (w_hbm, w_ref),
     ]
+    copies = [pltpu.make_async_copy(src, dst, sems.at[i]) for i, (src, dst) in enumerate(pairs)]
     for copy in copies:
         copy.start()
     copies[0].wait()
@@ -80,33 +90,29 @@
     copies[1].wait()
     dec_slot = slot_row(do_ref[...])
     slot_ref[...] = dec_slot
-    slot_id = iota((slots, pts), 0)
-    place = (slot_id == enc_slot).astype(F32).astype(BF16)
-    request = (slot_id == dec_slot).astype(F32).astype(BF16)
-    row_id = iota((LANES, pts), 0)
     copies[2].wait()
     copies[3].wait()
-    enc_meta = jnp.where(row_id == var_count, el_ref[...] + 1, 0).astype(F32)
-    dec_meta = jnp.where(row_id == var_count, dl_ref[...] + 1, 0).astype(F32)
-    asked = nt_dot(request, dec_meta.astype(BF16))
-    packed = []
     copies[4].wait()
-    for m in range(members):
-        aug_ref[...] = enc_meta if m == 0 else jnp.zeros_like(enc_meta)
-        field = x_ref[:, m, :]
-        aug_ref[0:var_count, :] = field.astype(F32)
-        states_ref[m] = field
-        rows = nt_dot(place, aug_ref[...].astype(BF16))
-        if m == 1:
-            rows = rows + asked
-        packed.append(rows.reshape(n_dest, 1, CAP, LANES))
-    out_ref[...] = jnp.concatenate(packed, axis=1).astype(BF16)
+    rows_in = members * var_count
+    lanes = members * LANES
+    row_id, col_id = iota((lanes, rows_in), 0), iota((lanes, rows_in), 1)
+    var, m = row_id & (LANES - 1), row_id >> 7
+    apart = ((var * members + m == col_id) & (var < var_count)).astype(F32).astype(BF16)
+    fields = jnp.dot(apart, x_ref[...].reshape(rows_in, pts), preferred_element_type=F32)
+    for i in range(members):
+        states_ref[i] = fields[i * LANES : i * LANES + var_count].astype(BF16)
+    line_id = iota((lanes, pts), 0)
+    fields += jnp.where(line_id == var_count, el_ref[...] + 1, 0).astype(F32)
+    rows = nt_dot(one_hot(slots, enc_slot), fields.astype(BF16)).reshape(n_dest, CAP, lanes)
+    rank = (dec_slot & (CAP - 1)) + META
+    requests = jnp.where(iota((LANES, pts), 0) == rank, dl_ref[...] + 1, 0).astype(F32)
+    asked = nt_dot(one_hot(n_dest, dec_slot >> CAP_BITS), requests.astype(BF16))
+    top = iota((n_dest, CAP, LANES), 1) == 0
+    asked = jnp.where(top, jnp.broadcast_to(asked[:, None, :], (n_dest, CAP, LANES)), 0.0)
+    out_ref[:, :, 0:LANES] = rows[:, :, 0:LANES].astype(BF16)
+    out_ref[:, :, LANES:] = (rows[:, :, LANES:] + asked).astype(BF16)
     copies[5].wait()
-
-
-def member_rows(ref, m):
-    n_dest = ref.shape[0]
-    return ref[:, m].astype(F32).reshape(n_dest * CAP, LANES).astype(BF16)
+    w_ref[...] = w_ref[...] * jnp.asarray(0.5, BF16)
 
 
 def encode_kernel(var_count, m, in_ref, w_ref, lo_ref, hi_ref, pooled_ref, ea_ref, eb_ref):
@@ -115,18 +121,17 @@
     width = w_ref.shape[1]
     nodes = NODE_DEV
     chunk = 256
+    arrived = in_ref[...].reshape(slots, in_ref.shape[2])
     lane_id = iota((8, LANES), 1)
     pick = (lane_id == var_count).astype(F32).astype(BF16)
-    node_row = nt_dot(pick, member_rows(in_ref, 0))[0:1, :]
-    node_id = (iota((nodes, slots), 0) + 1).astype(F32)
-    assign_f = (node_id == node_row).astype(F32)
-    share = 1.0 / jnp.maximum(jnp.sum(assign_f, axis=1, keepdims=True), 1.0)
-    assign = assign_f.astype(BF16)
-    x = member_rows(in_ref, m)[:, 0:var_count]
+    node_row = nt_dot(pick, arrived[:, 0:LANES])[0:1, :]
+    assign = one_hot(nodes, node_row.astype(jnp.int32) - 1)
+    share = 1.0 / jnp.maximum(jnp.sum(assign.astype(F32), axis=1, keepdims=True), 1.0)
+    x = arrived[:, m * LANES : m * LANES + var_count]
 
     def embed(c, e_ref):
         cols = pl.ds(pl.multiple_of(c * chunk, chunk), chunk)
-        raw = 0.5 * jnp.dot(x, w_ref[:, cols], preferred_element_type=F32)
+        raw = jnp.dot(x, w_ref[:, cols], preferred_element_type=F32)
         e_ref[...] = (raw + raw * jnp.tanh(raw)).astype(BF16)
 
     def pool(c, e_ref):
@@ -172,23 +177,23 @@
     w_dec_ref, *rest,
 ):
     if m == 0:
-        out_ref, kh_ref, vth_ref, att_ref, proc_ref, left_ref, right_ref, sa_ref, sb_ref, e_ref = rest
+        out_ref, kh_ref, vth_ref, att_ref, proc_ref, left_ref, right_ref, sa_ref, sb_ref, e_ref, halo_ref = rest
     else:
-        dec_ref, in_ref, out_ref, kh_ref, vth_ref, att_ref, proc_ref, left_ref, right_ref, sa_ref, sb_ref, e_ref = rest
+        dec_ref, in_ref, out_ref, kh_ref, vth_ref, att_ref, proc_ref, left_ref, right_ref, sa_ref, sb_ref, e_ref, halo_ref, reply_ref = rest
     half, width = lo_ref.shape
     me = lax.axis_index("space")
     at_first, at_last = (me == first_at).astype(jnp.int32), (me == last_at).astype(jnp.int32)
     nodes = 2 * half
     head_dim = width // HEADS
-    proc_ref[0:half, :] = bef_ref[...]
-    proc_ref[half:, :] = aft_ref[...]
+    halo_ref[0:half, :] = bef_ref[...]
+    halo_ref[half:, :] = aft_ref[...]
     chunk = 256
 
-    for c in range(0, width, chunk):
+    def project(c):
         k_src, v_src = slice(width + c, width + c + chunk), slice(2 * width + c, 2 * width + c + chunk)
-        kh = jnp.dot(proc_ref[...], w_kv_ref[:, k_src], preferred_element_type=F32)
+        kh = jnp.dot(halo_ref[...], w_kv_ref[:, k_src], preferred_element_type=F32)
         kh_ref[:, c : c + chunk] = kh.astype(BF16)
-        vh = jnp.dot(proc_ref[...], w_kv_ref[:, v_src], preferred_element_type=F32)
+        vh = jnp.dot(halo_ref[...], w_kv_ref[:, v_src], preferred_element_type=F32)
         vth_ref[c : c + chunk, :] = vh.astype(BF16).T
 
     key_id = iota((half, 2 * half), 0)
@@ -244,11 +249,25 @@
             pair = jnp.concatenate([out[0:head_dim, 0:half], out[head_dim:, half:]], axis=0)
             att_ref[row0 : row0 + half, cols] = pair.T.astype(BF16)
 
+    if m == 1:
+        n_dest = in_ref.shape[0]
+        slots = n_dest * CAP
+        cube = (n_dest, CAP, LANES)
+        asked = in_ref[:, :, LANES:].astype(F32)
+        asked = jnp.broadcast_to(asked[:, 0:1, :], cube)
+        asked = jnp.where(iota(cube, 2) == iota(cube, 1) + META, asked, 0.0)
+        asked = jnp.sum(asked, axis=2, keepdims=True).reshape(slots, 1)
+        node_lane = (iota((slots, nodes), 1) + 1).astype(F32)
+        reply_ref[...] = (node_lane == asked).astype(F32).astype(BF16)
+
     pairs = HEADS // 2
+    per_chunk = chunk // LANES
+    project(0)
     scores(0, sa_ref)
-
     for p in range(pairs):
         here, there = (sa_ref, sb_ref) if p % 2 == 0 else (sb_ref, sa_ref)
+        if p % per_chunk == 0 and p + per_chunk < pairs:
+            project((p // per_chunk + 1) * chunk)
         if p + 1 < pairs:
             scores(p + 1, there)
         finish(p, here)
@@ -263,29 +282,22 @@
         out_ref[...] = jnp.zeros_like(out_ref)
         out_ref[:, 0:var_count] = decoded
     else:
-        n_dest = in_ref.shape[0]
-        slots = n_dest * CAP
         mine_ref = att_ref.at[:, 0:LANES]
         mine_ref[...] = jnp.zeros_like(mine_ref)
         mine_ref[:, 0:var_count] = decoded
         both = jnp.concatenate([dec_ref[...], mine_ref[...]], axis=1)
-        node_lane = (iota((slots, nodes), 1) + 1).astype(F32)
-        asked = in_ref[:, 1].astype(F32).reshape(slots, LANES)[:, var_count : var_count + 1]
-        reply = (node_lane == asked).astype(F32).astype(BF16)
-        rows = jnp.dot(reply, both, preferred_element_type=F32)
-        packed = [rows[:, i * LANES : (i + 1) * LANES].reshape(n_dest, 1, CAP, LANES) for i in range(2)]
-        out_ref[...] = jnp.concatenate(packed, axis=1).astype(BF16)
+        reply = reply_ref[...]
+        rows = jnp.dot(reply, both, preferred_element_type=F32).astype(BF16)
+        out_ref[...] = rows.reshape(out_ref.shape)
 
 
 def predict_kernel(var_count, slot_ref, back_ref, x_ref, out_ref):
-    n_dest, members = back_ref.shape[:2]
-    slots = n_dest * CAP
-    pts = x_ref.shape[2]
-    place = (iota((slots, pts), 0) == slot_ref[...]).astype(F32).astype(BF16)
-    for m in range(members):
-        rows = member_rows(back_ref, m)
-        got = lax.dot_general(rows, place, TN, preferred_element_type=F32)
-        out_ref[m] = (x_ref[m].astype(F32) + got[0:var_count]).astype(BF16)
+    n_dest, _, lanes = back_ref.shape
+    place = one_hot(n_dest * CAP, slot_ref[...])
+    rows = back_ref[...].reshape(n_dest * CAP, lanes)
+    got = lax.dot_general(rows, place, TN, preferred_element_type=F32)
+    for m in range(x_ref.shape[0]):
+        out_ref[m] = (x_ref[m].astype(F32) + got[m * LANES : m * LANES + var_count]).astype(BF16)
 
 
 def score_kernel(mine_ref, other_ref, target_ref, out_ref):
@@ -327,7 +339,7 @@
     slots = n_space * CAP
     in_hbm = functools.partial(pltpu.with_memory_space_constraint, memory_space=pltpu.HBM)
     rows = [in_hbm(a.reshape(1, pts)) for a in (enc_owner, enc_local, dec_owner, dec_local)]
-    wire = jax.ShapeDtypeStruct((n_space, members, CAP, LANES), BF16)
+    wire = jax.ShapeDtypeStruct((n_space, CAP, members * LANES), BF16)
 
     row_shape = pltpu.VMEM((1, pts), jnp.int32)
     outgoing, dec_slot, w_enc, states = pl.pallas_call(
@@ -341,7 +353,7 @@
         ),
         scratch_shapes=[pltpu.VMEM((var_count, members, pts), BF16)]
         + [row_shape] * 4
-        + [pltpu.VMEM((LANES, pts), F32), pltpu.SemaphoreType.DMA((6,))],
+        + [pltpu.SemaphoreType.DMA((6,))],
         compiler_params=params(),
         cost_estimate=cost(2),
         name="pack",
@@ -393,7 +405,9 @@
                 pltpu.VMEM((2, nodes + half, nodes), F32),
                 pltpu.VMEM((2, nodes + half, nodes), F32),
                 pltpu.VMEM((2, nodes + half, nodes), F32),
-            ],
+                pltpu.VMEM((nodes, width), BF16),
+            ]
+            + [pltpu.VMEM((slots, nodes), BF16)] * m,
             compiler_params=params(),
             cost_estimate=cost(8),
             name=f"attend{m}",

time: 92 us -> 89.9 us (0.977)
  Pallas kernels: 21.5 us -> 19.4 us
    pallas_call x1, Pallas kernels: 3.46 us -> 2.06 us  [on_device(): pl.pallas_call(functools.partial(pack_kernel, var_count), in_specs=[HBM_S...]
where the time goes in v5:
time: 89.9 us; the launch traced here: 89.7 us
  blocking collectives  57.7 us (64%)
  Pallas kernels  19.4 us (22%)
  starting transfers between devices  10.7 us (12%)
    all_to_all x1, blocking collectives, on_device(): arrived = lax.all_to_all(outgoing, 'space', 0, 0, tiled=True)  35.3 us
    all_to_all x1, blocking collectives, on_device(): returned = lax.all_to_all(replies, 'space', 0, 0, tiled=True)  22.4 us
    pallas_call x2, Pallas kernels, on_device(): pl.pallas_call(functools.partial(attend_kernel, var_count, m, at[0], at[-...  9.2 us
    ppermute x1, starting transfers between devices, on_device(): other = lax.ppermute(predicted, 'member', [(0, 1), (1, 0)])  5.21 us
    ppermute x2, starting transfers between devices, on_device(): lax.ppermute(lo, 'space', down)  4.51 us
    pallas_call x1, Pallas kernels, on_device(): pl.pallas_call(functools.partial(qkv_kernel, len(hidden)), out_shape=(jax...  3.52 us
    pallas_call x2, Pallas kernels, on_device(): pl.pallas_call(functools.partial(encode_kernel, var_count, m), out_shape=...  3.24 us
    pallas_call x1, Pallas kernels, on_device(): pl.pallas_call(functools.partial(pack_kernel, var_count), in_specs=[HBM_S...  2.06 us
  transfers between devices with their start and end apart: 5, of which 1 were waited for; matrix products, arithmetic and copies ran while one was open for 1% of the time, Pallas kernels for 11%

profile of v5, /device:TPU:1, one launch (start us, length us, event | category | flops | bytes accessed | tf_op | source)
XLA Modules:
  0.0 89.7 jit_solution(7901743652793199973)
XLA Ops:
  0.6 2.1 %pack.1 = (bf16[128,8,256]{2,1,0:T(8,128)(2,1)S(1)}, s32[1,512]{1,0:T(1,128)S(1)}, bf16[98,1024]{1,0:T(8,128)(2,1)S(1)}, bf16[2,98,512]{2,1,0:T(8,128)(2,1)S(1)}) custom-call(bf16[98,2,512]{2,1,0:T(2,128)(2,1)} %bitcast.16, s32[1,512]{1,0:T(1,128)} %bitcast.17, s32[1,512]{1,0:T(1,128)} %bitcast.18, s32[1,512]{1,0:T(1,128)} %bitcast.19, s32[1,512]{1,0:T(1,128)} %bitcast.20, ...), custom_call_target="tpu_custom_call" | custom-call | flops 1400000000 | bytes 1048576 | tf_op jit(solution)/shard_map/pack/pallas_call | solution.py:345
  2.7 35.3 %all_to_all.10.in_ref.rest_1_ = bf16[128,8,256]{2,1,0:T(8,128)(2,1)S(1)} all-to-all(bf16[128,8,256]{2,1,0:T(8,128)(2,1)S(1)} %get-tuple-element.13), channel_id=1, replica_groups=mesh['member'=2,'space'=128] {'space'}, dimensions={0} | all-to-all | bytes 1048576 | tf_op jit(solution)/shard_map/all_to_all | solution.py:362
  38.0 0.0 slice-start
  38.0 1.6 %encode0.1 = (bf16[128,1024]{1,0:T(8,128)(2,1)S(1)}, bf16[128,1024]{1,0:T(8,128)(2,1)S(1)}) custom-call(bf16[128,8,256]{2,1,0:T(8,128)(2,1)S(1)} %all_to_all.10.in_ref.rest_1_, bf16[98,1024]{1,0:T(8,128)(2,1)S(1)} %get-tuple-element.14.w_ref), custom_call_target="tpu_custom_call" | custom-call | flops 2100000000 | bytes 1048576 | tf_op jit(solution)/shard_map/encode0/pallas_call | solution.py:369
  39.6 0.0 slice-start.1
  39.6 0.9 collective-permute-start.2
  40.5 1.9 %collective-permute-start.3 = (bf16[128,1024]{1,0:T(8,128)(2,1)S(1)}, bf16[128,1024]{1,0:T(8,128)(2,1)S(1)}, u32[]{:S(2)}, u32[]{:S(2)}) collective-permute-start(bf16[128,1024]{1,0:T(8,128)(2,1)S(1)} %get-tuple-element.15.refs_0_.lo_ref), channel_id=1, source_target_pairs={{1,0},{2,1},{3,2},{4,3},{5,4},{6,5},{7,6},{15,7},{14,15},{13,14},{... | collective-permute-start | bytes 786440 | tf_op jit(solution)/shard_map/ppermute | solution.py:378
  42.4 1.6 %encode1.1 = (bf16[128,1024]{1,0:T(8,128)(2,1)S(1)}, bf16[128,1024]{1,0:T(8,128)(2,1)S(1)}) custom-call(bf16[128,8,256]{2,1,0:T(8,128)(2,1)S(1)} %all_to_all.10.in_ref.rest_1_, bf16[98,1024]{1,0:T(8,128)(2,1)S(1)} %get-tuple-element.14.w_ref), custom_call_target="tpu_custom_call" | custom-call | flops 2100000000 | bytes 1048576 | tf_op jit(solution)/shard_map/encode1/pallas_call | solution.py:369
  44.0 0.1 collective-permute-start
  44.1 0.0 copy-start.1
  44.1 0.0 copy-start.2
  44.1 2.6 %collective-permute-start.1 = (bf16[128,1024]{1,0:T(8,128)(2,1)S(1)}, bf16[128,1024]{1,0:T(8,128)(2,1)S(1)}, u32[]{:S(2)}, u32[]{:S(2)}) collective-permute-start(bf16[128,1024]{1,0:T(8,128)(2,1)S(1)} %get-tuple-element.17.refs_2_.lo_ref), channel_id=1, source_target_pairs={{1,0},{2,1},{3,2},{4,3},{5,4},{6,5},{7,6},{15,7},{14,15},{13,14},{... | collective-permute-start | bytes 786440 | tf_op jit(solution)/shard_map/ppermute | solution.py:378
  46.8 0.0 slice-done
  46.8 0.0 slice-done.1
  46.8 3.5 %qkv.1 = (bf16[512,2048]{1,0:T(8,128)(2,1)S(1)}, bf16[1024,512]{1,0:T(8,128)(2,1)S(1)}) custom-call(bf16[128,1024]{1,0:T(8,128)(2,1)S(1)} %get-tuple-element.15.refs_0_.lo_ref, bf16[128,1024]{1,0:T(8,128)(2,1)S(1)} %get-tuple-element.16.refs_1_.hi_ref, bf16[128,1024]{1,0:T(8,128)(2,1)S(1)} %get-tuple-element.17.refs_2_.lo_ref, ...), custom_call_target="tpu_custom_call" | custom-call | flops 3500000000 | bytes 1048576 | tf_op jit(solution)/shard_map/qkv/pallas_call | solution.py:380
  50.3 0.0 collective-permute-done.2.bef_ref
  50.3 0.0 collective-permute-done.3.aft_ref
  50.3 0.0 copy-done.1
  50.3 0.0 copy-done.2
  50.4 4.4 %attend0.1.rest_0_ = bf16[256,128]{1,0:T(8,128)(2,1)S(1)} custom-call(bf16[512,2048]{1,0:T(8,128)(2,1)S(1)} %get-tuple-element.19.qk_ref, bf16[1024,512]{1,0:T(8,128)(2,1)S(1)} %get-tuple-element.20.vt_ref, bf16[128,1024]{1,0:T(8,128)(2,1)S(1)} %get-tuple-element.15.refs_0_.lo_ref, bf16[128,1024]{1,0:T(8,128)(2,1)S(1)} %get-tuple-element.16.refs_1_.hi_ref, ...), custom_call_target="tpu_custom_call" | custom-call | flops 5600000000 | bytes 1048576 | tf_op jit(solution)/shard_map/attend0/pallas_call | solution.py:395
  54.7 0.0 collective-permute-done.bef_ref
  54.7 0.0 collective-permute-done.1.aft_ref
  54.8 4.8 %attend1.1 = bf16[128,8,256]{2,1,0:T(8,128)(2,1)S(1)} custom-call(bf16[512,2048]{1,0:T(8,128)(2,1)S(1)} %get-tuple-element.19.qk_ref, bf16[1024,512]{1,0:T(8,128)(2,1)S(1)} %get-tuple-element.20.vt_ref, bf16[128,1024]{1,0:T(8,128)(2,1)S(1)} %get-tuple-element.17.refs_2_.lo_ref, bf16[128,1024]{1,0:T(8,128)(2,1)S(1)} %get-tuple-element.18.refs_3_.hi_ref, ...), custom_call_target="tpu_custom_call" | custom-call | flops 5600000000 | bytes 1048576 | tf_op jit(solution)/shard_map/attend1/pallas_call | solution.py:395
  59.6 0.0 copy-start
  59.6 22.4 %all_to_all.11.back_ref = bf16[128,8,256]{2,1,0:T(8,128)(2,1)S(1)} all-to-all(bf16[128,8,256]{2,1,0:T(8,128)(2,1)S(1)} %attend1.1), channel_id=1, replica_groups=mesh['member'=2,'space'=128] {'space'}, dimensions={0} | all-to-all | bytes 1048576 | tf_op jit(solution)/shard_map/all_to_all | solution.py:417
  82.0 0.5 predict.1.mine_ref
  82.5 5.2 %collective-permute-start.4 = (bf16[2,98,512]{2,1,0:T(8,128)(2,1)S(1)}, bf16[2,98,512]{2,1,0:T(8,128)(2,1)S(1)}, u32[]{:S(2)}, u32[]{:S(2)}) collective-permute-start(bf16[2,98,512]{2,1,0:T(8,128)(2,1)S(1)} %predict.1.mine_ref), channel_id=1, source_target_pairs={{0,128},{128,0},{1,129},{129,1},{2,130},{130,2},{3,131},{131,3},{4... | collective-permute-start | bytes 602120 | tf_op jit(solution)/shard_map/ppermute | solution.py:424
  87.7 0.8 copy.12
  88.5 0.3 collective-permute-done.4.other_ref
  88.8 0.0 copy-done
  88.8 0.9 %score.1 = f32[98,512]{1,0:T(8,128)} custom-call(bf16[2,98,512]{2,1,0:T(8,128)(2,1)S(1)} %predict.1.mine_ref, bf16[2,98,512]{2,1,0:T(8,128)(2,1)S(1)} %collective-permute-done.4.other_ref, f32[98,512]{1,0:T(8,128)S(1)} %bitcast.10), custom_call_target="tpu_custom_call" | custom-call | tf_op jit(solution)/shard_map/score/pallas_call | solution.py:425
  (1 shorter events, 0.0 us)
Async XLA Ops:
  38.0 8.8 %slice-start = ((s8[6291456]{0:T(1024)(128)(4,1)}), s8[4194304]{0:T(1024)(128)(4,1)S(1)}, s32[]{:S(2)}) async-start(s8[6291456]{0:T(1024)(128)(4,1)} %bitcast.11), calls=%async_computation.2 | async-start | bytes 8388608
  39.6 7.2 %slice-start.1 = ((s8[6291456]{0:T(1024)(128)(4,1)}), s8[2097152]{0:T(1024)(128)(4,1)S(1)}, s32[]{:S(2)}) async-start(s8[6291456]{0:T(1024)(128)(4,1)} %bitcast.11), calls=%async_computation.3 | async-start | bytes 4194304
  39.6 10.7 %collective-permute-start.2 = (bf16[128,1024]{1,0:T(8,128)(2,1)S(1)}, bf16[128,1024]{1,0:T(8,128)(2,1)S(1)}, u32[]{:S(2)}, u32[]{:S(2)}) collective-permute-start(bf16[128,1024]{1,0:T(8,128)(2,1)S(1)} %get-tuple-element.16.refs_1_.hi_ref), channel_id=1, source_target_pairs={{0,1},{1,2},{2,3},{3,4},{4,5},{5,6},{6,7},{7,15},{15,14},{14,13},{... | collective-permute-start | bytes 786440 | tf_op jit(solution)/shard_map/ppermute | solution.py:378
  40.5 9.8 %collective-permute-start.3 = (bf16[128,1024]{1,0:T(8,128)(2,1)S(1)}, bf16[128,1024]{1,0:T(8,128)(2,1)S(1)}, u32[]{:S(2)}, u32[]{:S(2)}) collective-permute-start(bf16[128,1024]{1,0:T(8,128)(2,1)S(1)} %get-tuple-element.15.refs_0_.lo_ref), channel_id=1, source_target_pairs={{1,0},{2,1},{3,2},{4,3},{5,4},{6,5},{7,6},{15,7},{14,15},{13,14},{... | collective-permute-start | bytes 786440 | tf_op jit(solution)/shard_map/ppermute | solution.py:378
  44.0 10.7 %collective-permute-start = (bf16[128,1024]{1,0:T(8,128)(2,1)S(1)}, bf16[128,1024]{1,0:T(8,128)(2,1)S(1)}, u32[]{:S(2)}, u32[]{:S(2)}) collective-permute-start(bf16[128,1024]{1,0:T(8,128)(2,1)S(1)} %get-tuple-element.18.refs_3_.hi_ref), channel_id=1, source_target_pairs={{0,1},{1,2},{2,3},{3,4},{4,5},{5,6},{6,7},{7,15},{15,14},{14,13},{... | collective-permute-start | bytes 786440 | tf_op jit(solution)/shard_map/ppermute | solution.py:378
  44.1 6.2 %copy-start.1 = (bf16[1024,1024]{1,0:T(8,128)(2,1)S(1)}, bf16[1024,1024]{1,0:T(8,128)(2,1)}, u32[]{:S(2)}) copy-start(bf16[1024,1024]{1,0:T(8,128)(2,1)} %w_out_ref.3) | copy-start | bytes 6291460
  44.1 6.2 %copy-start.2 = (bf16[1024,98]{0,1:T(8,128)(2,1)S(1)}, bf16[1024,98]{0,1:T(8,128)(2,1)}, u32[]{:S(2)}) copy-start(bf16[1024,98]{0,1:T(8,128)(2,1)} %param.19) | copy-start | bytes 602116
  44.1 10.6 %collective-permute-start.1 = (bf16[128,1024]{1,0:T(8,128)(2,1)S(1)}, bf16[128,1024]{1,0:T(8,128)(2,1)S(1)}, u32[]{:S(2)}, u32[]{:S(2)}) collective-permute-start(bf16[128,1024]{1,0:T(8,128)(2,1)S(1)} %get-tuple-element.17.refs_2_.lo_ref), channel_id=1, source_target_pairs={{1,0},{2,1},{3,2},{4,3},{5,4},{6,5},{7,6},{15,7},{14,15},{13,14},{... | collective-permute-start | bytes 786440 | tf_op jit(solution)/shard_map/ppermute | solution.py:378
  59.6 29.2 %copy-start = (f32[512,98]{0,1:T(8,128)S(1)}, f32[512,98]{0,1:T(8,128)}, u32[]{:S(2)}) copy-start(f32[512,98]{0,1:T(8,128)} %param.11) | copy-start | bytes 602116
  82.5 6.3 %collective-permute-start.4 = (bf16[2,98,512]{2,1,0:T(8,128)(2,1)S(1)}, bf16[2,98,512]{2,1,0:T(8,128)(2,1)S(1)}, u32[]{:S(2)}, u32[]{:S(2)}) collective-permute-start(bf16[2,98,512]{2,1,0:T(8,128)(2,1)S(1)} %predict.1.mine_ref), channel_id=1, source_target_pairs={{0,128},{128,0},{1,129},{129,1},{2,130},{130,2},{3,131},{131,3},{4... | collective-permute-start | bytes 602120 | tf_op jit(solution)/shard_map/ppermute | solution.py:424

commit v6 on v5

--- a/solution.py
+++ b/solution.py
@@ -2,6 +2,7 @@
 
 import jax
 import jax.numpy as jnp
+import numpy as np
 from jax import lax
 from jax.experimental import pallas as pl
 from jax.experimental.pallas import tpu as pltpu
@@ -14,8 +15,28 @@
 CAP_BITS = 3
 META = 104
 LANES = 128
-GRID = (4, 4, 8)
-Y_BITS, Z_BITS = 2, 3
+PATHS = (
+    (
+        32, 40, 72, 64, 96, 104, 112, 120, 88, 80, 48, 56, 24, 16, 8, 0,
+        1, 33, 65, 97, 105, 73, 41, 49, 81, 113, 121, 89, 57, 25, 17, 9,
+        10, 2, 34, 66, 98, 106, 74, 42, 50, 82, 114, 122, 90, 58, 26, 18,
+        19, 51, 83, 75, 43, 11, 3, 35, 67, 99, 107, 115, 123, 91, 59, 27,
+        28, 124, 100, 4, 36, 68, 76, 108, 12, 44, 52, 20, 116, 84, 92, 60,
+        61, 93, 125, 29, 5, 37, 69, 101, 109, 13, 45, 77, 85, 117, 21, 53,
+        54, 86, 118, 126, 94, 62, 30, 22, 14, 6, 38, 70, 102, 110, 78, 46,
+        47, 79, 111, 15, 23, 55, 87, 119, 127, 31, 63, 95, 71, 103, 7, 39,
+    ),
+    (
+        0, 7, 6, 5, 4, 3, 2, 1, 9, 8, 15, 14, 13, 12, 11, 10,
+        18, 17, 16, 23, 22, 21, 20, 19, 27, 26, 25, 24, 31, 30, 29, 28,
+        60, 59, 58, 57, 56, 63, 62, 61, 53, 52, 51, 50, 49, 48, 55, 54,
+        46, 45, 44, 43, 42, 41, 40, 47, 39, 38, 37, 36, 35, 34, 33, 32,
+        64, 71, 70, 69, 68, 67, 66, 65, 73, 72, 79, 78, 77, 76, 75, 74,
+        82, 81, 80, 87, 86, 85, 84, 83, 91, 90, 89, 88, 95, 94, 93, 92,
+        124, 123, 122, 121, 120, 127, 126, 125, 117, 116, 115, 114, 113, 112, 119, 118,
+        110, 109, 108, 107, 106, 105, 104, 111, 103, 102, 101, 100, 99, 98, 97, 96,
+    ),
+)
 
 FAIR_ALPHA = 0.95
 NORM_EPS = 1e-05
@@ -36,19 +57,13 @@
     return lax.broadcasted_iota(jnp.int32, shape, dim)
 
 
-def path_place(block):
-    _, ny, nz = GRID
-    line, z = block >> Z_BITS, block & (nz - 1)
-    x, y = line >> Y_BITS, line & (ny - 1)
-    z = z + (line & 1) * (nz - 1 - 2 * z)
-    y = y + (x & 1) * (ny - 1 - 2 * y)
-    return (((x << Y_BITS) + y) << Z_BITS) + z
-
-
-def slot_row(owner_row):
-    pts = owner_row.shape[1]
-    owner = owner_row.astype(F32)
-    owner_col = jnp.broadcast_to(owner, (8, pts)).T[:, 0:1]
+def column(row):
+    return jnp.broadcast_to(row, (8, row.shape[1])).T[:, 0:1]
+
+
+def rank_row(owner):
+    pts = owner.shape[1]
+    owner_col = column(owner)
     block = LANES
     ahead = iota((block, block), 0) < iota((block, block), 1)
     ranks = []
@@ -58,8 +73,13 @@
         for r in range(0, c, block):
             count += jnp.where(owner_col[r : r + block] == wide, 1.0, 0.0)
         ranks.append(jnp.sum(count, axis=0, keepdims=True))
-    rank = jnp.concatenate(ranks, axis=1).astype(jnp.int32)
-    return path_place(owner_row) * CAP + rank
+    return jnp.concatenate(ranks, axis=1)
+
+
+def device_row(owner, block_of):
+    shape = (block_of.shape[0], owner.shape[1])
+    found = block_of == jnp.broadcast_to(owner, shape)
+    return jnp.sum(jnp.where(found, iota(shape, 0).astype(F32), 0.0), axis=0, keepdims=True)
 
 
 def one_hot(count, row):
@@ -67,9 +87,19 @@
     return jnp.where(ids == row.astype(jnp.int16), jnp.ones((), BF16), jnp.zeros((), BF16))
 
 
+def place_color(place):
+    return (place >> 5) + ((place >> 3) & 3) + (place & 7)
+
+
+def first_half():
+    start = jnp.where(lax.axis_index("member") == 0, place_color(PATHS[0][0]), place_color(PATHS[1][0]))
+    odd = (place_color(lax.axis_index("space")) + start) & 1
+    return pl.multiple_of((1 - odd) * HALF_WIN, HALF_WIN), pl.multiple_of(odd * HALF_WIN, HALF_WIN)
+
+
 def pack_kernel(
-    var_count, x_hbm, eo_hbm, el_hbm, do_hbm, dl_hbm, w_hbm, out_ref, slot_ref, w_ref, states_ref,
-    x_ref, eo_ref, el_ref, do_ref, dl_ref, sems,
+    var_count, x_hbm, eo_hbm, el_hbm, do_hbm, dl_hbm, w_hbm, block_hbm, out_ref, slot_ref, w_ref, states_ref,
+    x_ref, eo_ref, el_ref, do_ref, dl_ref, block_ref, sems,
 ):
     members, _, pts = states_ref.shape
     n_dest = out_ref.shape[0]
@@ -81,23 +111,28 @@
         (dl_hbm, dl_ref),
         (x_hbm, x_ref),
         (w_hbm, w_ref),
+        (block_hbm.at[lax.axis_index("member")], block_ref),
     ]
     copies = [pltpu.make_async_copy(src, dst, sems.at[i]) for i, (src, dst) in enumerate(pairs)]
     for copy in copies:
         copy.start()
-    copies[0].wait()
-    enc_slot = slot_row(eo_ref[...])
-    copies[1].wait()
-    dec_slot = slot_row(do_ref[...])
-    slot_ref[...] = dec_slot
-    copies[2].wait()
-    copies[3].wait()
-    copies[4].wait()
     rows_in = members * var_count
     lanes = members * LANES
     row_id, col_id = iota((lanes, rows_in), 0), iota((lanes, rows_in), 1)
     var, m = row_id & (LANES - 1), row_id >> 7
     apart = ((var * members + m == col_id) & (var < var_count)).astype(F32).astype(BF16)
+    copies[0].wait()
+    copies[1].wait()
+    copies[6].wait()
+    owners = [eo_ref[...].astype(F32), do_ref[...].astype(F32)]
+    block_of = column(block_ref[...])
+    enc_slot, dec_slot = (
+        (device_row(owner, block_of) * CAP + rank_row(owner)).astype(jnp.int32) for owner in owners
+    )
+    slot_ref[...] = dec_slot
+    copies[2].wait()
+    copies[3].wait()
+    copies[4].wait()
     fields = jnp.dot(apart, x_ref[...].reshape(rows_in, pts), preferred_element_type=F32)
     for i in range(members):
         states_ref[i] = fields[i * LANES : i * LANES + var_count].astype(BF16)
@@ -115,7 +150,7 @@
     w_ref[...] = w_ref[...] * jnp.asarray(0.5, BF16)
 
 
-def encode_kernel(var_count, m, in_ref, w_ref, lo_ref, hi_ref, pooled_ref, ea_ref, eb_ref):
+def encode_kernel(var_count, m, in_ref, w_ref, one_ref, two_ref, pooled_ref, ea_ref, eb_ref):
     n_dest = in_ref.shape[0]
     slots = n_dest * CAP
     width = w_ref.shape[1]
@@ -146,21 +181,28 @@
             embed(c + 1, there)
         pool(c, here)
     step = 32
-    for out_ref, first in ((lo_ref, 0), (hi_ref, HALF_WIN)):
-        for r in range(0, HALF_WIN, step):
-            part = slice(first + r, first + r + step)
-            pooled = pooled_ref[part, :] * share[part]
-            centred = pooled - jnp.mean(pooled, axis=1, keepdims=True)
-            variance = jnp.mean(centred * centred, axis=1, keepdims=True)
-            out_ref[r : r + step, :] = (centred * lax.rsqrt(variance + NORM_EPS)).astype(BF16)
+    odd = first_half()[0] == 0
+    for r in range(0, HALF_WIN, step):
+        lower, upper = slice(r, r + step), slice(HALF_WIN + r, HALF_WIN + r + step)
+        halves = []
+        for part in (lower, upper):
+            summed, part_share = pooled_ref[part, :], share[part]
+            centred = summed - jnp.mean(summed, axis=1, keepdims=True)
+            variance = jnp.mean(centred * centred, axis=1, keepdims=True) * (part_share * part_share)
+            halves.append((centred * (part_share * lax.rsqrt(variance + NORM_EPS))).astype(BF16))
+        one_ref[lower, :] = jnp.where(odd, halves[0], halves[1])
+        two_ref[lower, :] = jnp.where(odd, halves[1], halves[0])
 
 
 def qkv_kernel(halves, *refs):
     hidden_refs, (w_ref, qk_ref, vt_ref, rows_ref) = refs[:halves], refs[halves:]
     width = rows_ref.shape[1]
     half = rows_ref.shape[0] // halves
-    for i, ref in enumerate(hidden_refs):
-        rows_ref[i * half : (i + 1) * half, :] = ref[...]
+    odd = first_half()[0] == 0
+    for i in range(0, halves, 2):
+        one, two = hidden_refs[i][...], hidden_refs[i + 1][...]
+        rows_ref[i * half : (i + 1) * half, :] = jnp.where(odd, one, two)
+        rows_ref[(i + 1) * half : (i + 2) * half, :] = jnp.where(odd, two, one)
 
     def project(cols):
         return jnp.dot(rows_ref[...], w_ref[:, cols], preferred_element_type=F32).astype(BF16)
@@ -173,20 +215,24 @@
 
 
 def attend_kernel(
-    var_count, m, first_at, last_at, qk_ref, vt_ref, lo_ref, hi_ref, bef_ref, aft_ref, w_kv_ref, w_out_ref,
+    var_count, m, qk_ref, vt_ref, rows_ref, one_ref, two_ref, w_kv_ref, w_out_ref,
     w_dec_ref, *rest,
 ):
     if m == 0:
         out_ref, kh_ref, vth_ref, att_ref, proc_ref, left_ref, right_ref, sa_ref, sb_ref, e_ref, halo_ref = rest
     else:
         dec_ref, in_ref, out_ref, kh_ref, vth_ref, att_ref, proc_ref, left_ref, right_ref, sa_ref, sb_ref, e_ref, halo_ref, reply_ref = rest
-    half, width = lo_ref.shape
-    me = lax.axis_index("space")
+    half, width = one_ref.shape
+    core, me = lax.axis_index("member"), lax.axis_index("space")
+    first_at = jnp.where(core == 0, PATHS[0][0], PATHS[1][0])
+    last_at = jnp.where(core == 0, PATHS[0][-1], PATHS[1][-1])
     at_first, at_last = (me == first_at).astype(jnp.int32), (me == last_at).astype(jnp.int32)
     nodes = 2 * half
     head_dim = width // HEADS
-    halo_ref[0:half, :] = bef_ref[...]
-    halo_ref[half:, :] = aft_ref[...]
+    one, two = one_ref[...], two_ref[...]
+    odd = first_half()[0] == 0
+    halo_ref[0:half, :] = jnp.where(odd, one, two)
+    halo_ref[half:, :] = jnp.where(odd, two, one)
     chunk = 256
 
     def project(c):
@@ -275,8 +321,8 @@
     for c in range(0, width, chunk):
         cols = slice(c, c + chunk)
         mixed = jnp.dot(att_ref[...], w_out_ref[:, cols], preferred_element_type=F32)
-        proc_ref[0:half, cols] = (lo_ref[:, cols].astype(F32) + mixed[0:half]).astype(BF16)
-        proc_ref[half:, cols] = (hi_ref[:, cols].astype(F32) + mixed[half:]).astype(BF16)
+        hidden = rows_ref[base : base + nodes, cols].astype(F32)
+        proc_ref[:, cols] = (hidden + mixed).astype(BF16)
     decoded = nt_dot(proc_ref[...], w_dec_ref[...]).astype(BF16)
     if m == 0:
         out_ref[...] = jnp.zeros_like(out_ref)
@@ -300,16 +346,26 @@
         out_ref[m] = (x_ref[m].astype(F32) + got[m * LANES : m * LANES + var_count]).astype(BF16)
 
 
-def score_kernel(mine_ref, other_ref, target_ref, out_ref):
-    fields = [r[m].astype(F32) for r in (mine_ref, other_ref) for m in range(mine_ref.shape[0])]
-    count = len(fields)
-    target = target_ref[...]
-    skill = sum(jnp.abs(f - target) for f in fields) / count
-    spread = 2.0 * sum(
-        jnp.abs(fields[i] - fields[j]) for i in range(count) for j in range(i + 1, count)
-    )
+def score_kernel(mine_ref, other_ref, target_ref, out_hbm, out_ref, sems):
+    refs = [(r, m) for r in (mine_ref, other_ref) for m in range(mine_ref.shape[0])]
+    count = len(refs)
     fair_eps = (1.0 - FAIR_ALPHA) / count
-    out_ref[...] = skill - (1.0 - fair_eps) / (2.0 * count * (count - 1)) * spread
+    weight = (1.0 - fair_eps) / (2.0 * count * (count - 1)) * 2.0
+    edges = [0, 32, 64, out_ref.shape[0]]
+    copies = []
+    for i, (lo, hi) in enumerate(zip(edges, edges[1:])):
+        fields = [r[m, lo:hi].astype(F32) for r, m in refs]
+        target = target_ref[lo:hi]
+        skill = sum(jnp.abs(f - target) for f in fields) / count
+        spread = sum(
+            jnp.abs(fields[i] - fields[j]) for i in range(count) for j in range(i + 1, count)
+        )
+        out_ref[lo:hi] = skill - weight * spread
+        rows = pl.ds(lo, hi - lo)
+        copies.append(pltpu.make_async_copy(out_ref.at[rows], out_hbm.at[rows], sems.at[i]))
+        copies[-1].start()
+    for copy in copies:
+        copy.wait()
 
 
 def params(mib=32):
@@ -341,10 +397,13 @@
     rows = [in_hbm(a.reshape(1, pts)) for a in (enc_owner, enc_local, dec_owner, dec_local)]
     wire = jax.ShapeDtypeStruct((n_space, CAP, members * LANES), BF16)
 
+    block_of = np.zeros((len(PATHS), 1, n_space), np.float32)
+    for core, path in enumerate(PATHS):
+        block_of[core, 0, list(path)] = np.arange(n_space)
     row_shape = pltpu.VMEM((1, pts), jnp.int32)
     outgoing, dec_slot, w_enc, states = pl.pallas_call(
         functools.partial(pack_kernel, var_count),
-        in_specs=[HBM_SPEC] * 6,
+        in_specs=[HBM_SPEC] * 7,
         out_shape=(
             wire,
             jax.ShapeDtypeStruct((1, pts), jnp.int32),
@@ -353,20 +412,23 @@
         ),
         scratch_shapes=[pltpu.VMEM((var_count, members, pts), BF16)]
         + [row_shape] * 4
-        + [pltpu.SemaphoreType.DMA((6,))],
+        + [pltpu.VMEM((1, n_space), F32), pltpu.SemaphoreType.DMA((7,))],
         compiler_params=params(),
         cost_estimate=cost(2),
         name="pack",
-    )(in_hbm(jnp.transpose(initial_states, (2, 0, 1))), *rows, in_hbm(w_embed))
-    at = [path_place(b) for b in range(n_space)]
+    )(in_hbm(jnp.transpose(initial_states, (2, 0, 1))), *rows, in_hbm(w_embed), in_hbm(jnp.asarray(block_of)))
     arrived = lax.all_to_all(outgoing, "space", 0, 0, tiled=True)
 
     half_shape = jax.ShapeDtypeStruct((half, width), BF16)
-    up = [(at[i], at[(i + 1) % n_space]) for i in range(n_space)]
-    down = [(j, i) for i, j in up]
+    swaps = [[], []]
+    for c, path in enumerate(PATHS):
+        for i, a in enumerate(path):
+            b = path[(i + 1) % n_space]
+            swaps[i % 2] += [(c * n_space + a, c * n_space + b), (c * n_space + b, c * n_space + a)]
+    both_axes = ("member", "space")
     hidden, halos = [], []
     for m in range(members):
-        lo, hi = pl.pallas_call(
+        ends = pl.pallas_call(
             functools.partial(encode_kernel, var_count, m),
             out_shape=(half_shape, half_shape),
             scratch_shapes=[pltpu.VMEM((nodes, width), F32)] + [pltpu.VMEM((slots, 256), BF16)] * 2,
@@ -374,16 +436,16 @@
             cost_estimate=cost(3),
             name=f"encode{m}",
         )(arrived, w_enc)
-        hidden += [lo, hi]
-        halos.append((lax.ppermute(hi, "space", up), lax.ppermute(lo, "space", down)))
-
-    qk, vt = pl.pallas_call(
+        hidden += ends
+        halos.append([lax.ppermute(end, both_axes, swap) for end, swap in zip(ends, swaps)])
+
+    qk, vt, node_rows = pl.pallas_call(
         functools.partial(qkv_kernel, len(hidden)),
         out_shape=(
             jax.ShapeDtypeStruct((members * nodes, 2 * width), BF16),
             jax.ShapeDtypeStruct((width, members * nodes), BF16),
+            jax.ShapeDtypeStruct((members * nodes, width), BF16),
         ),
-        scratch_shapes=[pltpu.VMEM((members * nodes, width), BF16)],
         cost_estimate=cost(5),
         compiler_params=params(),
         name="qkv",
@@ -393,7 +455,7 @@
     for m in range(members):
         extra = () if m == 0 else (decoded, arrived)
         decoded = pl.pallas_call(
-            functools.partial(attend_kernel, var_count, m, at[0], at[-1]),
+            functools.partial(attend_kernel, var_count, m),
             out_shape=jax.ShapeDtypeStruct((nodes, LANES), BF16) if m == 0 else wire,
             scratch_shapes=[
                 pltpu.VMEM((nodes, width), BF16),
@@ -411,7 +473,7 @@
             compiler_params=params(),
             cost_estimate=cost(8),
             name=f"attend{m}",
-        )(qk, vt, *hidden[2 * m : 2 * m + 2], *halos[m], w_qkv, w_out, w_decode.T, *extra)
+        )(qk, vt, node_rows, *halos[m], w_qkv, w_out, w_decode.T, *extra)
     replies = decoded
 
     returned = lax.all_to_all(replies, "space", 0, 0, tiled=True)
@@ -424,7 +486,10 @@
     other = lax.ppermute(predicted, "member", [(0, 1), (1, 0)])
     error = pl.pallas_call(
         score_kernel,
+        in_specs=[VMEM_SPEC] * 3,
+        out_specs=HBM_SPEC,
         out_shape=jax.ShapeDtypeStruct((var_count, pts), F32),
+        scratch_shapes=[pltpu.VMEM((var_count, pts), F32), pltpu.SemaphoreType.DMA((3,))],
         compiler_params=params(),
         name="score",
     )(predicted, other, target.T)

time: 89.9 us -> 89.7 us (level)
  starting transfers between devices: 10.7 us -> 8.37 us
  blocking collectives: 57.7 us -> 59.4 us
    ppermute x4, starting transfers between devices: 5.48 us -> 3.24 us  [on_device(): lax.ppermute(end, both_axes, swap)]
    all_to_all x1, blocking collectives: 22.4 us -> 24.1 us  [on_device(): returned = lax.all_to_all(replies, 'space', 0, 0, tiled=True)]
where the time goes in v6:
time: 89.7 us; the launch traced here: 89.5 us
  blocking collectives  59.4 us (66%)
  Pallas kernels  19.6 us (22%)
  starting transfers between devices  8.37 us (9%)
  between operations  0.94 us (1%)
    all_to_all x1, blocking collectives, on_device(): arrived = lax.all_to_all(outgoing, 'space', 0, 0, tiled=True)  35.3 us
    all_to_all x1, blocking collectives, on_device(): returned = lax.all_to_all(replies, 'space', 0, 0, tiled=True)  24.1 us
    pallas_call x2, Pallas kernels, on_device(): pl.pallas_call(functools.partial(attend_kernel, var_count, m), out_shape=...  9.23 us
    ppermute x1, starting transfers between devices, on_device(): other = lax.ppermute(predicted, 'member', [(0, 1), (1, 0)])  5.13 us
    pallas_call x1, Pallas kernels, on_device(): pl.pallas_call(functools.partial(qkv_kernel, len(hidden)), out_shape=(jax...  3.55 us
    ppermute x4, starting transfers between devices, on_device(): lax.ppermute(end, both_axes, swap)  3.24 us
    pallas_call x2, Pallas kernels, on_device(): pl.pallas_call(functools.partial(encode_kernel, var_count, m), out_shape=...  3.17 us
    pallas_call x1, Pallas kernels, on_device(): pl.pallas_call(functools.partial(pack_kernel, var_count), in_specs=[HBM_S...  2.28 us
  transfers between devices with their start and end apart: 5, of which 1 were waited for; matrix products, arithmetic and copies ran while one was open for 1% of the time, Pallas kernels for 11%

profile of v6, /device:TPU:1, one launch (start us, length us, event | category | flops | bytes accessed | tf_op | source)
XLA Modules:
  0.0 89.5 jit_solution(13421912762940399128)
XLA Ops:
  0.6 2.3 %pack.1 = (bf16[128,8,256]{2,1,0:T(8,128)(2,1)S(1)}, s32[1,512]{1,0:T(1,128)S(1)}, bf16[98,1024]{1,0:T(8,128)(2,1)S(1)}, bf16[2,98,512]{2,1,0:T(8,128)(2,1)S(1)}) custom-call(bf16[98,2,512]{2,1,0:T(2,128)(2,1)} %bitcast.16, s32[1,512]{1,0:T(1,128)} %bitcast.17, s32[1,512]{1,0:T(1,128)} %bitcast.18, s32[1,512]{1,0:T(1,128)} %bitcast.19, s32[1,512]{1,0:T(1,128)} %bitcast.20, ...), custom_call_target="tpu_custom_call" | custom-call | flops 1400000000 | bytes 1048576 | tf_op jit(solution)/shard_map/pack/pallas_call | solution.py:404
  2.9 35.3 %all_to_all.10.in_ref.rest_1_ = bf16[128,8,256]{2,1,0:T(8,128)(2,1)S(1)} all-to-all(bf16[128,8,256]{2,1,0:T(8,128)(2,1)S(1)} %get-tuple-element.14), channel_id=1, replica_groups=mesh['member'=2,'space'=128] {'space'}, dimensions={0} | all-to-all | bytes 1048576 | tf_op jit(solution)/shard_map/all_to_all | solution.py:420
  38.2 0.0 slice-start
  38.2 1.6 %encode0.1 = (bf16[128,1024]{1,0:T(8,128)(2,1)S(1)}, bf16[128,1024]{1,0:T(8,128)(2,1)S(1)}) custom-call(bf16[128,8,256]{2,1,0:T(8,128)(2,1)S(1)} %all_to_all.10.in_ref.rest_1_, bf16[98,1024]{1,0:T(8,128)(2,1)S(1)} %get-tuple-element.15.w_ref), custom_call_target="tpu_custom_call" | custom-call | flops 2100000000 | bytes 1048576 | tf_op jit(solution)/shard_map/encode0/pallas_call | solution.py:431
  39.8 0.1 collective-permute-start.2
  39.9 0.0 slice-start.1
  39.9 1.1 %collective-permute-start.3 = (bf16[128,1024]{1,0:T(8,128)(2,1)S(1)}, bf16[128,1024]{1,0:T(8,128)(2,1)S(1)}, u32[]{:S(2)}, u32[]{:S(2)}) collective-permute-start(bf16[128,1024]{1,0:T(8,128)(2,1)S(1)} %get-tuple-element.17.refs_1_), channel_id=1, source_target_pairs={{40,72},{72,40},{64,96},{96,64},{104,112},{112,104},{120,88},{88,1... | collective-permute-start | bytes 786440 | tf_op jit(solution)/shard_map/ppermute | solution.py:440
  41.1 1.6 %encode1.1 = (bf16[128,1024]{1,0:T(8,128)(2,1)S(1)}, bf16[128,1024]{1,0:T(8,128)(2,1)S(1)}) custom-call(bf16[128,8,256]{2,1,0:T(8,128)(2,1)S(1)} %all_to_all.10.in_ref.rest_1_, bf16[98,1024]{1,0:T(8,128)(2,1)S(1)} %get-tuple-element.15.w_ref), custom_call_target="tpu_custom_call" | custom-call | flops 2100000000 | bytes 1048576 | tf_op jit(solution)/shard_map/encode1/pallas_call | solution.py:431
  42.6 1.6 %collective-permute-start = (bf16[128,1024]{1,0:T(8,128)(2,1)S(1)}, bf16[128,1024]{1,0:T(8,128)(2,1)S(1)}, u32[]{:S(2)}, u32[]{:S(2)}) collective-permute-start(bf16[128,1024]{1,0:T(8,128)(2,1)S(1)} %get-tuple-element.18.refs_2_), channel_id=1, source_target_pairs={{32,40},{40,32},{72,64},{64,72},{96,104},{104,96},{112,120},{120,1... | collective-permute-start | bytes 786440 | tf_op jit(solution)/shard_map/ppermute | solution.py:440
  44.2 0.0 copy-start.1
  44.2 0.0 copy-start.2
  44.3 0.4 collective-permute-start.1
  44.7 0.0 slice-done
  44.7 0.0 slice-done.1
  44.7 3.6 %qkv.1 = (bf16[512,2048]{1,0:T(8,128)(2,1)S(1)}, bf16[1024,512]{1,0:T(8,128)(2,1)S(1)}, bf16[512,1024]{1,0:T(8,128)(2,1)S(1)}) custom-call(bf16[128,1024]{1,0:T(8,128)(2,1)S(1)} %get-tuple-element.16.refs_0_, bf16[128,1024]{1,0:T(8,128)(2,1)S(1)} %get-tuple-element.17.refs_1_, bf16[128,1024]{1,0:T(8,128)(2,1)S(1)} %get-tuple-element.18.refs_2_, ...), custom_call_target="tpu_custom_call" | custom-call | flops 3500000000 | bytes 1048576 | tf_op jit(solution)/shard_map/qkv/pallas_call | solution.py:442
  48.2 0.0 collective-permute-done.2.one_ref
  48.2 0.0 collective-permute-done.3.two_ref
  48.2 0.0 copy-done.1
  48.3 0.0 copy-done.2
  48.3 4.4 %attend0.1.rest_0_ = bf16[256,128]{1,0:T(8,128)(2,1)S(1)} custom-call(bf16[512,2048]{1,0:T(8,128)(2,1)S(1)} %get-tuple-element.20.qk_ref, bf16[1024,512]{1,0:T(8,128)(2,1)S(1)} %get-tuple-element.21.vt_ref, bf16[512,1024]{1,0:T(8,128)(2,1)S(1)} %get-tuple-element.22.rows_ref, bf16[128,1024]{1,0:T(8,128)(2,1)S(1)} %collective-permute-done.2.one_ref, ...), custom_call_target="tpu_custom_call" | custom-call | flops 5600000000 | bytes 1048576 | tf_op jit(solution)/shard_map/attend0/pallas_call | solution.py:457
  52.7 0.0 collective-permute-done.one_ref
  52.7 0.0 collective-permute-done.1.two_ref
  52.7 4.8 %attend1.1 = bf16[128,8,256]{2,1,0:T(8,128)(2,1)S(1)} custom-call(bf16[512,2048]{1,0:T(8,128)(2,1)S(1)} %get-tuple-element.20.qk_ref, bf16[1024,512]{1,0:T(8,128)(2,1)S(1)} %get-tuple-element.21.vt_ref, bf16[512,1024]{1,0:T(8,128)(2,1)S(1)} %get-tuple-element.22.rows_ref, bf16[128,1024]{1,0:T(8,128)(2,1)S(1)} %collective-permute-done.one_ref, ...), custom_call_target="tpu_custom_call" | custom-call | flops 5600000000 | bytes 1048576 | tf_op jit(solution)/shard_map/attend1/pallas_call | solution.py:457
  57.5 0.0 copy-start
  57.5 24.1 %all_to_all.11.back_ref = bf16[128,8,256]{2,1,0:T(8,128)(2,1)S(1)} all-to-all(bf16[128,8,256]{2,1,0:T(8,128)(2,1)S(1)} %attend1.1), channel_id=1, replica_groups=mesh['member'=2,'space'=128] {'space'}, dimensions={0} | all-to-all | bytes 1048576 | tf_op jit(solution)/shard_map/all_to_all | solution.py:479
  81.7 0.5 predict.1.mine_ref
  82.2 5.1 %collective-permute-start.4 = (bf16[2,98,512]{2,1,0:T(8,128)(2,1)S(1)}, bf16[2,98,512]{2,1,0:T(8,128)(2,1)S(1)}, u32[]{:S(2)}, u32[]{:S(2)}) collective-permute-start(bf16[2,98,512]{2,1,0:T(8,128)(2,1)S(1)} %predict.1.mine_ref), channel_id=1, source_target_pairs={{0,128},{128,0},{1,129},{129,1},{2,130},{130,2},{3,131},{131,3},{4... | collective-permute-start | bytes 602120 | tf_op jit(solution)/shard_map/ppermute | solution.py:486
  87.3 0.8 copy.13
  88.1 0.3 collective-permute-done.4.other_ref
  88.4 0.0 copy-done
  88.4 0.9 %score.1 = f32[98,512]{1,0:T(8,128)} custom-call(bf16[2,98,512]{2,1,0:T(8,128)(2,1)S(1)} %predict.1.mine_ref, bf16[2,98,512]{2,1,0:T(8,128)(2,1)S(1)} %collective-permute-done.4.other_ref, f32[98,512]{1,0:T(8,128)S(1)} %bitcast.10), custom_call_target="tpu_custom_call" | custom-call | tf_op jit(solution)/shard_map/score/pallas_call | solution.py:487
  (1 shorter events, 0.0 us)
Async XLA Ops:
  38.2 6.5 %slice-start = ((s8[6291456]{0:T(1024)(128)(4,1)}), s8[4194304]{0:T(1024)(128)(4,1)S(1)}, s32[]{:S(2)}) async-start(s8[6291456]{0:T(1024)(128)(4,1)} %bitcast.11), calls=%async_computation.2 | async-start | bytes 8388608
  39.8 8.4 %collective-permute-start.2 = (bf16[128,1024]{1,0:T(8,128)(2,1)S(1)}, bf16[128,1024]{1,0:T(8,128)(2,1)S(1)}, u32[]{:S(2)}, u32[]{:S(2)}) collective-permute-start(bf16[128,1024]{1,0:T(8,128)(2,1)S(1)} %get-tuple-element.16.refs_0_), channel_id=1, source_target_pairs={{32,40},{40,32},{72,64},{64,72},{96,104},{104,96},{112,120},{120,1... | collective-permute-start | bytes 786440 | tf_op jit(solution)/shard_map/ppermute | solution.py:440
  39.9 4.8 %slice-start.1 = ((s8[6291456]{0:T(1024)(128)(4,1)}), s8[2097152]{0:T(1024)(128)(4,1)S(1)}, s32[]{:S(2)}) async-start(s8[6291456]{0:T(1024)(128)(4,1)} %bitcast.11), calls=%async_computation.3 | async-start | bytes 4194304
  39.9 8.3 %collective-permute-start.3 = (bf16[128,1024]{1,0:T(8,128)(2,1)S(1)}, bf16[128,1024]{1,0:T(8,128)(2,1)S(1)}, u32[]{:S(2)}, u32[]{:S(2)}) collective-permute-start(bf16[128,1024]{1,0:T(8,128)(2,1)S(1)} %get-tuple-element.17.refs_1_), channel_id=1, source_target_pairs={{40,72},{72,40},{64,96},{96,64},{104,112},{112,104},{120,88},{88,1... | collective-permute-start | bytes 786440 | tf_op jit(solution)/shard_map/ppermute | solution.py:440
  42.6 10.0 %collective-permute-start = (bf16[128,1024]{1,0:T(8,128)(2,1)S(1)}, bf16[128,1024]{1,0:T(8,128)(2,1)S(1)}, u32[]{:S(2)}, u32[]{:S(2)}) collective-permute-start(bf16[128,1024]{1,0:T(8,128)(2,1)S(1)} %get-tuple-element.18.refs_2_), channel_id=1, source_target_pairs={{32,40},{40,32},{72,64},{64,72},{96,104},{104,96},{112,120},{120,1... | collective-permute-start | bytes 786440 | tf_op jit(solution)/shard_map/ppermute | solution.py:440
  44.2 4.0 %copy-start.1 = (bf16[1024,1024]{1,0:T(8,128)(2,1)S(1)}, bf16[1024,1024]{1,0:T(8,128)(2,1)}, u32[]{:S(2)}) copy-start(bf16[1024,1024]{1,0:T(8,128)(2,1)} %w_out_ref.3) | copy-start | bytes 6291460
  44.2 4.0 %copy-start.2 = (bf16[1024,98]{0,1:T(8,128)(2,1)S(1)}, bf16[1024,98]{0,1:T(8,128)(2,1)}, u32[]{:S(2)}) copy-start(bf16[1024,98]{0,1:T(8,128)(2,1)} %param.20) | copy-start | bytes 602116
  44.3 8.4 %collective-permute-start.1 = (bf16[128,1024]{1,0:T(8,128)(2,1)S(1)}, bf16[128,1024]{1,0:T(8,128)(2,1)S(1)}, u32[]{:S(2)}, u32[]{:S(2)}) collective-permute-start(bf16[128,1024]{1,0:T(8,128)(2,1)S(1)} %get-tuple-element.19.refs_3_), channel_id=1, source_target_pairs={{40,72},{72,40},{64,96},{96,64},{104,112},{112,104},{120,88},{88,1... | collective-permute-start | bytes 786440 | tf_op jit(solution)/shard_map/ppermute | solution.py:440
  57.5 30.8 %copy-start = (f32[512,98]{0,1:T(8,128)S(1)}, f32[512,98]{0,1:T(8,128)}, u32[]{:S(2)}) copy-start(f32[512,98]{0,1:T(8,128)} %param.12) | copy-start | bytes 602116
  82.2 6.2 %collective-permute-start.4 = (bf16[2,98,512]{2,1,0:T(8,128)(2,1)S(1)}, bf16[2,98,512]{2,1,0:T(8,128)(2,1)S(1)}, u32[]{:S(2)}, u32[]{:S(2)}) collective-permute-start(bf16[2,98,512]{2,1,0:T(8,128)(2,1)S(1)} %predict.1.mine_ref), channel_id=1, source_target_pairs={{0,128},{128,0},{1,129},{129,1},{2,130},{130,2},{3,131},{131,3},{4... | collective-permute-start | bytes 602120 | tf_op jit(solution)/shard_map/ppermute | solution.py:486

commit v7 on v6

--- a/solution.py
+++ b/solution.py
@@ -2,7 +2,6 @@
 
 import jax
 import jax.numpy as jnp
-import numpy as np
 from jax import lax
 from jax.experimental import pallas as pl
 from jax.experimental.pallas import tpu as pltpu
@@ -15,28 +14,8 @@
 CAP_BITS = 3
 META = 104
 LANES = 128
-PATHS = (
-    (
-        32, 40, 72, 64, 96, 104, 112, 120, 88, 80, 48, 56, 24, 16, 8, 0,
-        1, 33, 65, 97, 105, 73, 41, 49, 81, 113, 121, 89, 57, 25, 17, 9,
-        10, 2, 34, 66, 98, 106, 74, 42, 50, 82, 114, 122, 90, 58, 26, 18,
-        19, 51, 83, 75, 43, 11, 3, 35, 67, 99, 107, 115, 123, 91, 59, 27,
-        28, 124, 100, 4, 36, 68, 76, 108, 12, 44, 52, 20, 116, 84, 92, 60,
-        61, 93, 125, 29, 5, 37, 69, 101, 109, 13, 45, 77, 85, 117, 21, 53,
-        54, 86, 118, 126, 94, 62, 30, 22, 14, 6, 38, 70, 102, 110, 78, 46,
-        47, 79, 111, 15, 23, 55, 87, 119, 127, 31, 63, 95, 71, 103, 7, 39,
-    ),
-    (
-        0, 7, 6, 5, 4, 3, 2, 1, 9, 8, 15, 14, 13, 12, 11, 10,
-        18, 17, 16, 23, 22, 21, 20, 19, 27, 26, 25, 24, 31, 30, 29, 28,
-        60, 59, 58, 57, 56, 63, 62, 61, 53, 52, 51, 50, 49, 48, 55, 54,
-        46, 45, 44, 43, 42, 41, 40, 47, 39, 38, 37, 36, 35, 34, 33, 32,
-        64, 71, 70, 69, 68, 67, 66, 65, 73, 72, 79, 78, 77, 76, 75, 74,
-        82, 81, 80, 87, 86, 85, 84, 83, 91, 90, 89, 88, 95, 94, 93, 92,
-        124, 123, 122, 121, 120, 127, 126, 125, 117, 116, 115, 114, 113, 112, 119, 118,
-        110, 109, 108, 107, 106, 105, 104, 111, 103, 102, 101, 100, 99, 98, 97, 96,
-    ),
-)
+GRID = (4, 4, 8)
+Y_BITS, Z_BITS = 2, 3
 
 FAIR_ALPHA = 0.95
 NORM_EPS = 1e-05
@@ -76,10 +55,13 @@
     return jnp.concatenate(ranks, axis=1)
 
 
-def device_row(owner, block_of):
-    shape = (block_of.shape[0], owner.shape[1])
-    found = block_of == jnp.broadcast_to(owner, shape)
-    return jnp.sum(jnp.where(found, iota(shape, 0).astype(F32), 0.0), axis=0, keepdims=True)
+def path_place(block):
+    _, ny, nz = GRID
+    line, z = block >> Z_BITS, block & (nz - 1)
+    x, y = line >> Y_BITS, line & (ny - 1)
+    z = z + (line & 1) * (nz - 1 - 2 * z)
+    y = y + (x & 1) * (ny - 1 - 2 * y)
+    return (((x << Y_BITS) + y) << Z_BITS) + z
 
 
 def one_hot(count, row):
@@ -92,14 +74,13 @@
 
 
 def first_half():
-    start = jnp.where(lax.axis_index("member") == 0, place_color(PATHS[0][0]), place_color(PATHS[1][0]))
-    odd = (place_color(lax.axis_index("space")) + start) & 1
+    odd = place_color(lax.axis_index("space")) & 1
     return pl.multiple_of((1 - odd) * HALF_WIN, HALF_WIN), pl.multiple_of(odd * HALF_WIN, HALF_WIN)
 
 
 def pack_kernel(
-    var_count, x_hbm, eo_hbm, el_hbm, do_hbm, dl_hbm, w_hbm, block_hbm, out_ref, slot_ref, w_ref, states_ref,
-    x_ref, eo_ref, el_ref, do_ref, dl_ref, block_ref, sems,
+    var_count, x_hbm, eo_hbm, el_hbm, do_hbm, dl_hbm, w_hbm, out_ref, slot_ref, w_ref, states_ref,
+    x_ref, eo_ref, el_ref, do_ref, dl_ref, sems,
 ):
     members, _, pts = states_ref.shape
     n_dest = out_ref.shape[0]
@@ -111,7 +92,6 @@
         (dl_hbm, dl_ref),
         (x_hbm, x_ref),
         (w_hbm, w_ref),
-        (block_hbm.at[lax.axis_index("member")], block_ref),
     ]
     copies = [pltpu.make_async_copy(src, dst, sems.at[i]) for i, (src, dst) in enumerate(pairs)]
     for copy in copies:
@@ -123,11 +103,9 @@
     apart = ((var * members + m == col_id) & (var < var_count)).astype(F32).astype(BF16)
     copies[0].wait()
     copies[1].wait()
-    copies[6].wait()
-    owners = [eo_ref[...].astype(F32), do_ref[...].astype(F32)]
-    block_of = column(block_ref[...])
     enc_slot, dec_slot = (
-        (device_row(owner, block_of) * CAP + rank_row(owner)).astype(jnp.int32) for owner in owners
+        path_place(ref[...]) * CAP + rank_row(ref[...].astype(F32)).astype(jnp.int32)
+        for ref in (eo_ref, do_ref)
     )
     slot_ref[...] = dec_slot
     copies[2].wait()
@@ -223,10 +201,8 @@
     else:
         dec_ref, in_ref, out_ref, kh_ref, vth_ref, att_ref, proc_ref, left_ref, right_ref, sa_ref, sb_ref, e_ref, halo_ref, reply_ref = rest
     half, width = one_ref.shape
-    core, me = lax.axis_index("member"), lax.axis_index("space")
-    first_at = jnp.where(core == 0, PATHS[0][0], PATHS[1][0])
-    last_at = jnp.where(core == 0, PATHS[0][-1], PATHS[1][-1])
-    at_first, at_last = (me == first_at).astype(jnp.int32), (me == last_at).astype(jnp.int32)
+    me = lax.axis_index("space")
+    at_first, at_last = (me == path_place(0)).astype(jnp.int32), (me == path_place((1 << 7) - 1)).astype(jnp.int32)
     nodes = 2 * half
     head_dim = width // HEADS
     one, two = one_ref[...], two_ref[...]
@@ -397,13 +373,11 @@
     rows = [in_hbm(a.reshape(1, pts)) for a in (enc_owner, enc_local, dec_owner, dec_local)]
     wire = jax.ShapeDtypeStruct((n_space, CAP, members * LANES), BF16)
 
-    block_of = np.zeros((len(PATHS), 1, n_space), np.float32)
-    for core, path in enumerate(PATHS):
-        block_of[core, 0, list(path)] = np.arange(n_space)
+    path = [path_place(b) for b in range(n_space)]
     row_shape = pltpu.VMEM((1, pts), jnp.int32)
     outgoing, dec_slot, w_enc, states = pl.pallas_call(
         functools.partial(pack_kernel, var_count),
-        in_specs=[HBM_SPEC] * 7,
+        in_specs=[HBM_SPEC] * 6,
         out_shape=(
             wire,
             jax.ShapeDtypeStruct((1, pts), jnp.int32),
@@ -412,20 +386,18 @@
         ),
         scratch_shapes=[pltpu.VMEM((var_count, members, pts), BF16)]
         + [row_shape] * 4
-        + [pltpu.VMEM((1, n_space), F32), pltpu.SemaphoreType.DMA((7,))],
+        + [pltpu.SemaphoreType.DMA((6,))],
         compiler_params=params(),
         cost_estimate=cost(2),
         name="pack",
-    )(in_hbm(jnp.transpose(initial_states, (2, 0, 1))), *rows, in_hbm(w_embed), in_hbm(jnp.asarray(block_of)))
+    )(in_hbm(jnp.transpose(initial_states, (2, 0, 1))), *rows, in_hbm(w_embed))
     arrived = lax.all_to_all(outgoing, "space", 0, 0, tiled=True)
 
     half_shape = jax.ShapeDtypeStruct((half, width), BF16)
     swaps = [[], []]
-    for c, path in enumerate(PATHS):
-        for i, a in enumerate(path):
-            b = path[(i + 1) % n_space]
-            swaps[i % 2] += [(c * n_space + a, c * n_space + b), (c * n_space + b, c * n_space + a)]
-    both_axes = ("member", "space")
+    for i, a in enumerate(path):
+        b = path[(i + 1) % n_space]
+        swaps[i % 2] += [(a, b), (b, a)]
     hidden, halos = [], []
     for m in range(members):
         ends = pl.pallas_call(
@@ -437,7 +409,7 @@
             name=f"encode{m}",
         )(arrived, w_enc)
         hidden += ends
-        halos.append([lax.ppermute(end, both_axes, swap) for end, swap in zip(ends, swaps)])
+        halos.append([lax.ppermute(end, "space", swap) for end, swap in zip(ends, swaps)])
 
     qk, vt, node_rows = pl.pallas_call(
         functools.partial(qkv_kernel, len(hidden)),

time: 89.7 us -> 89.3 us (level)
  no operation moved by 1% of the time
where the time goes in v7:
time: 89.3 us; the launch traced here: 89.1 us
  blocking collectives  58.7 us (66%)
  Pallas kernels  19.3 us (22%)
  starting transfers between devices  9.08 us (10%)
  between operations  0.93 us (1%)
    all_to_all x1, blocking collectives, on_device(): arrived = lax.all_to_all(outgoing, 'space', 0, 0, tiled=True)  35.3 us
    all_to_all x1, blocking collectives, on_device(): returned = lax.all_to_all(replies, 'space', 0, 0, tiled=True)  23.4 us
    pallas_call x2, Pallas kernels, on_device(): pl.pallas_call(functools.partial(attend_kernel, var_count, m), out_shape=...  9.21 us
    ppermute x1, starting transfers between devices, on_device(): other = lax.ppermute(predicted, 'member', [(0, 1), (1, 0)])  5.13 us
    ppermute x4, starting transfers between devices, on_device(): lax.ppermute(end, 'space', swap)  3.95 us
    pallas_call x1, Pallas kernels, on_device(): pl.pallas_call(functools.partial(qkv_kernel, len(hidden)), out_shape=(jax...  3.55 us
    pallas_call x2, Pallas kernels, on_device(): pl.pallas_call(functools.partial(encode_kernel, var_count, m), out_shape=...  3.18 us
    pallas_call x1, Pallas kernels, on_device(): pl.pallas_call(functools.partial(pack_kernel, var_count), in_specs=[HBM_S...  1.95 us
  transfers between devices with their start and end apart: 5, of which 1 were waited for; matrix products, arithmetic and copies ran while one was open for 1% of the time, Pallas kernels for 11%

profile of v7, /device:TPU:1, one launch (start us, length us, event | category | flops | bytes accessed | tf_op | source)
XLA Modules:
  0.0 89.1 jit_solution(16565258887729282327)
XLA Ops:
  0.6 2.0 %pack.1 = (bf16[128,8,256]{2,1,0:T(8,128)(2,1)S(1)}, s32[1,512]{1,0:T(1,128)S(1)}, bf16[98,1024]{1,0:T(8,128)(2,1)S(1)}, bf16[2,98,512]{2,1,0:T(8,128)(2,1)S(1)}) custom-call(bf16[98,2,512]{2,1,0:T(2,128)(2,1)} %bitcast.16, s32[1,512]{1,0:T(1,128)} %bitcast.17, s32[1,512]{1,0:T(1,128)} %bitcast.18, s32[1,512]{1,0:T(1,128)} %bitcast.19, s32[1,512]{1,0:T(1,128)} %bitcast.20, ...), custom_call_target="tpu_custom_call" | custom-call | flops 1400000000 | bytes 1048576 | tf_op jit(solution)/shard_map/pack/pallas_call | solution.py:378
  2.6 35.3 %all_to_all.10.in_ref.rest_1_ = bf16[128,8,256]{2,1,0:T(8,128)(2,1)S(1)} all-to-all(bf16[128,8,256]{2,1,0:T(8,128)(2,1)S(1)} %get-tuple-element.14), channel_id=1, replica_groups=mesh['member'=2,'space'=128] {'space'}, dimensions={0} | all-to-all | bytes 1048576 | tf_op jit(solution)/shard_map/all_to_all | solution.py:394
  37.9 0.0 slice-start
  37.9 1.6 %encode0.1 = (bf16[128,1024]{1,0:T(8,128)(2,1)S(1)}, bf16[128,1024]{1,0:T(8,128)(2,1)S(1)}) custom-call(bf16[128,8,256]{2,1,0:T(8,128)(2,1)S(1)} %all_to_all.10.in_ref.rest_1_, bf16[98,1024]{1,0:T(8,128)(2,1)S(1)} %get-tuple-element.15.w_ref), custom_call_target="tpu_custom_call" | custom-call | flops 2100000000 | bytes 1048576 | tf_op jit(solution)/shard_map/encode0/pallas_call | solution.py:403
  39.5 0.0 slice-start.1
  39.5 0.9 collective-permute-start.2
  40.4 0.4 collective-permute-start.3
  40.7 1.6 %encode1.1 = (bf16[128,1024]{1,0:T(8,128)(2,1)S(1)}, bf16[128,1024]{1,0:T(8,128)(2,1)S(1)}) custom-call(bf16[128,8,256]{2,1,0:T(8,128)(2,1)S(1)} %all_to_all.10.in_ref.rest_1_, bf16[98,1024]{1,0:T(8,128)(2,1)S(1)} %get-tuple-element.15.w_ref), custom_call_target="tpu_custom_call" | custom-call | flops 2100000000 | bytes 1048576 | tf_op jit(solution)/shard_map/encode1/pallas_call | solution.py:403
  42.3 0.6 collective-permute-start
  42.9 0.0 copy-start.1
  42.9 0.0 copy-start.2
  42.9 2.1 %collective-permute-start.1 = (bf16[128,1024]{1,0:T(8,128)(2,1)S(1)}, bf16[128,1024]{1,0:T(8,128)(2,1)S(1)}, u32[]{:S(2)}, u32[]{:S(2)}) collective-permute-start(bf16[128,1024]{1,0:T(8,128)(2,1)S(1)} %get-tuple-element.19.refs_3_), channel_id=1, source_target_pairs={{1,2},{2,1},{3,4},{4,3},{5,6},{6,5},{7,15},{15,7},{14,13},{13,14},... | collective-permute-start | bytes 786440 | tf_op jit(solution)/shard_map/ppermute | solution.py:412
  45.0 0.0 slice-done
  45.0 0.0 slice-done.1
  45.0 3.6 %qkv.1 = (bf16[512,2048]{1,0:T(8,128)(2,1)S(1)}, bf16[1024,512]{1,0:T(8,128)(2,1)S(1)}, bf16[512,1024]{1,0:T(8,128)(2,1)S(1)}) custom-call(bf16[128,1024]{1,0:T(8,128)(2,1)S(1)} %get-tuple-element.16.refs_0_, bf16[128,1024]{1,0:T(8,128)(2,1)S(1)} %get-tuple-element.17.refs_1_, bf16[128,1024]{1,0:T(8,128)(2,1)S(1)} %get-tuple-element.18.refs_2_, ...), custom_call_target="tpu_custom_call" | custom-call | flops 3500000000 | bytes 1048576 | tf_op jit(solution)/shard_map/qkv/pallas_call | solution.py:414
  48.6 0.0 collective-permute-done.2.one_ref
  48.6 0.0 collective-permute-done.3.two_ref
  48.6 0.0 copy-done.1
  48.6 0.0 copy-done.2
  48.6 4.4 %attend0.1.rest_0_ = bf16[256,128]{1,0:T(8,128)(2,1)S(1)} custom-call(bf16[512,2048]{1,0:T(8,128)(2,1)S(1)} %get-tuple-element.20.qk_ref, bf16[1024,512]{1,0:T(8,128)(2,1)S(1)} %get-tuple-element.21.vt_ref, bf16[512,1024]{1,0:T(8,128)(2,1)S(1)} %get-tuple-element.22.rows_ref, bf16[128,1024]{1,0:T(8,128)(2,1)S(1)} %collective-permute-done.2.one_ref, ...), custom_call_target="tpu_custom_call" | custom-call | flops 5600000000 | bytes 1048576 | tf_op jit(solution)/shard_map/attend0/pallas_call | solution.py:429
  53.0 0.0 collective-permute-done.one_ref
  53.1 0.0 collective-permute-done.1.two_ref
  53.1 4.8 %attend1.1 = bf16[128,8,256]{2,1,0:T(8,128)(2,1)S(1)} custom-call(bf16[512,2048]{1,0:T(8,128)(2,1)S(1)} %get-tuple-element.20.qk_ref, bf16[1024,512]{1,0:T(8,128)(2,1)S(1)} %get-tuple-element.21.vt_ref, bf16[512,1024]{1,0:T(8,128)(2,1)S(1)} %get-tuple-element.22.rows_ref, bf16[128,1024]{1,0:T(8,128)(2,1)S(1)} %collective-permute-done.one_ref, ...), custom_call_target="tpu_custom_call" | custom-call | flops 5600000000 | bytes 1048576 | tf_op jit(solution)/shard_map/attend1/pallas_call | solution.py:429
  57.9 0.0 copy-start
  57.9 23.4 %all_to_all.11.back_ref = bf16[128,8,256]{2,1,0:T(8,128)(2,1)S(1)} all-to-all(bf16[128,8,256]{2,1,0:T(8,128)(2,1)S(1)} %attend1.1), channel_id=1, replica_groups=mesh['member'=2,'space'=128] {'space'}, dimensions={0} | all-to-all | bytes 1048576 | tf_op jit(solution)/shard_map/all_to_all | solution.py:451
  81.3 0.5 predict.1.mine_ref
  81.8 5.1 %collective-permute-start.4 = (bf16[2,98,512]{2,1,0:T(8,128)(2,1)S(1)}, bf16[2,98,512]{2,1,0:T(8,128)(2,1)S(1)}, u32[]{:S(2)}, u32[]{:S(2)}) collective-permute-start(bf16[2,98,512]{2,1,0:T(8,128)(2,1)S(1)} %predict.1.mine_ref), channel_id=1, source_target_pairs={{0,128},{128,0},{1,129},{129,1},{2,130},{130,2},{3,131},{131,3},{4... | collective-permute-start | bytes 602120 | tf_op jit(solution)/shard_map/ppermute | solution.py:458
  86.9 0.8 copy.12
  87.7 0.3 collective-permute-done.4.other_ref
  88.0 0.0 copy-done
  88.0 0.9 %score.1 = f32[98,512]{1,0:T(8,128)} custom-call(bf16[2,98,512]{2,1,0:T(8,128)(2,1)S(1)} %predict.1.mine_ref, bf16[2,98,512]{2,1,0:T(8,128)(2,1)S(1)} %collective-permute-done.4.other_ref, f32[98,512]{1,0:T(8,128)S(1)} %bitcast.10), custom_call_target="tpu_custom_call" | custom-call | tf_op jit(solution)/shard_map/score/pallas_call | solution.py:459
  (1 shorter events, 0.0 us)
Async XLA Ops:
  37.9 7.2 %slice-start = ((s8[6291456]{0:T(1024)(128)(4,1)}), s8[4194304]{0:T(1024)(128)(4,1)S(1)}, s32[]{:S(2)}) async-start(s8[6291456]{0:T(1024)(128)(4,1)} %bitcast.11), calls=%async_computation.2 | async-start | bytes 8388608
  39.5 5.6 %slice-start.1 = ((s8[6291456]{0:T(1024)(128)(4,1)}), s8[2097152]{0:T(1024)(128)(4,1)S(1)}, s32[]{:S(2)}) async-start(s8[6291456]{0:T(1024)(128)(4,1)} %bitcast.11), calls=%async_computation.3 | async-start | bytes 4194304
  39.5 9.1 %collective-permute-start.2 = (bf16[128,1024]{1,0:T(8,128)(2,1)S(1)}, bf16[128,1024]{1,0:T(8,128)(2,1)S(1)}, u32[]{:S(2)}, u32[]{:S(2)}) collective-permute-start(bf16[128,1024]{1,0:T(8,128)(2,1)S(1)} %get-tuple-element.16.refs_0_), channel_id=1, source_target_pairs={{0,1},{1,0},{2,3},{3,2},{4,5},{5,4},{6,7},{7,6},{15,14},{14,15},{1... | collective-permute-start | bytes 786440 | tf_op jit(solution)/shard_map/ppermute | solution.py:412
  40.4 8.2 %collective-permute-start.3 = (bf16[128,1024]{1,0:T(8,128)(2,1)S(1)}, bf16[128,1024]{1,0:T(8,128)(2,1)S(1)}, u32[]{:S(2)}, u32[]{:S(2)}) collective-permute-start(bf16[128,1024]{1,0:T(8,128)(2,1)S(1)} %get-tuple-element.17.refs_1_), channel_id=1, source_target_pairs={{1,2},{2,1},{3,4},{4,3},{5,6},{6,5},{7,15},{15,7},{14,13},{13,14},... | collective-permute-start | bytes 786440 | tf_op jit(solution)/shard_map/ppermute | solution.py:412
  42.3 10.7 %collective-permute-start = (bf16[128,1024]{1,0:T(8,128)(2,1)S(1)}, bf16[128,1024]{1,0:T(8,128)(2,1)S(1)}, u32[]{:S(2)}, u32[]{:S(2)}) collective-permute-start(bf16[128,1024]{1,0:T(8,128)(2,1)S(1)} %get-tuple-element.18.refs_2_), channel_id=1, source_target_pairs={{0,1},{1,0},{2,3},{3,2},{4,5},{5,4},{6,7},{7,6},{15,14},{14,15},{1... | collective-permute-start | bytes 786440 | tf_op jit(solution)/shard_map/ppermute | solution.py:412
  42.9 5.7 %copy-start.1 = (bf16[1024,1024]{1,0:T(8,128)(2,1)S(1)}, bf16[1024,1024]{1,0:T(8,128)(2,1)}, u32[]{:S(2)}) copy-start(bf16[1024,1024]{1,0:T(8,128)(2,1)} %w_out_ref.3) | copy-start | bytes 6291460
  42.9 5.7 %copy-start.2 = (bf16[1024,98]{0,1:T(8,128)(2,1)S(1)}, bf16[1024,98]{0,1:T(8,128)(2,1)}, u32[]{:S(2)}) copy-start(bf16[1024,98]{0,1:T(8,128)(2,1)} %param.19) | copy-start | bytes 602116
  42.9 10.2 %collective-permute-start.1 = (bf16[128,1024]{1,0:T(8,128)(2,1)S(1)}, bf16[128,1024]{1,0:T(8,128)(2,1)S(1)}, u32[]{:S(2)}, u32[]{:S(2)}) collective-permute-start(bf16[128,1024]{1,0:T(8,128)(2,1)S(1)} %get-tuple-element.19.refs_3_), channel_id=1, source_target_pairs={{1,2},{2,1},{3,4},{4,3},{5,6},{6,5},{7,15},{15,7},{14,13},{13,14},... | collective-permute-start | bytes 786440 | tf_op jit(solution)/shard_map/ppermute | solution.py:412
  57.9 30.1 %copy-start = (f32[512,98]{0,1:T(8,128)S(1)}, f32[512,98]{0,1:T(8,128)}, u32[]{:S(2)}) copy-start(f32[512,98]{0,1:T(8,128)} %param.11) | copy-start | bytes 602116
  81.8 6.2 %collective-permute-start.4 = (bf16[2,98,512]{2,1,0:T(8,128)(2,1)S(1)}, bf16[2,98,512]{2,1,0:T(8,128)(2,1)S(1)}, u32[]{:S(2)}, u32[]{:S(2)}) collective-permute-start(bf16[2,98,512]{2,1,0:T(8,128)(2,1)S(1)} %predict.1.mine_ref), channel_id=1, source_target_pairs={{0,128},{128,0},{1,129},{129,1},{2,130},{130,2},{3,131},{131,3},{4... | collective-permute-start | bytes 602120 | tf_op jit(solution)/shard_map/ppermute | solution.py:458

commit v8 on v7

--- a/solution.py
+++ b/solution.py
@@ -79,7 +79,7 @@
 
 
 def pack_kernel(
-    var_count, x_hbm, eo_hbm, el_hbm, do_hbm, dl_hbm, w_hbm, out_ref, slot_ref, w_ref, states_ref,
+    var_count, x_hbm, eo_hbm, el_hbm, do_hbm, dl_hbm, w_hbm, out_ref, slot_ref, w_ref, states_ref, left_ref, right_ref,
     x_ref, eo_ref, el_ref, do_ref, dl_ref, sems,
 ):
     members, _, pts = states_ref.shape
@@ -96,6 +96,17 @@
     copies = [pltpu.make_async_copy(src, dst, sems.at[i]) for i, (src, dst) in enumerate(pairs)]
     for copy in copies:
         copy.start()
+    me = lax.axis_index("space")
+    at_first = (me == path_place(0)).astype(jnp.int32)
+    at_last = (me == path_place((1 << 7) - 1)).astype(jnp.int32)
+    _, half, across = left_ref.shape
+    key_id = iota((half, across), 0)
+    query_id = iota((half, across), 1) & (half - 1)
+    zero, low = jnp.zeros((half, across), F32), jnp.full((half, across), -1e30, F32)
+    left_ref[0] = jnp.where(key_id >= query_id + at_first * across, zero, low)
+    left_ref[1] = jnp.where(key_id >= query_id, zero, low)
+    right_ref[0] = jnp.where(key_id <= query_id, zero, low)
+    right_ref[1] = jnp.where(key_id + at_last * across <= query_id, zero, low)
     rows_in = members * var_count
     lanes = members * LANES
     row_id, col_id = iota((lanes, rows_in), 0), iota((lanes, rows_in), 1)
@@ -193,16 +204,14 @@
 
 
 def attend_kernel(
-    var_count, m, qk_ref, vt_ref, rows_ref, one_ref, two_ref, w_kv_ref, w_out_ref,
+    var_count, m, left_ref, right_ref, qk_ref, vt_ref, rows_ref, one_ref, two_ref, w_kv_ref, w_out_ref,
     w_dec_ref, *rest,
 ):
     if m == 0:
-        out_ref, kh_ref, vth_ref, att_ref, proc_ref, left_ref, right_ref, sa_ref, sb_ref, e_ref, halo_ref = rest
+        out_ref, kh_ref, vth_ref, att_ref, proc_ref, sa_ref, sb_ref, e_ref, halo_ref = rest
     else:
-        dec_ref, in_ref, out_ref, kh_ref, vth_ref, att_ref, proc_ref, left_ref, right_ref, sa_ref, sb_ref, e_ref, halo_ref, reply_ref = rest
+        dec_ref, in_ref, out_ref, kh_ref, vth_ref, att_ref, proc_ref, sa_ref, sb_ref, e_ref, halo_ref, reply_ref = rest
     half, width = one_ref.shape
-    me = lax.axis_index("space")
-    at_first, at_last = (me == path_place(0)).astype(jnp.int32), (me == path_place((1 << 7) - 1)).astype(jnp.int32)
     nodes = 2 * half
     head_dim = width // HEADS
     one, two = one_ref[...], two_ref[...]
@@ -218,15 +227,6 @@
         vh = jnp.dot(halo_ref[...], w_kv_ref[:, v_src], preferred_element_type=F32)
         vth_ref[c : c + chunk, :] = vh.astype(BF16).T
 
-    key_id = iota((half, 2 * half), 0)
-    query_id = iota((half, 2 * half), 1)
-    query_id = jnp.where(query_id >= half, query_id - half, query_id)
-    big = 4 * half
-    zero, low = jnp.zeros((half, 2 * half), F32), jnp.full((half, 2 * half), -1e30, F32)
-    left_ref[0] = jnp.where(key_id >= query_id + at_first * big, zero, low)
-    left_ref[1] = jnp.where(key_id >= query_id, zero, low)
-    right_ref[0] = jnp.where(key_id <= query_id, zero, low)
-    right_ref[1] = jnp.where(key_id + at_last * big <= query_id, zero, low)
     even = iota((half, LANES), 1) < head_dim
     gain = head_dim ** (-0.5) * 1.4426950408889634
     base = m * nodes
@@ -375,7 +375,8 @@
 
     path = [path_place(b) for b in range(n_space)]
     row_shape = pltpu.VMEM((1, pts), jnp.int32)
-    outgoing, dec_slot, w_enc, states = pl.pallas_call(
+    mask = jax.ShapeDtypeStruct((2, half, nodes), F32)
+    outgoing, dec_slot, w_enc, states, left, right = pl.pallas_call(
         functools.partial(pack_kernel, var_count),
         in_specs=[HBM_SPEC] * 6,
         out_shape=(
@@ -383,6 +384,8 @@
             jax.ShapeDtypeStruct((1, pts), jnp.int32),
             jax.ShapeDtypeStruct(w_embed.shape, BF16),
             jax.ShapeDtypeStruct((members, var_count, pts), BF16),
+            mask,
+            mask,
         ),
         scratch_shapes=[pltpu.VMEM((var_count, members, pts), BF16)]
         + [row_shape] * 4
@@ -434,8 +437,6 @@
                 pltpu.VMEM((width, nodes), BF16),
                 pltpu.VMEM((nodes, width), BF16),
                 pltpu.VMEM((nodes, width), BF16),
-                pltpu.VMEM((2, half, nodes), F32),
-                pltpu.VMEM((2, half, nodes), F32),
                 pltpu.VMEM((2, nodes + half, nodes), F32),
                 pltpu.VMEM((2, nodes + half, nodes), F32),
                 pltpu.VMEM((2, nodes + half, nodes), F32),
@@ -445,7 +446,7 @@
             compiler_params=params(),
             cost_estimate=cost(8),
             name=f"attend{m}",
-        )(qk, vt, node_rows, *halos[m], w_qkv, w_out, w_decode.T, *extra)
+        )(left, right, qk, vt, node_rows, *halos[m], w_qkv, w_out, w_decode.T, *extra)
     replies = decoded
 
     returned = lax.all_to_all(replies, "space", 0, 0, tiled=True)

time: 89.3 us -> 89.3 us (level)
  no operation moved by 1% of the time
where the time goes in v8:
time: 89.3 us; the launch traced here: 89.2 us
  blocking collectives  58.7 us (66%)
  Pallas kernels  19.3 us (22%)
  starting transfers between devices  9.09 us (10%)
  between operations  0.93 us (1%)
    all_to_all x1, blocking collectives, on_device(): arrived = lax.all_to_all(outgoing, 'space', 0, 0, tiled=True)  35.3 us
    all_to_all x1, blocking collectives, on_device(): returned = lax.all_to_all(replies, 'space', 0, 0, tiled=True)  23.4 us
    pallas_call x2, Pallas kernels, on_device(): pl.pallas_call(functools.partial(attend_kernel, var_count, m), out_shape=...  9.27 us
    ppermute x1, starting transfers between devices, on_device(): other = lax.ppermute(predicted, 'member', [(0, 1), (1, 0)])  5.14 us
    ppermute x4, starting transfers between devices, on_device(): lax.ppermute(end, 'space', swap)  3.95 us
    pallas_call x1, Pallas kernels, on_device(): pl.pallas_call(functools.partial(qkv_kernel, len(hidden)), out_shape=(jax...  3.55 us
    pallas_call x2, Pallas kernels, on_device(): pl.pallas_call(functools.partial(encode_kernel, var_count, m), out_shape=...  3.18 us
    pallas_call x1, Pallas kernels, on_device(): pl.pallas_call(functools.partial(pack_kernel, var_count), in_specs=[HBM_S...  1.95 us
  transfers between devices with their start and end apart: 5, of which 1 were waited for; matrix products, arithmetic and copies ran while one was open for 1% of the time, Pallas kernels for 11%

profile of v8, /device:TPU:1, one launch (start us, length us, event | category | flops | bytes accessed | tf_op | source)
XLA Modules:
  0.0 89.2 jit_solution(202880913459708230)
XLA Ops:
  0.6 1.9 %pack.1 = (bf16[128,8,256]{2,1,0:T(8,128)(2,1)S(1)}, s32[1,512]{1,0:T(1,128)S(1)}, bf16[98,1024]{1,0:T(8,128)(2,1)S(1)}, bf16[2,98,512]{2,1,0:T(8,128)(2,1)S(1)}...) custom-call(bf16[98,2,512]{2,1,0:T(2,128)(2,1)} %bitcast.16, s32[1,512]{1,0:T(1,128)} %bitcast.17, ...), custom_call_target="tpu_custom_call" | custom-call | flops 1400000000 | bytes 1048576 | tf_op jit(solution)/shard_map/pack/pallas_call | solution.py:379
  2.6 35.3 %all_to_all.10.in_ref.rest_1_ = bf16[128,8,256]{2,1,0:T(8,128)(2,1)S(1)} all-to-all(bf16[128,8,256]{2,1,0:T(8,128)(2,1)S(1)} %get-tuple-element.18), channel_id=1, replica_groups=mesh['member'=2,'space'=128] {'space'}, dimensions={0} | all-to-all | bytes 1048576 | tf_op jit(solution)/shard_map/all_to_all | solution.py:397
  37.9 0.0 slice-start
  37.9 1.6 %encode0.1 = (bf16[128,1024]{1,0:T(8,128)(2,1)S(1)}, bf16[128,1024]{1,0:T(8,128)(2,1)S(1)}) custom-call(bf16[128,8,256]{2,1,0:T(8,128)(2,1)S(1)} %all_to_all.10.in_ref.rest_1_, bf16[98,1024]{1,0:T(8,128)(2,1)S(1)} %get-tuple-element.19.w_ref), custom_call_target="tpu_custom_call" | custom-call | flops 2100000000 | bytes 1048576 | tf_op jit(solution)/shard_map/encode0/pallas_call | solution.py:406
  39.5 0.0 slice-start.1
  39.5 0.9 collective-permute-start.2
  40.4 0.4 collective-permute-start.3
  40.7 1.6 %encode1.1 = (bf16[128,1024]{1,0:T(8,128)(2,1)S(1)}, bf16[128,1024]{1,0:T(8,128)(2,1)S(1)}) custom-call(bf16[128,8,256]{2,1,0:T(8,128)(2,1)S(1)} %all_to_all.10.in_ref.rest_1_, bf16[98,1024]{1,0:T(8,128)(2,1)S(1)} %get-tuple-element.19.w_ref), custom_call_target="tpu_custom_call" | custom-call | flops 2100000000 | bytes 1048576 | tf_op jit(solution)/shard_map/encode1/pallas_call | solution.py:406
  42.3 0.6 collective-permute-start
  42.9 0.0 copy-start.1
  42.9 0.0 copy-start.2
  42.9 2.1 %collective-permute-start.1 = (bf16[128,1024]{1,0:T(8,128)(2,1)S(1)}, bf16[128,1024]{1,0:T(8,128)(2,1)S(1)}, u32[]{:S(2)}, u32[]{:S(2)}) collective-permute-start(bf16[128,1024]{1,0:T(8,128)(2,1)S(1)} %get-tuple-element.23.refs_3_), channel_id=1, source_target_pairs={{1,2},{2,1},{3,4},{4,3},{5,6},{6,5},{7,15},{15,7},{14,13},{13,14},... | collective-permute-start | bytes 786440 | tf_op jit(solution)/shard_map/ppermute | solution.py:415
  45.0 0.0 slice-done
  45.0 0.0 slice-done.1
  45.0 3.6 %qkv.1 = (bf16[512,2048]{1,0:T(8,128)(2,1)S(1)}, bf16[1024,512]{1,0:T(8,128)(2,1)S(1)}, bf16[512,1024]{1,0:T(8,128)(2,1)S(1)}) custom-call(bf16[128,1024]{1,0:T(8,128)(2,1)S(1)} %get-tuple-element.20.refs_0_, bf16[128,1024]{1,0:T(8,128)(2,1)S(1)} %get-tuple-element.21.refs_1_, bf16[128,1024]{1,0:T(8,128)(2,1)S(1)} %get-tuple-element.22.refs_2_, ...), custom_call_target="tpu_custom_call" | custom-call | flops 3500000000 | bytes 1048576 | tf_op jit(solution)/shard_map/qkv/pallas_call | solution.py:417
  48.6 0.0 collective-permute-done.2.one_ref
  48.6 0.0 collective-permute-done.3.two_ref
  48.6 0.0 copy-done.1
  48.6 0.0 copy-done.2
  48.6 4.4 %attend0.1.rest_0_ = bf16[256,128]{1,0:T(8,128)(2,1)S(1)} custom-call(f32[2,128,256]{2,1,0:T(8,128)S(1)} %get-tuple-element.16.left_ref, f32[2,128,256]{2,1,0:T(8,128)S(1)} %get-tuple-element.17.right_ref, bf16[512,2048]{1,0:T(8,128)(2,1)S(1)} %get-tuple-element.24.qk_ref, bf16[1024,512]{1,0:T(8,128)(2,1)S(1)} %get-tuple-element.25.vt_ref, ...), custom_call_target="tpu_custom_call" | custom-call | flops 5600000000 | bytes 1048576 | tf_op jit(solution)/shard_map/attend0/pallas_call | solution.py:432
  53.0 0.0 collective-permute-done.one_ref
  53.0 0.0 collective-permute-done.1.two_ref
  53.1 4.9 %attend1.1 = bf16[128,8,256]{2,1,0:T(8,128)(2,1)S(1)} custom-call(f32[2,128,256]{2,1,0:T(8,128)S(1)} %get-tuple-element.16.left_ref, f32[2,128,256]{2,1,0:T(8,128)S(1)} %get-tuple-element.17.right_ref, bf16[512,2048]{1,0:T(8,128)(2,1)S(1)} %get-tuple-element.24.qk_ref, bf16[1024,512]{1,0:T(8,128)(2,1)S(1)} %get-tuple-element.25.vt_ref, ...), custom_call_target="tpu_custom_call" | custom-call | flops 5600000000 | bytes 1048576 | tf_op jit(solution)/shard_map/attend1/pallas_call | solution.py:432
  58.0 0.0 copy-start
  58.0 23.4 %all_to_all.11.back_ref = bf16[128,8,256]{2,1,0:T(8,128)(2,1)S(1)} all-to-all(bf16[128,8,256]{2,1,0:T(8,128)(2,1)S(1)} %attend1.1), channel_id=1, replica_groups=mesh['member'=2,'space'=128] {'space'}, dimensions={0} | all-to-all | bytes 1048576 | tf_op jit(solution)/shard_map/all_to_all | solution.py:452
  81.4 0.5 predict.1.mine_ref
  81.8 5.1 %collective-permute-start.4 = (bf16[2,98,512]{2,1,0:T(8,128)(2,1)S(1)}, bf16[2,98,512]{2,1,0:T(8,128)(2,1)S(1)}, u32[]{:S(2)}, u32[]{:S(2)}) collective-permute-start(bf16[2,98,512]{2,1,0:T(8,128)(2,1)S(1)} %predict.1.mine_ref), channel_id=1, source_target_pairs={{0,128},{128,0},{1,129},{129,1},{2,130},{130,2},{3,131},{131,3},{4... | collective-permute-start | bytes 602120 | tf_op jit(solution)/shard_map/ppermute | solution.py:459
  87.0 0.8 copy.12
  87.8 0.3 collective-permute-done.4.other_ref
  88.1 0.0 copy-done
  88.1 0.9 %score.1 = f32[98,512]{1,0:T(8,128)} custom-call(bf16[2,98,512]{2,1,0:T(8,128)(2,1)S(1)} %predict.1.mine_ref, bf16[2,98,512]{2,1,0:T(8,128)(2,1)S(1)} %collective-permute-done.4.other_ref, f32[98,512]{1,0:T(8,128)S(1)} %bitcast.10), custom_call_target="tpu_custom_call" | custom-call | tf_op jit(solution)/shard_map/score/pallas_call | solution.py:460
  (1 shorter events, 0.0 us)
Async XLA Ops:
  37.9 7.2 %slice-start = ((s8[6291456]{0:T(1024)(128)(4,1)}), s8[4194304]{0:T(1024)(128)(4,1)S(1)}, s32[]{:S(2)}) async-start(s8[6291456]{0:T(1024)(128)(4,1)} %bitcast.11), calls=%async_computation.2 | async-start | bytes 8388608
  39.5 5.6 %slice-start.1 = ((s8[6291456]{0:T(1024)(128)(4,1)}), s8[2097152]{0:T(1024)(128)(4,1)S(1)}, s32[]{:S(2)}) async-start(s8[6291456]{0:T(1024)(128)(4,1)} %bitcast.11), calls=%async_computation.3 | async-start | bytes 4194304
  39.5 9.1 %collective-permute-start.2 = (bf16[128,1024]{1,0:T(8,128)(2,1)S(1)}, bf16[128,1024]{1,0:T(8,128)(2,1)S(1)}, u32[]{:S(2)}, u32[]{:S(2)}) collective-permute-start(bf16[128,1024]{1,0:T(8,128)(2,1)S(1)} %get-tuple-element.20.refs_0_), channel_id=1, source_target_pairs={{0,1},{1,0},{2,3},{3,2},{4,5},{5,4},{6,7},{7,6},{15,14},{14,15},{1... | collective-permute-start | bytes 786440 | tf_op jit(solution)/shard_map/ppermute | solution.py:415
  40.4 8.2 %collective-permute-start.3 = (bf16[128,1024]{1,0:T(8,128)(2,1)S(1)}, bf16[128,1024]{1,0:T(8,128)(2,1)S(1)}, u32[]{:S(2)}, u32[]{:S(2)}) collective-permute-start(bf16[128,1024]{1,0:T(8,128)(2,1)S(1)} %get-tuple-element.21.refs_1_), channel_id=1, source_target_pairs={{1,2},{2,1},{3,4},{4,3},{5,6},{6,5},{7,15},{15,7},{14,13},{13,14},... | collective-permute-start | bytes 786440 | tf_op jit(solution)/shard_map/ppermute | solution.py:415
  42.3 10.7 %collective-permute-start = (bf16[128,1024]{1,0:T(8,128)(2,1)S(1)}, bf16[128,1024]{1,0:T(8,128)(2,1)S(1)}, u32[]{:S(2)}, u32[]{:S(2)}) collective-permute-start(bf16[128,1024]{1,0:T(8,128)(2,1)S(1)} %get-tuple-element.22.refs_2_), channel_id=1, source_target_pairs={{0,1},{1,0},{2,3},{3,2},{4,5},{5,4},{6,7},{7,6},{15,14},{14,15},{1... | collective-permute-start | bytes 786440 | tf_op jit(solution)/shard_map/ppermute | solution.py:415
  42.9 5.7 %copy-start.1 = (bf16[1024,1024]{1,0:T(8,128)(2,1)S(1)}, bf16[1024,1024]{1,0:T(8,128)(2,1)}, u32[]{:S(2)}) copy-start(bf16[1024,1024]{1,0:T(8,128)(2,1)} %w_out_ref.3) | copy-start | bytes 6291460
  42.9 5.7 %copy-start.2 = (bf16[1024,98]{0,1:T(8,128)(2,1)S(1)}, bf16[1024,98]{0,1:T(8,128)(2,1)}, u32[]{:S(2)}) copy-start(bf16[1024,98]{0,1:T(8,128)(2,1)} %param.19) | copy-start | bytes 602116
  42.9 10.1 %collective-permute-start.1 = (bf16[128,1024]{1,0:T(8,128)(2,1)S(1)}, bf16[128,1024]{1,0:T(8,128)(2,1)S(1)}, u32[]{:S(2)}, u32[]{:S(2)}) collective-permute-start(bf16[128,1024]{1,0:T(8,128)(2,1)S(1)} %get-tuple-element.23.refs_3_), channel_id=1, source_target_pairs={{1,2},{2,1},{3,4},{4,3},{5,6},{6,5},{7,15},{15,7},{14,13},{13,14},... | collective-permute-start | bytes 786440 | tf_op jit(solution)/shard_map/ppermute | solution.py:415
  58.0 30.1 %copy-start = (f32[512,98]{0,1:T(8,128)S(1)}, f32[512,98]{0,1:T(8,128)}, u32[]{:S(2)}) copy-start(f32[512,98]{0,1:T(8,128)} %param.11) | copy-start | bytes 602116
  81.8 6.2 %collective-permute-start.4 = (bf16[2,98,512]{2,1,0:T(8,128)(2,1)S(1)}, bf16[2,98,512]{2,1,0:T(8,128)(2,1)S(1)}, u32[]{:S(2)}, u32[]{:S(2)}) collective-permute-start(bf16[2,98,512]{2,1,0:T(8,128)(2,1)S(1)} %predict.1.mine_ref), channel_id=1, source_target_pairs={{0,128},{128,0},{1,129},{129,1},{2,130},{130,2},{3,131},{131,3},{4... | collective-permute-start | bytes 602120 | tf_op jit(solution)/shard_map/ppermute | solution.py:459
